TPU v7x, 128 devices: a whole 4x4x4 slice. The times are simulated.
128 devices in a mesh: mem: 2 (over z_lo), tile: 64 (over y, x, z_hi, core).
Axes of the slice: x: 4, y: 4, z: 4 (z_hi: 2, z_lo: 2; z = z_hi * 2 + z_lo), core: 2. Of those that a mesh axis runs over, the one named last changes fastest.
Arguments:
- prior_members: bfloat16 [256, 10, 131072], P('mem', None, 'tile'), may hold values from -6 to 6
- members_in_reading_space: bfloat16 [256, 524288], P('mem', 'tile'), may hold values from -6 to 6
- measured_values: float32 [524288], P('tile'), may hold values from -6 to 6
- obs_precision_weights: float32 [524288], P('tile'), may hold values from 0.5 to 4
- valid_reading_numbers: int32 [4096], P('tile'), may hold values from 1 to 128, as said below
- neighbour_lists: int32 [1024, 8], P('tile'), may hold values from 0 to 4095, as said below
Outputs:
- analysis: bfloat16 [256, 10, 131072], P('mem', None, 'tile')
Inputs may be any that keep to these rules, and one draw needn't show every extreme that they name: `valid_reading_numbers`: every block count is at least 1; some block has 128 valid observations and some has 1. `neighbour_lists`: each row lists 8 different observation blocks. Column block b lies on tile b // 16; every block it lists lies on that tile or on one of the two tiles beside it, that is, in blocks (b // 16 - 1) * 64 to (b // 16 + 2) * 64 - 1.
All inputs are finite; a program needn't handle non-finite values.
Results may differ from a plain program's by a relative error of at most 0.0064.
Values may be sent and summed in bfloat16 or wider, within the bound.
No kernel may reach another device: no remote copies, remote signals or barrier semaphores. Data moves between devices by JAX's collectives and lax.ppermute only.
A program may use at most 128 MiB of HBM per device.

v0:
```python
import functools

import jax
import jax.numpy as jnp
from jax import lax
from jax.experimental import pallas as pl
from jax.experimental.pallas import tpu as pltpu
from jax.sharding import PartitionSpec as P


NSTEPS = 3
CHUNKS = 4
ROWS = 16


def side_pairs(tiles, mems, step):
    pairs = []
    for mem in range(mems):
        for tile in range(tiles):
            source = tile + step
            if 0 <= source < tiles:
                crossed = (min(tile, source) % 2) == 1
                source_mem = mems - 1 - mem if crossed else mem
                pairs.append((source_mem * tiles + source, mem * tiles + tile))
    return pairs


def gather_body(lists, meta, low, own, high, *refs, for_self, chunks, blocks_dev, width):
    outs = refs[:chunks]
    sems = refs[chunks]
    nloc, count = lists.shape
    half = count // 2
    mem, tile = meta[0], meta[1]
    base = (tile - 1) * blocks_dev
    owner = mem if for_self else 1 - mem
    per_chunk = half // chunks
    for chunk in range(chunks):
        out = outs[chunk]
        for block in range(per_chunk):
            row = owner * half + chunk * per_chunk + block
            for n in range(nloc):
                local = lists[n, row] - base
                which = lax.div(local, blocks_dev)
                start = pl.multiple_of((local - which * blocks_dev) * width, width)
                target = out.at[:, pl.ds((block * nloc + n) * width, width)]
                for index, source in enumerate((low, own, high)):

                    @pl.when(which == index)
                    def _(source=source):
                        pltpu.make_async_copy(
                            source.at[:, pl.ds(start, width)], target, sems.at[chunk]
                        ).start()

    for chunk in range(chunks):
        size = outs[chunk].shape[1]
        pltpu.make_async_copy(own.at[:, pl.ds(0, size)], outs[chunk], sems.at[chunk]).wait()


def gather_blocks(lists, meta, low, own, high, for_self, blocks_dev, width):
    nloc, count = lists.shape
    members = own.shape[0]
    size = (count // 2 // CHUNKS) * nloc * width
    whole = pl.BlockSpec((members, size), lambda i, *_: (0, 0))
    return pl.pallas_call(
        functools.partial(
            gather_body, for_self=for_self, chunks=CHUNKS, blocks_dev=blocks_dev, width=width
        ),
        grid_spec=pltpu.PrefetchScalarGridSpec(
            num_scalar_prefetch=2,
            grid=(1,),
            in_specs=[pl.BlockSpec(memory_space=pltpu.HBM)] * 3,
            out_specs=[whole] * CHUNKS,
            scratch_shapes=[pltpu.SemaphoreType.DMA((CHUNKS,))],
        ),
        out_shape=[jax.ShapeDtypeStruct((members, size), own.dtype)] * CHUNKS,
        cost_estimate=pl.CostEstimate(
            flops=0, bytes_accessed=4 * CHUNKS * members * size, transcendentals=0
        ),
        compiler_params=pltpu.CompilerParams(vmem_limit_bytes=8 << 20),
        name="gather_self" if for_self else "gather_send",
    )(lists, meta, low, own, high)


def split(value):
    high = value.astype(jnp.bfloat16)
    return high, (value - high.astype(jnp.float32)).astype(jnp.bfloat16)


def dot(left, right):
    return lax.dot_general(
        left, right, (((1,), (0,)), ((), ())), preferred_element_type=jnp.float32
    )


def dot3(left, right):
    lh, ll = left
    rh, rl = right
    return dot(lh, rh) + (dot(lh, rl) + dot(ll, rh))


def analysis_body(
    lists, meta, mine, theirs, held, received, low, own, high, *refs, chunk, blocks_dev, width
):
    kept, sent, table, ybuf, sbuf, xbuf, mbuf = refs[-7:]
    nloc, count = lists.shape
    half = count // 2
    mem, tile = meta[0], meta[1]
    parity = lax.rem(tile, 2)
    base = (tile - 1) * blocks_dev
    block = pl.program_id(0)
    row = mem * half + chunk * (half // CHUNKS) + block
    rows = held.shape[0]
    members = 2 * rows
    side = table.shape[0] // 3

    @pl.when(block == 0)
    def _():
        for index, source in enumerate((low, own, high)):
            table[pl.ds(index * side, side), :] = source[...]
        ybuf[pl.ds(members, ROWS), :] = jnp.zeros((ROWS, nloc * width), jnp.bfloat16)

    for n in range(nloc):
        local = lists[n, row] - base
        which = lax.div(local, blocks_dev)
        entry = which * side + (local - which * blocks_dev)
        crossed = ((which == 0) & (parity == 0)) | ((which == 2) & (parity == 1))
        at = pl.ds(n * width, width)
        first = held[:, at].astype(jnp.float32)
        second = received[:, at].astype(jnp.float32)
        mean = (
            jnp.sum(first, axis=0, keepdims=True) + jnp.sum(second, axis=0, keepdims=True)
        ) / members
        value = table[pl.ds(entry, 1), :]
        weight = table[pl.ds(entry + blocks_dev, 1), :]
        innov = value - mean
        d0 = innov.astype(jnp.bfloat16)
        rest = innov - d0.astype(jnp.float32)
        d1, d2 = split(rest)
        ybuf[pl.ds(members, ROWS), at] = jnp.concatenate(
            [d0, d1, d2, jnp.zeros((ROWS - 3, width), jnp.bfloat16)], axis=0
        )
        pert1 = (first - mean).astype(jnp.bfloat16)
        pert2 = (second - mean).astype(jnp.bfloat16)
        scaled1 = (pert1.astype(jnp.float32) * weight).astype(jnp.bfloat16)
        scaled2 = (pert2.astype(jnp.float32) * weight).astype(jnp.bfloat16)
        place1 = pl.multiple_of(jnp.where(crossed, rows, 0), rows)
        place2 = pl.multiple_of(jnp.where(crossed, 0, rows), rows)
        ybuf[pl.ds(place1, rows), at] = pert1
        ybuf[pl.ds(place2, rows), at] = pert2
        sbuf[pl.ds(place1, rows), at] = scaled1
        sbuf[pl.ds(place2, rows), at] = scaled2

    gram = lax.dot_general(
        ybuf[...], sbuf[...], (((1,), (1,)), ((), ())), preferred_element_type=jnp.float32
    )
    matrix = gram[:members]
    rhs = jnp.sum(gram[members:], axis=0, keepdims=True)
    diagonal = lax.broadcasted_iota(jnp.int32, (members, members), 0) == lax.broadcasted_iota(
        jnp.int32, (members, members), 1
    )
    matrix = matrix + jnp.where(diagonal, members - 1.0, 0.0)
    trace = jnp.sum(
        jnp.sum(jnp.where(diagonal, matrix, 0.0), axis=0, keepdims=True), axis=1, keepdims=True
    )
    scale = trace / members
    iterate = matrix / scale
    eye15 = jnp.where(diagonal, 1.5, 0.0)
    inverse_root = eye15 - 0.5 * iterate
    factor = split(inverse_root)
    iterate = dot3(factor, split(iterate))
    for step in range(1, NSTEPS):
        root_parts = split(inverse_root)
        iterate_parts = split(iterate)
        factor = split(eye15 - 0.5 * dot3(iterate_parts, root_parts))
        if step + 1 < NSTEPS:
            iterate = dot3(factor, iterate_parts)
        inverse_root = dot3(root_parts, factor)
    root_parts = split(inverse_root)
    shift = jnp.broadcast_to(rhs, (ROWS, members))
    shift = dot3(split(shift), root_parts)
    shift = dot3(split(shift), root_parts)[:1] / scale
    trans = (jnp.sqrt((members - 1.0) / scale) * inverse_root + shift).astype(jnp.bfloat16)

    layers = mine.shape[0]
    for layer in range(layers):
        at = pl.ds(layer * width, width)
        first = mine[layer].astype(jnp.float32)
        second = theirs[layer].astype(jnp.float32)
        mean = (
            jnp.sum(first, axis=0, keepdims=True) + jnp.sum(second, axis=0, keepdims=True)
        ) / members
        mbuf[:, at] = mean
        xbuf[pl.ds(0, rows), at] = (first - mean).astype(jnp.bfloat16)
        xbuf[pl.ds(rows, rows), at] = (second - mean).astype(jnp.bfloat16)
    result = (dot(trans, xbuf[...]) + mbuf[...]).astype(jnp.bfloat16)
    for layer in range(layers):
        at = slice(layer * width, (layer + 1) * width)
        kept[layer] = result[:rows, at]
        sent[layer] = result[rows:, at]


def analyse(
    lists, meta, mine, theirs, held, received, tables, output, chunk, skipped, blocks_dev, width
):
    nloc, count = lists.shape
    half = count // 2
    per_chunk = half // CHUNKS
    layers, rows, _ = mine.shape
    members = 2 * rows
    flops = 2 * per_chunk * members * members * (nloc * width + 18 * members + layers * width)
    span = nloc * width

    def mine_at(i, lists, meta):
        return (0, 0, meta[0] * half + chunk * per_chunk + i)

    tile_block = (layers, rows, width)
    table_spec = pl.BlockSpec(tables[0].shape, lambda i, *_: (0, 0))
    in_specs = [
        pl.BlockSpec(tile_block, mine_at),
        pl.BlockSpec(tile_block, lambda i, *_: (0, 0, (chunk - skipped) * per_chunk + i)),
        pl.BlockSpec((rows, span), lambda i, *_: (0, i)),
        pl.BlockSpec((rows, span), lambda i, *_: (0, i)),
        table_spec,
        table_spec,
        table_spec,
    ]
    operands = [mine, theirs, held, received, *tables]
    aliases = {}
    if output is not None:
        in_specs.append(pl.BlockSpec(memory_space=pl.ANY))
        aliases = {2 + len(operands): 0}
        operands.append(output)
    return pl.pallas_call(
        functools.partial(analysis_body, chunk=chunk, blocks_dev=blocks_dev, width=width),
        grid_spec=pltpu.PrefetchScalarGridSpec(
            num_scalar_prefetch=2,
            grid=(per_chunk,),
            in_specs=in_specs,
            out_specs=[
                pl.BlockSpec(tile_block, mine_at),
                pl.BlockSpec(tile_block, lambda i, *_: (0, 0, i)),
            ],
            scratch_shapes=[
                pltpu.VMEM((3 * tables[0].shape[0], width), jnp.float32),
                pltpu.VMEM((members + ROWS, span), jnp.bfloat16),
                pltpu.VMEM((members, span), jnp.bfloat16),
                pltpu.VMEM((members, layers * width), jnp.bfloat16),
                pltpu.VMEM((1, layers * width), jnp.float32),
            ],
        ),
        out_shape=[
            jax.ShapeDtypeStruct(mine.shape, jnp.bfloat16),
            jax.ShapeDtypeStruct((layers, rows, per_chunk * width), jnp.bfloat16),
        ],
        input_output_aliases=aliases,
        cost_estimate=pl.CostEstimate(
            flops=flops, bytes_accessed=per_chunk * 2 * rows * 2 * (span + 2 * layers * width),
            transcendentals=0,
        ),
        compiler_params=pltpu.CompilerParams(vmem_limit_bytes=24 << 20),
        name="analyse",
    )(lists, meta, *operands)


def place_body(meta, piece, output, placed, sem, *, chunk):
    cols = piece.shape[2]
    start = (1 - meta[0]) * (placed.shape[2] // 2) + chunk * cols
    copy = pltpu.make_async_copy(
        piece, placed.at[:, :, pl.ds(pl.multiple_of(start, cols), cols)], sem
    )
    copy.start()
    copy.wait()


def place(meta, piece, output, chunk):
    return pl.pallas_call(
        functools.partial(place_body, chunk=chunk),
        grid_spec=pltpu.PrefetchScalarGridSpec(
            num_scalar_prefetch=1,
            grid=(1,),
            in_specs=[pl.BlockSpec(memory_space=pl.ANY)] * 2,
            out_specs=pl.BlockSpec(memory_space=pl.ANY),
            scratch_shapes=[pltpu.SemaphoreType.DMA],
        ),
        out_shape=jax.ShapeDtypeStruct(output.shape, output.dtype),
        input_output_aliases={2: 0},
        cost_estimate=pl.CostEstimate(
            flops=0, bytes_accessed=4 * piece.size, transcendentals=0
        ),
        compiler_params=pltpu.CompilerParams(vmem_limit_bytes=2 << 20),
        name="place",
    )(meta, piece, output)


def per_device(
    prior_members,
    members_in_reading_space,
    measured_values,
    obs_precision_weights,
    valid_reading_numbers,
    neighbour_lists,
):
    tile_no = lax.axis_index("tile")
    member_no = lax.axis_index("mem")
    tiles = lax.axis_size("tile")
    mems = lax.axis_size("mem")
    both = ("mem", "tile")
    swap = [(0, 1), (1, 0)]
    from_low = side_pairs(tiles, mems, -1)
    from_high = side_pairs(tiles, mems, 1)
    blocks_dev = valid_reading_numbers.shape[0]
    width = members_in_reading_space.shape[1] // blocks_dev
    cols = prior_members.shape[2]

    mine = jnp.transpose(prior_members, (1, 0, 2))
    lists = neighbour_lists.T
    meta = jnp.stack([member_no, tile_no]).astype(jnp.int32)

    own = members_in_reading_space
    half = cols // 2
    piece = half // CHUNKS
    prior = []
    for start, size in ((0, piece), (piece, half - piece)):
        outgoing = lax.dynamic_slice_in_dim(mine, (1 - member_no) * half + start, size, 2)
        prior.append(lax.ppermute(outgoing, "mem", swap))
    low = lax.ppermute(own, both, from_low)
    high = lax.ppermute(own, both, from_high)
    slots = jnp.arange(width, dtype=jnp.int32)
    valid = slots[None, :] < valid_reading_numbers[:, None]
    weight = jnp.where(valid, obs_precision_weights.reshape(blocks_dev, width), 0.0)
    table = jnp.concatenate([measured_values.reshape(blocks_dev, width), weight], axis=0)
    table_low = lax.ppermute(table, both, from_low)
    table_high = lax.ppermute(table, both, from_high)
    tables = (table_low, table, table_high)

    to_send = gather_blocks(lists, meta, low, own, high, False, blocks_dev, width)
    received = []
    for chunk in range(CHUNKS):
        received.append(lax.ppermute(to_send[chunk], "mem", swap))
    held = gather_blocks(lists, meta, low, own, high, True, blocks_dev, width)
    output = None
    arrived = []
    for chunk in range(CHUNKS):
        output, sent = analyse(
            lists, meta, mine, prior[min(chunk, 1)], held[chunk], received[chunk], tables,
            output, chunk, min(chunk, 1), blocks_dev, width,
        )
        arrived.append(lax.ppermute(sent, "mem", swap))
    for chunk in range(CHUNKS):
        output = place(meta, arrived[chunk], output, chunk)
    return jnp.transpose(output, (1, 0, 2))


def solution(mesh):
    in_specs = (
        P("mem", None, "tile"),
        P("mem", "tile"),
        P("tile"),
        P("tile"),
        P("tile"),
        P("tile", None),
    )
    out_specs = P("mem", None, "tile")

    return jax.shard_map(
        per_device, mesh=mesh, in_specs=in_specs, out_specs=out_specs, check_vma=False
    )
```

profile of v0, /device:TPU:1, one launch (start us, length us, event | category | flops | bytes accessed | tf_op | source)
XLA Modules:
  0.0 172.8 jit_solution(15316029018755728596)
XLA Ops:
  0.0 0.0 copy-start.2
  0.0 3.4 %collective-permute-start.2 = (bf16[128,8192]{1,0:T(8,128)(2,1)}, bf16[128,8192]{1,0:T(8,128)(2,1)}, u32[]{:S(2)}, u32[]{:S(2)}) collective-permute-start(bf16[128,8192]{1,0:T(8,128)(2,1)} %own.3), channel_id=1, source_target_pairs={{1,0},{66,1},{3,2},{68,3},{5,4},{70,5},{7,6},{72,7},{9,8},{74,9},{... | collective-permute-start | bytes 6291464 | tf_op jit(solution)/shard_map/ppermute | solution.py:327
  3.4 5.7 %collective-permute-start.1 = (bf16[128,8192]{1,0:T(8,128)(2,1)}, bf16[128,8192]{1,0:T(8,128)(2,1)}, u32[]{:S(2)}, u32[]{:S(2)}) collective-permute-start(bf16[128,8192]{1,0:T(8,128)(2,1)} %own.3), channel_id=1, source_target_pairs={{0,1},{65,2},{2,3},{67,4},{4,5},{69,6},{6,7},{71,8},{8,9},{73,10},... | collective-permute-start | bytes 6291464 | tf_op jit(solution)/shard_map/ppermute | solution.py:326
  9.1 0.0 copy-start.3
  9.1 0.0 copy-start.5
  9.1 0.0 copy-start.4
  9.1 3.0 %dynamic-slice_bitcast_fusion = bf16[10,128,768]{2,1,0:T(8,128)(2,1)} fusion(bf16[128,10,2048]{2,0,1:T(8,128)(2,1)} %param.6, s32[]{:T(128)S(6)} %select_n.10), kind=kLoop, calls=%fused_computation | loop fusion | bytes 3932164 | tf_op jit(solution)/shard_map/dynamic_slice | solution.py:324
  12.1 0.0 collective-permute-start
  12.1 0.0 slice-start
  12.2 2.1 %dynamic-slice_bitcast_fusion.1 = bf16[10,128,256]{2,1,0:T(8,128)(2,1)} fusion(bf16[128,10,2048]{2,0,1:T(8,128)(2,1)} %param.6, s32[]{:T(128)S(6)} %select_n.12), kind=kLoop, calls=%fused_computation.1 | loop fusion | bytes 1310724 | tf_op jit(solution)/shard_map/dynamic_slice | solution.py:324
  14.2 1.5 collective-permute-start.8
  15.7 0.1 pad_add_fusion.meta
  15.7 15.5 %collective-permute-done.2.high = bf16[128,8192]{1,0:T(8,128)(2,1)} collective-permute-done((bf16[128,8192]{1,0:T(8,128)(2,1)}, bf16[128,8192]{1,0:T(8,128)(2,1)}, u32[]{:S(2)}, u32[]{:S(2)}) %collective-permute-start.2) | collective-permute-done | bytes 2097184 | tf_op jit(solution)/shard_map/ppermute | solution.py:327
  31.2 23.3 %collective-permute-done.1.low = bf16[128,8192]{1,0:T(8,128)(2,1)} collective-permute-done((bf16[128,8192]{1,0:T(8,128)(2,1)}, bf16[128,8192]{1,0:T(8,128)(2,1)}, u32[]{:S(2)}, u32[]{:S(2)}) %collective-permute-start.1) | collective-permute-done | bytes 2097184 | tf_op jit(solution)/shard_map/ppermute | solution.py:326
  54.5 0.0 copy-done.2
  54.5 0.0 copy-start
  54.5 1.6 copy-done
  56.1 0.0 copy-start.1
  56.1 0.0 slice-start.1
  56.1 2.5 %gather_send.1 = (bf16[128,2048]{1,0:T(8,128)(2,1)S(1)}, bf16[128,2048]{1,0:T(8,128)(2,1)S(1)}, bf16[128,2048]{1,0:T(8,128)(2,1)S(1)}, bf16[128,2048]{1,0:T(8,128)(2,1)S(1)}) custom-call(s32[8,16]{1,0:T(8,128)S(1)} %bitcast.18, s32[2]{0:T(128)S(1)} %pad_add_fusion.meta, bf16[128,8192]{1,0:T(8,128)(2,1)} %collective-permute-done.1.low, ...), custom_call_target="tpu_custom_call" | custom-call | bytes 4194304 | tf_op jit(solution)/shard_map/gather_send/pallas_call | solution.py:64
  58.7 0.1 collective-permute-start.9
  58.7 0.0 copy-done.3
  58.8 0.0 copy-done.5
  58.8 0.1 bitcast_select_fusion
  58.8 1.5 collective-permute-start.7
  60.3 0.0 copy-done.4
  60.3 1.9 %collective-permute-start.5 = (f32[128,128]{1,0:T(8,128)S(1)}, f32[128,128]{1,0:T(8,128)S(1)}, u32[]{:S(2)}, u32[]{:S(2)}) collective-permute-start(f32[128,128]{1,0:T(8,128)S(1)} %pad_maximum_fusion.own), channel_id=1, source_target_pairs={{1,0},{66,1},{3,2},{68,3},{5,4},{70,5},{7,6},{72,7},{9,8},{74,9},{... | collective-permute-start | bytes 196616 | tf_op jit(solution)/shard_map/ppermute | solution.py:333
  62.3 6.2 %collective-permute-done.5.high = f32[128,128]{1,0:T(8,128)S(1)} collective-permute-done((f32[128,128]{1,0:T(8,128)S(1)}, f32[128,128]{1,0:T(8,128)S(1)}, u32[]{:S(2)}, u32[]{:S(2)}) %collective-permute-start.5) | collective-permute-done | bytes 65568 | tf_op jit(solution)/shard_map/ppermute | solution.py:333
  68.4 1.9 %collective-permute-start.4 = (f32[128,128]{1,0:T(8,128)S(1)}, f32[128,128]{1,0:T(8,128)S(1)}, u32[]{:S(2)}, u32[]{:S(2)}) collective-permute-start(f32[128,128]{1,0:T(8,128)S(1)} %pad_maximum_fusion.own), channel_id=1, source_target_pairs={{0,1},{65,2},{2,3},{67,4},{4,5},{69,6},{6,7},{71,8},{8,9},{73,10},... | collective-permute-start | bytes 196616 | tf_op jit(solution)/shard_map/ppermute | solution.py:332
  70.4 1.3 collective-permute-done.4.low
  71.7 0.0 collective-permute-start.6
  71.7 0.0 collective-permute-done.8.theirs
  71.7 1.5 collective-permute-start.3
  73.1 0.0 copy-done.1
  73.1 2.7 %gather_self.1 = (bf16[128,2048]{1,0:T(8,128)(2,1)S(1)}, bf16[128,2048]{1,0:T(8,128)(2,1)S(1)}, bf16[128,2048]{1,0:T(8,128)(2,1)S(1)}, bf16[128,2048]{1,0:T(8,128)(2,1)S(1)}) custom-call(s32[8,16]{1,0:T(8,128)S(1)} %bitcast.19, s32[2]{0:T(128)S(1)} %pad_add_fusion.meta, bf16[128,8192]{1,0:T(8,128)(2,1)} %collective-permute-done.1.low, ...), custom_call_target="tpu_custom_call" | custom-call | bytes 4194304 | tf_op jit(solution)/shard_map/gather_self/pallas_call | solution.py:64
  75.9 6.6 %collective-permute-done.9.received = bf16[128,2048]{1,0:T(8,128)(2,1)S(1)} collective-permute-done((bf16[128,2048]{1,0:T(8,128)(2,1)S(1)}, bf16[128,2048]{1,0:T(8,128)(2,1)S(1)}, u32[]{:S(2)}, u32[]{:S(2)}) %collective-permute-start.9) | collective-permute-done | bytes 524320 | tf_op jit(solution)/shard_map/ppermute | solution.py:339
  82.5 0.0 slice-done
  82.5 0.0 slice-done.1
  82.5 9.0 %analyse.4 = (bf16[10,128,2048]{2,1,0:T(8,128)(2,1)}, bf16[10,128,256]{2,1,0:T(8,128)(2,1)S(1)}) custom-call(s32[8,16]{1,0:T(8,128)S(1)} %bitcast.20, s32[2]{0:T(128)S(1)} %pad_add_fusion.meta, bf16[10,128,2048]{2,1,0:T(8,128)(2,1)S(1)} %bitcast.14, bf16[10,128,256]{2,1,0:T(8,128)(2,1)} %collective-permute-done.8.theirs, ...), custom_call_target="tpu_custom_call" | custom-call | flops 1811939328 | bytes 3670016 | tf_op jit(solution)/shard_map/analyse/pallas_call | solution.py:233
  91.4 0.0 collective-permute-done.theirs
  91.4 2.3 %collective-permute-done.7.received = bf16[128,2048]{1,0:T(8,128)(2,1)S(1)} collective-permute-done((bf16[128,2048]{1,0:T(8,128)(2,1)S(1)}, bf16[128,2048]{1,0:T(8,128)(2,1)S(1)}, u32[]{:S(2)}, u32[]{:S(2)}) %collective-permute-start.7) | collective-permute-done | bytes 524320 | tf_op jit(solution)/shard_map/ppermute | solution.py:339
  93.7 8.3 %analyse.5 = (bf16[10,128,2048]{2,1,0:T(8,128)(2,1)}, bf16[10,128,256]{2,1,0:T(8,128)(2,1)S(1)}) custom-call(s32[8,16]{1,0:T(8,128)S(1)} %bitcast.21, s32[2]{0:T(128)S(1)} %pad_add_fusion.meta, bf16[10,128,2048]{2,1,0:T(8,128)(2,1)S(1)} %bitcast.15, bf16[10,128,768]{2,1,0:T(8,128)(2,1)S(1)} %collective-permute-done.theirs, ...), custom_call_target="tpu_custom_call", output_to_operand_aliasing={{0}: (9, {})} | custom-call | flops 1811939328 | bytes 3670016 | tf_op jit(solution)/shard_map/analyse/pallas_call | solution.py:233
  102.0 2.9 %collective-permute-done.6.received = bf16[128,2048]{1,0:T(8,128)(2,1)S(1)} collective-permute-done((bf16[128,2048]{1,0:T(8,128)(2,1)S(1)}, bf16[128,2048]{1,0:T(8,128)(2,1)S(1)}, u32[]{:S(2)}, u32[]{:S(2)}) %collective-permute-start.6) | collective-permute-done | bytes 524320 | tf_op jit(solution)/shard_map/ppermute | solution.py:339
  104.9 8.3 %analyse.6 = (bf16[10,128,2048]{2,1,0:T(8,128)(2,1)}, bf16[10,128,256]{2,1,0:T(8,128)(2,1)S(1)}) custom-call(s32[8,16]{1,0:T(8,128)S(1)} %bitcast.22, s32[2]{0:T(128)S(1)} %pad_add_fusion.meta, bf16[10,128,2048]{2,1,0:T(8,128)(2,1)S(1)} %bitcast.16, bf16[10,128,768]{2,1,0:T(8,128)(2,1)S(1)} %collective-permute-done.theirs, ...), custom_call_target="tpu_custom_call", output_to_operand_aliasing={{0}: (9, {})} | custom-call | flops 1811939328 | bytes 3670016 | tf_op jit(solution)/shard_map/analyse/pallas_call | solution.py:233
  113.3 0.0 collective-permute-start.11
  113.3 1.5 collective-permute-start.12
  114.7 0.0 collective-permute-start.13
  114.8 0.0 collective-permute-done.3.received
  114.8 8.3 %analyse.7 = (bf16[10,128,2048]{2,1,0:T(8,128)(2,1)}, bf16[10,128,256]{2,1,0:T(8,128)(2,1)S(1)}) custom-call(s32[8,16]{1,0:T(8,128)S(1)} %bitcast.23, s32[2]{0:T(128)S(1)} %pad_add_fusion.meta, bf16[10,128,2048]{2,1,0:T(8,128)(2,1)S(1)} %bitcast.17, bf16[10,128,768]{2,1,0:T(8,128)(2,1)S(1)} %collective-permute-done.theirs, ...), custom_call_target="tpu_custom_call", output_to_operand_aliasing={{0}: (9, {})} | custom-call | flops 1811939328 | bytes 3670016 | tf_op jit(solution)/shard_map/analyse/pallas_call | solution.py:233
  123.1 1.4 collective-permute-start.10
  124.5 33.6 %collective-permute-done.13.piece = bf16[10,128,256]{2,1,0:T(8,128)(2,1)S(1)} collective-permute-done((bf16[10,128,256]{2,1,0:T(8,128)(2,1)S(1)}, bf16[10,128,256]{2,1,0:T(8,128)(2,1)S(1)}, u32[]{:S(2)}, u32[]{:S(2)}) %collective-permute-start.13) | collective-permute-done | bytes 655392 | tf_op jit(solution)/shard_map/ppermute | solution.py:348
  158.1 1.4 place.4.output
  159.5 0.0 collective-permute-done.12.piece
  159.5 1.4 place.5.output
  160.9 0.0 collective-permute-done.11.piece
  160.9 1.4 place.6.output
  162.3 8.9 %collective-permute-done.10.piece = bf16[10,128,256]{2,1,0:T(8,128)(2,1)S(1)} collective-permute-done((bf16[10,128,256]{2,1,0:T(8,128)(2,1)S(1)}, bf16[10,128,256]{2,1,0:T(8,128)(2,1)S(1)}, u32[]{:S(2)}, u32[]{:S(2)}) %collective-permute-start.10) | collective-permute-done | bytes 655392 | tf_op jit(solution)/shard_map/ppermute | solution.py:348
  171.2 1.4 place.7
  (2 shorter events, 0.0 us)
Async XLA Ops:
  0.0 54.5 %copy-start.2 = (s32[16,8]{0,1:T(8,128)S(1)}, s32[16,8]{0,1:T(8,128)}, u32[]{:S(2)}) copy-start(s32[16,8]{0,1:T(8,128)} %param.11) | copy-start | bytes 1540
  0.0 31.2 %collective-permute-start.2 = (bf16[128,8192]{1,0:T(8,128)(2,1)}, bf16[128,8192]{1,0:T(8,128)(2,1)}, u32[]{:S(2)}, u32[]{:S(2)}) collective-permute-start(bf16[128,8192]{1,0:T(8,128)(2,1)} %own.3), channel_id=1, source_target_pairs={{1,0},{66,1},{3,2},{68,3},{5,4},{70,5},{7,6},{72,7},{9,8},{74,9},{... | collective-permute-start | bytes 6291464 | tf_op jit(solution)/shard_map/ppermute | solution.py:327
  3.4 51.1 %collective-permute-start.1 = (bf16[128,8192]{1,0:T(8,128)(2,1)}, bf16[128,8192]{1,0:T(8,128)(2,1)}, u32[]{:S(2)}, u32[]{:S(2)}) collective-permute-start(bf16[128,8192]{1,0:T(8,128)(2,1)} %own.3), channel_id=1, source_target_pairs={{0,1},{65,2},{2,3},{67,4},{4,5},{69,6},{6,7},{71,8},{8,9},{73,10},... | collective-permute-start | bytes 6291464 | tf_op jit(solution)/shard_map/ppermute | solution.py:326
  9.1 49.6 %copy-start.3 = (f32[8192]{0:T(1024)S(1)}, f32[8192]{0:T(1024)}, u32[]{:S(2)}) copy-start(f32[8192]{0:T(1024)} %param.9) | copy-start | bytes 98308
  9.1 49.6 %copy-start.5 = (s32[64]{0:T(128)S(1)}, s32[64]{0:T(128)}, u32[]{:S(2)}) copy-start(s32[64]{0:T(128)} %param.10) | copy-start | bytes 772
  9.1 51.2 %copy-start.4 = (f32[8192]{0:T(1024)S(1)}, f32[8192]{0:T(1024)}, u32[]{:S(2)}) copy-start(f32[8192]{0:T(1024)} %param.8) | copy-start | bytes 98308
  12.1 79.3 %collective-permute-start = (bf16[10,128,768]{2,1,0:T(8,128)(2,1)}, bf16[10,128,768]{2,1,0:T(8,128)(2,1)S(1)}, u32[]{:S(2)}, u32[]{:S(2)}) collective-permute-start(bf16[10,128,768]{2,1,0:T(8,128)(2,1)} %dynamic-slice_bitcast_fusion), channel_id=1, source_target_pairs={{0,64},{64,0},{1,65},{65,1},{2,66},{66,2},{3,67},{67,3},{4,68},{68... | collective-permute-start | bytes 5898248 | tf_op jit(solution)/shard_map/ppermute | solution.py:325
  12.1 70.3 %slice-start = ((s8[5242880]{0:T(1024)(128)(4,1)}), s8[1048576]{0:T(1024)(128)(4,1)S(1)}, s32[]{:S(2)}) async-start(s8[5242880]{0:T(1024)(128)(4,1)} %bitcast.12), calls=%async_computation | async-start | bytes 2097152
  14.2 57.5 %collective-permute-start.8 = (bf16[10,128,256]{2,1,0:T(8,128)(2,1)}, bf16[10,128,256]{2,1,0:T(8,128)(2,1)}, u32[]{:S(2)}, u32[]{:S(2)}) collective-permute-start(bf16[10,128,256]{2,1,0:T(8,128)(2,1)} %dynamic-slice_bitcast_fusion.1), channel_id=1, source_target_pairs={{0,64},{64,0},{1,65},{65,1},{2,66},{66,2},{3,67},{67,3},{4,68},{68... | collective-permute-start | bytes 1966088 | tf_op jit(solution)/shard_map/ppermute | solution.py:325
  54.5 1.6 copy-start
  56.1 17.0 %copy-start.1 = (bf16[128,8192]{1,0:T(8,128)(2,1)S(1)}, bf16[128,8192]{1,0:T(8,128)(2,1)}, u32[]{:S(2)}) copy-start(bf16[128,8192]{1,0:T(8,128)(2,1)} %own.3) | copy-start | bytes 6291460
  56.1 26.3 %slice-start.1 = ((s8[5242880]{0:T(1024)(128)(4,1)}), s8[4194304]{0:T(1024)(128)(4,1)S(1)}, s32[]{:S(2)}) async-start(s8[5242880]{0:T(1024)(128)(4,1)} %bitcast.12), calls=%async_computation.1 | async-start | bytes 8388608
  58.7 23.8 %collective-permute-start.9 = (bf16[128,2048]{1,0:T(8,128)(2,1)S(1)}, bf16[128,2048]{1,0:T(8,128)(2,1)S(1)}, u32[]{:S(2)}, u32[]{:S(2)}) collective-permute-start(bf16[128,2048]{1,0:T(8,128)(2,1)S(1)} %get-tuple-element.28), channel_id=1, source_target_pairs={{0,64},{64,0},{1,65},{65,1},{2,66},{66,2},{3,67},{67,3},{4,68},{68... | collective-permute-start | bytes 1572872 | tf_op jit(solution)/shard_map/ppermute | solution.py:339
  58.8 34.9 %collective-permute-start.7 = (bf16[128,2048]{1,0:T(8,128)(2,1)S(1)}, bf16[128,2048]{1,0:T(8,128)(2,1)S(1)}, u32[]{:S(2)}, u32[]{:S(2)}) collective-permute-start(bf16[128,2048]{1,0:T(8,128)(2,1)S(1)} %get-tuple-element.26), channel_id=1, source_target_pairs={{0,64},{64,0},{1,65},{65,1},{2,66},{66,2},{3,67},{67,3},{4,68},{68... | collective-permute-start | bytes 1572872 | tf_op jit(solution)/shard_map/ppermute | solution.py:339
  60.3 8.1 %collective-permute-start.5 = (f32[128,128]{1,0:T(8,128)S(1)}, f32[128,128]{1,0:T(8,128)S(1)}, u32[]{:S(2)}, u32[]{:S(2)}) collective-permute-start(f32[128,128]{1,0:T(8,128)S(1)} %pad_maximum_fusion.own), channel_id=1, source_target_pairs={{1,0},{66,1},{3,2},{68,3},{5,4},{70,5},{7,6},{72,7},{9,8},{74,9},{... | collective-permute-start | bytes 196616 | tf_op jit(solution)/shard_map/ppermute | solution.py:333
  68.4 3.2 %collective-permute-start.4 = (f32[128,128]{1,0:T(8,128)S(1)}, f32[128,128]{1,0:T(8,128)S(1)}, u32[]{:S(2)}, u32[]{:S(2)}) collective-permute-start(f32[128,128]{1,0:T(8,128)S(1)} %pad_maximum_fusion.own), channel_id=1, source_target_pairs={{0,1},{65,2},{2,3},{67,4},{4,5},{69,6},{6,7},{71,8},{8,9},{73,10},... | collective-permute-start | bytes 196616 | tf_op jit(solution)/shard_map/ppermute | solution.py:332
  71.7 33.3 %collective-permute-start.6 = (bf16[128,2048]{1,0:T(8,128)(2,1)S(1)}, bf16[128,2048]{1,0:T(8,128)(2,1)S(1)}, u32[]{:S(2)}, u32[]{:S(2)}) collective-permute-start(bf16[128,2048]{1,0:T(8,128)(2,1)S(1)} %get-tuple-element.24), channel_id=1, source_target_pairs={{0,64},{64,0},{1,65},{65,1},{2,66},{66,2},{3,67},{67,3},{4,68},{68... | collective-permute-start | bytes 1572872 | tf_op jit(solution)/shard_map/ppermute | solution.py:339
  71.7 43.1 %collective-permute-start.3 = (bf16[128,2048]{1,0:T(8,128)(2,1)S(1)}, bf16[128,2048]{1,0:T(8,128)(2,1)S(1)}, u32[]{:S(2)}, u32[]{:S(2)}) collective-permute-start(bf16[128,2048]{1,0:T(8,128)(2,1)S(1)} %get-tuple-element.22), channel_id=1, source_target_pairs={{0,64},{64,0},{1,65},{65,1},{2,66},{66,2},{3,67},{67,3},{4,68},{68... | collective-permute-start | bytes 1572872 | tf_op jit(solution)/shard_map/ppermute | solution.py:339
  113.3 47.6 %collective-permute-start.11 = (bf16[10,128,256]{2,1,0:T(8,128)(2,1)S(1)}, bf16[10,128,256]{2,1,0:T(8,128)(2,1)S(1)}, u32[]{:S(2)}, u32[]{:S(2)}) collective-permute-start(bf16[10,128,256]{2,1,0:T(8,128)(2,1)S(1)} %get-tuple-element.33), channel_id=1, source_target_pairs={{0,64},{64,0},{1,65},{65,1},{2,66},{66,2},{3,67},{67,3},{4,68},{68... | collective-permute-start | bytes 1966088 | tf_op jit(solution)/shard_map/ppermute | solution.py:348
  113.3 46.2 %collective-permute-start.12 = (bf16[10,128,256]{2,1,0:T(8,128)(2,1)S(1)}, bf16[10,128,256]{2,1,0:T(8,128)(2,1)S(1)}, u32[]{:S(2)}, u32[]{:S(2)}) collective-permute-start(bf16[10,128,256]{2,1,0:T(8,128)(2,1)S(1)} %get-tuple-element.34), channel_id=1, source_target_pairs={{0,64},{64,0},{1,65},{65,1},{2,66},{66,2},{3,67},{67,3},{4,68},{68... | collective-permute-start | bytes 1966088 | tf_op jit(solution)/shard_map/ppermute | solution.py:348
  114.7 43.4 %collective-permute-start.13 = (bf16[10,128,256]{2,1,0:T(8,128)(2,1)S(1)}, bf16[10,128,256]{2,1,0:T(8,128)(2,1)S(1)}, u32[]{:S(2)}, u32[]{:S(2)}) collective-permute-start(bf16[10,128,256]{2,1,0:T(8,128)(2,1)S(1)} %get-tuple-element.35), channel_id=1, source_target_pairs={{0,64},{64,0},{1,65},{65,1},{2,66},{66,2},{3,67},{67,3},{4,68},{68... | collective-permute-start | bytes 1966088 | tf_op jit(solution)/shard_map/ppermute | solution.py:348
  123.1 48.1 %collective-permute-start.10 = (bf16[10,128,256]{2,1,0:T(8,128)(2,1)S(1)}, bf16[10,128,256]{2,1,0:T(8,128)(2,1)S(1)}, u32[]{:S(2)}, u32[]{:S(2)}) collective-permute-start(bf16[10,128,256]{2,1,0:T(8,128)(2,1)S(1)} %get-tuple-element.32), channel_id=1, source_target_pairs={{0,64},{64,0},{1,65},{65,1},{2,66},{66,2},{3,67},{67,3},{4,68},{68... | collective-permute-start | bytes 1966088 | tf_op jit(solution)/shard_map/ppermute | solution.py:348
where the time goes:
time: 173 us
  waiting for transfers between devices  101 us (58%)
  Pallas kernels  44.7 us (26%)
  starting transfers between devices  20.4 us (12%)
  local copies, waits for them, and re-layouts  6.67 us (4%)
    ppermute x4, waiting for transfers between devices, per_device(): arrived.append(lax.ppermute(sent, 'mem', swap))  42.5 us
    pallas_call x4, Pallas kernels, analyse(): pl.pallas_call(functools.partial(analysis_body, chunk=chunk, blocks_dev=b...  33.9 us
    ppermute x1, waiting for transfers between devices, per_device(): low = lax.ppermute(own, both, from_low)  23.3 us
    ppermute x1, waiting for transfers between devices, per_device(): high = lax.ppermute(own, both, from_high)  15.5 us
    ppermute x4, waiting for transfers between devices, per_device(): received.append(lax.ppermute(to_send[chunk], 'mem', swap))  11.8 us
    ppermute x1, waiting for transfers between devices, per_device(): table_high = lax.ppermute(table, both, from_high)  6.18 us
    ppermute x1, starting transfers between devices, per_device(): low = lax.ppermute(own, both, from_low)  5.68 us
    pallas_call x4, Pallas kernels, place(): pl.pallas_call(functools.partial(place_body, chunk=chunk), grid_spec=pltp...  5.56 us
  transfers between devices with their start and end apart: 14, of which 9 were waited for; matrix products, arithmetic and copies ran while one was open for 3% of the time, Pallas kernels for 25%

commit v1 on v0

--- a/solution.py
+++ b/solution.py
@@ -25,60 +25,90 @@
     return pairs
 
 
-def gather_body(lists, meta, low, own, high, *refs, for_self, chunks, blocks_dev, width):
-    outs = refs[:chunks]
-    sems = refs[chunks]
+def locate(lists, meta, row, n, blocks_dev):
+    mem, tile = meta[0], meta[1]
+    parity = lax.rem(tile, 2)
+    local = lists[n, row] - (tile - 1) * blocks_dev
+    which = lax.div(local, blocks_dev)
+    inside = local - which * blocks_dev
+    crossed = ((which == 0) & (parity == 0)) | ((which == 2) & (parity == 1))
+    source = jnp.where(crossed, 1 - mem, mem)
+    part = lax.div(inside, blocks_dev // 2)
+    return which, inside, source, part == source, inside - part * (blocks_dev // 2)
+
+
+def gather_body(lists, meta, *refs, for_self, chunks, blocks_dev, width):
+    tiles = [(refs[2 * k], refs[2 * k + 1]) for k in range(3)]
+    outs = refs[6 : 6 + chunks]
+    sem = refs[6 + chunks]
     nloc, count = lists.shape
     half = count // 2
-    mem, tile = meta[0], meta[1]
-    base = (tile - 1) * blocks_dev
-    owner = mem if for_self else 1 - mem
+    owner = meta[0] if for_self else 1 - meta[0]
     per_chunk = half // chunks
+    rows = tiles[0][0].shape[0]
+
     for chunk in range(chunks):
         out = outs[chunk]
-        for block in range(per_chunk):
+
+        @pl.loop(0, per_chunk * nloc)
+        def _(slot, chunk=chunk, out=out):
+            block = lax.div(slot, nloc)
+            n = slot - block * nloc
             row = owner * half + chunk * per_chunk + block
-            for n in range(nloc):
-                local = lists[n, row] - base
-                which = lax.div(local, blocks_dev)
-                start = pl.multiple_of((local - which * blocks_dev) * width, width)
-                target = out.at[:, pl.ds((block * nloc + n) * width, width)]
-                for index, source in enumerate((low, own, high)):
-
-                    @pl.when(which == index)
-                    def _(source=source):
-                        pltpu.make_async_copy(
-                            source.at[:, pl.ds(start, width)], target, sems.at[chunk]
-                        ).start()
+            which, _, source, here, index = locate(lists, meta, row, n, blocks_dev)
+            start = pl.multiple_of(index * width, width)
+            at = pl.ds(pl.multiple_of(slot * width, width), width)
+            first = pl.multiple_of(jnp.where(source == owner, 0, rows), rows)
+            second = pl.multiple_of(jnp.where(source == owner, rows, 0), rows)
+            for k, (own_part, other_part) in enumerate(tiles):
+
+                @pl.when(here & (which == k))
+                def _(own_part=own_part, other_part=other_part):
+                    pltpu.make_async_copy(
+                        own_part.at[:, pl.ds(start, width)], out.at[pl.ds(first, rows), at], sem
+                    ).start()
+                    pltpu.make_async_copy(
+                        other_part.at[:, pl.ds(start, width)], out.at[pl.ds(second, rows), at], sem
+                    ).start()
 
     for chunk in range(chunks):
-        size = outs[chunk].shape[1]
-        pltpu.make_async_copy(own.at[:, pl.ds(0, size)], outs[chunk], sems.at[chunk]).wait()
-
-
-def gather_blocks(lists, meta, low, own, high, for_self, blocks_dev, width):
+        out = outs[chunk]
+
+        @pl.loop(0, per_chunk * nloc)
+        def _(slot, chunk=chunk, out=out):
+            block = lax.div(slot, nloc)
+            row = owner * half + chunk * per_chunk + block
+            _, _, _, here, _ = locate(lists, meta, row, slot - block * nloc, blocks_dev)
+
+            @pl.when(here)
+            def _():
+                whole = out.at[:, pl.ds(0, width)]
+                pltpu.make_async_copy(whole, whole, sem).wait()
+
+
+def gather_blocks(lists, meta, tiles, for_self, chunks, blocks_dev, width):
     nloc, count = lists.shape
-    members = own.shape[0]
-    size = (count // 2 // CHUNKS) * nloc * width
+    members = 2 * tiles[0].shape[0]
+    size = (count // 2 // chunks) * nloc * width
     whole = pl.BlockSpec((members, size), lambda i, *_: (0, 0))
     return pl.pallas_call(
         functools.partial(
-            gather_body, for_self=for_self, chunks=CHUNKS, blocks_dev=blocks_dev, width=width
+            gather_body, for_self=for_self, chunks=chunks, blocks_dev=blocks_dev, width=width
         ),
         grid_spec=pltpu.PrefetchScalarGridSpec(
             num_scalar_prefetch=2,
             grid=(1,),
-            in_specs=[pl.BlockSpec(memory_space=pltpu.HBM)] * 3,
-            out_specs=[whole] * CHUNKS,
-            scratch_shapes=[pltpu.SemaphoreType.DMA((CHUNKS,))],
-        ),
-        out_shape=[jax.ShapeDtypeStruct((members, size), own.dtype)] * CHUNKS,
+            in_specs=[pl.BlockSpec(memory_space=pl.ANY)] * 6,
+            out_specs=[whole] * chunks,
+            scratch_shapes=[pltpu.SemaphoreType.DMA],
+        ),
+        out_shape=[jax.ShapeDtypeStruct((members, size), tiles[0].dtype)] * chunks,
         cost_estimate=pl.CostEstimate(
-            flops=0, bytes_accessed=4 * CHUNKS * members * size, transcendentals=0
-        ),
-        compiler_params=pltpu.CompilerParams(vmem_limit_bytes=8 << 20),
+            flops=0, bytes_accessed=2 * chunks * members * size, transcendentals=0
+        ),
+        compiler_params=pltpu.CompilerParams(vmem_limit_bytes=12 << 20),
         name="gather_self" if for_self else "gather_send",
-    )(lists, meta, low, own, high)
+    )(lists, meta, *tiles)
 
 
 def split(value):
@@ -98,66 +128,152 @@
     return dot(lh, rh) + (dot(lh, rl) + dot(ll, rh))
 
 
+def parts3(value):
+    high = value.astype(jnp.bfloat16)
+    mid, low = split(value - high.astype(jnp.float32))
+    return [high, mid, low]
+
+
+def local_gram(lists, meta, row, held, low, own, high, ybuf, sbuf, blocks_dev, width):
+    nloc = lists.shape[0]
+    members = held.shape[0]
+    for n in range(nloc):
+        which, inside, _, here, _ = locate(lists, meta, row, n, blocks_dev)
+        at = pl.ds(n * width, width)
+
+        @pl.when(jnp.logical_not(here))
+        def _(at=at):
+            ybuf[:, at] = jnp.zeros((members + ROWS, width), jnp.bfloat16)
+            sbuf[:, at] = jnp.zeros((members, width), jnp.bfloat16)
+
+        @pl.when(here)
+        def _(at=at, which=which, inside=inside):
+            raw = held[:, at].astype(jnp.float32)
+            mean = jnp.sum(raw, axis=0, keepdims=True) / members
+
+            def entry(index):
+                at_low = low[pl.ds(index, 1), :]
+                at_own = own[pl.ds(index, 1), :]
+                at_high = high[pl.ds(index, 1), :]
+                return jnp.where(which == 0, at_low, jnp.where(which == 1, at_own, at_high))
+
+            value = entry(inside)
+            weight = entry(inside + blocks_dev)
+            ybuf[pl.ds(members, ROWS), at] = jnp.concatenate(
+                [*parts3(value - mean), jnp.zeros((ROWS - 3, width), jnp.bfloat16)], axis=0
+            )
+            pert = (raw - mean).astype(jnp.bfloat16)
+            ybuf[pl.ds(0, members), at] = pert
+            sbuf[:, at] = (pert.astype(jnp.float32) * weight).astype(jnp.bfloat16)
+
+    gram = lax.dot_general(
+        ybuf[...], sbuf[...], (((1,), (1,)), ((), ())), preferred_element_type=jnp.float32
+    )
+    return gram[:members], jnp.sum(gram[members:], axis=0, keepdims=True)
+
+
+def on_diagonal(size):
+    return lax.broadcasted_iota(jnp.int32, (size, size), 0) == lax.broadcasted_iota(
+        jnp.int32, (size, size), 1
+    )
+
+
+def partial_body(lists, meta, held, low, own, high, *refs, blocks_dev, width):
+    outs, ybuf, sbuf = refs[:CHUNKS], refs[CHUNKS], refs[CHUNKS + 1]
+    half = lists.shape[1] // 2
+    block = pl.program_id(0)
+    matrix, rhs = local_gram(
+        lists, meta, (1 - meta[0]) * half + block, held, low, own, high, ybuf, sbuf,
+        blocks_dev, width,
+    )
+    members = matrix.shape[0]
+    q = members // 4
+    diagonal = jnp.sum(jnp.where(on_diagonal(members), matrix, 0.0), axis=0, keepdims=True)
+    lane = lax.broadcasted_iota(jnp.int32, (q, members), 1)
+    second = jnp.where(lane < q, pltpu.roll(matrix[3 * q :], q, 1), matrix[q : 2 * q])
+    third = jnp.concatenate(
+        [matrix[2 * q + q // 2 : 3 * q, 2 * q :], matrix[2 * q : 2 * q + q // 2, 2 * q :]], axis=1
+    )
+    extra = jnp.concatenate(
+        [*parts3(rhs), *parts3(diagonal), jnp.zeros((ROWS - 6, members), jnp.bfloat16)], axis=0
+    )
+    per_chunk = half // CHUNKS
+    for chunk in range(CHUNKS):
+
+        @pl.when((block >= chunk * per_chunk) & (block < (chunk + 1) * per_chunk))
+        def _(out=outs[chunk]):
+            out[0, pl.ds(0, q), :] = matrix[:q].astype(jnp.bfloat16)
+            out[0, pl.ds(q, q), :] = second.astype(jnp.bfloat16)
+            out[0, pl.ds(2 * q, q // 2), :] = third.astype(jnp.bfloat16)
+            out[0, pl.ds(2 * q + q // 2, ROWS), :] = extra
+
+
+def partial_sums(lists, meta, held, tables, blocks_dev, width):
+    nloc, count = lists.shape
+    half = count // 2
+    per_chunk = half // CHUNKS
+    members = held.shape[0]
+    span = nloc * width
+    packed = (1, members // 2 + members // 8 + ROWS, members)
+    table_spec = pl.BlockSpec(tables[0].shape, lambda i, *_: (0, 0))
+
+    def out_spec(chunk):
+        return pl.BlockSpec(
+            packed, lambda i, *_: (jnp.clip(i - chunk * per_chunk, 0, per_chunk - 1), 0, 0)
+        )
+
+    return pl.pallas_call(
+        functools.partial(partial_body, blocks_dev=blocks_dev, width=width),
+        grid_spec=pltpu.PrefetchScalarGridSpec(
+            num_scalar_prefetch=2,
+            grid=(half,),
+            in_specs=[pl.BlockSpec((members, span), lambda i, *_: (0, i))] + [table_spec] * 3,
+            out_specs=[out_spec(chunk) for chunk in range(CHUNKS)],
+            scratch_shapes=[
+                pltpu.VMEM((members + ROWS, span), jnp.bfloat16),
+                pltpu.VMEM((members, span), jnp.bfloat16),
+            ],
+        ),
+        out_shape=[jax.ShapeDtypeStruct((per_chunk, *packed[1:]), jnp.bfloat16)] * CHUNKS,
+        cost_estimate=pl.CostEstimate(
+            flops=2 * half * members * members * span,
+            bytes_accessed=2 * members * half * span,
+            transcendentals=0,
+        ),
+        compiler_params=pltpu.CompilerParams(vmem_limit_bytes=16 << 20),
+        name="partial_sums",
+    )(lists, meta, held, *tables)
+
+
 def analysis_body(
     lists, meta, mine, theirs, held, received, low, own, high, *refs, chunk, blocks_dev, width
 ):
-    kept, sent, table, ybuf, sbuf, xbuf, mbuf = refs[-7:]
-    nloc, count = lists.shape
-    half = count // 2
-    mem, tile = meta[0], meta[1]
-    parity = lax.rem(tile, 2)
-    base = (tile - 1) * blocks_dev
-    block = pl.program_id(0)
-    row = mem * half + chunk * (half // CHUNKS) + block
-    rows = held.shape[0]
+    kept, sent, ubuf, ybuf, sbuf, xbuf, mbuf = refs[-7:]
+    half = lists.shape[1] // 2
+    row = meta[0] * half + chunk * (half // CHUNKS) + pl.program_id(0)
+    rows = mine.shape[1]
     members = 2 * rows
-    side = table.shape[0] // 3
-
-    @pl.when(block == 0)
-    def _():
-        for index, source in enumerate((low, own, high)):
-            table[pl.ds(index * side, side), :] = source[...]
-        ybuf[pl.ds(members, ROWS), :] = jnp.zeros((ROWS, nloc * width), jnp.bfloat16)
-
-    for n in range(nloc):
-        local = lists[n, row] - base
-        which = lax.div(local, blocks_dev)
-        entry = which * side + (local - which * blocks_dev)
-        crossed = ((which == 0) & (parity == 0)) | ((which == 2) & (parity == 1))
-        at = pl.ds(n * width, width)
-        first = held[:, at].astype(jnp.float32)
-        second = received[:, at].astype(jnp.float32)
-        mean = (
-            jnp.sum(first, axis=0, keepdims=True) + jnp.sum(second, axis=0, keepdims=True)
-        ) / members
-        value = table[pl.ds(entry, 1), :]
-        weight = table[pl.ds(entry + blocks_dev, 1), :]
-        innov = value - mean
-        d0 = innov.astype(jnp.bfloat16)
-        rest = innov - d0.astype(jnp.float32)
-        d1, d2 = split(rest)
-        ybuf[pl.ds(members, ROWS), at] = jnp.concatenate(
-            [d0, d1, d2, jnp.zeros((ROWS - 3, width), jnp.bfloat16)], axis=0
-        )
-        pert1 = (first - mean).astype(jnp.bfloat16)
-        pert2 = (second - mean).astype(jnp.bfloat16)
-        scaled1 = (pert1.astype(jnp.float32) * weight).astype(jnp.bfloat16)
-        scaled2 = (pert2.astype(jnp.float32) * weight).astype(jnp.bfloat16)
-        place1 = pl.multiple_of(jnp.where(crossed, rows, 0), rows)
-        place2 = pl.multiple_of(jnp.where(crossed, 0, rows), rows)
-        ybuf[pl.ds(place1, rows), at] = pert1
-        ybuf[pl.ds(place2, rows), at] = pert2
-        sbuf[pl.ds(place1, rows), at] = scaled1
-        sbuf[pl.ds(place2, rows), at] = scaled2
-
-    gram = lax.dot_general(
-        ybuf[...], sbuf[...], (((1,), (1,)), ((), ())), preferred_element_type=jnp.float32
-    )
-    matrix = gram[:members]
-    rhs = jnp.sum(gram[members:], axis=0, keepdims=True)
-    diagonal = lax.broadcasted_iota(jnp.int32, (members, members), 0) == lax.broadcasted_iota(
-        jnp.int32, (members, members), 1
-    )
+
+    matrix, rhs = local_gram(
+        lists, meta, row, held, low, own, high, ybuf, sbuf, blocks_dev, width
+    )
+    q = members // 4
+    ubuf[pl.ds(0, q), :] = received[0, pl.ds(0, q), :].astype(jnp.float32)
+    second = received[0, pl.ds(q, q), :].astype(jnp.float32)
+    ubuf[pl.ds(q, q), :] = second
+    third = received[0, pl.ds(2 * q, q // 2), :].astype(jnp.float32)
+    ubuf[pl.ds(2 * q, q // 2), pl.ds(2 * q, 2 * q)] = third[:, 2 * q :]
+    ubuf[pl.ds(2 * q + q // 2, q // 2), pl.ds(2 * q, 2 * q)] = third[:, : 2 * q]
+    ubuf[pl.ds(3 * q, q), :] = pltpu.roll(second, 3 * q, 1)
+    extra = received[0, pl.ds(2 * q + q // 2, ROWS), :].astype(jnp.float32)
+    rhs = rhs + jnp.sum(extra[:3], axis=0, keepdims=True)
+    upper = ubuf[...]
+    block_row = lax.div(lax.broadcasted_iota(jnp.int32, (members, members), 0), q)
+    block_col = lax.div(lax.broadcasted_iota(jnp.int32, (members, members), 1), q)
+    other = jnp.where(block_row <= block_col, upper, upper.T)
+    diagonal = on_diagonal(members)
+    other = jnp.where(diagonal, jnp.sum(extra[3:6], axis=0, keepdims=True), other)
+    matrix = matrix + other
     matrix = matrix + jnp.where(diagonal, members - 1.0, 0.0)
     trace = jnp.sum(
         jnp.sum(jnp.where(diagonal, matrix, 0.0), axis=0, keepdims=True), axis=1, keepdims=True
@@ -200,7 +316,7 @@
 
 
 def analyse(
-    lists, meta, mine, theirs, held, received, tables, output, chunk, skipped, blocks_dev, width
+    lists, meta, mine, theirs, held, received, tables, output, chunk, blocks_dev, width
 ):
     nloc, count = lists.shape
     half = count // 2
@@ -217,9 +333,9 @@
     table_spec = pl.BlockSpec(tables[0].shape, lambda i, *_: (0, 0))
     in_specs = [
         pl.BlockSpec(tile_block, mine_at),
-        pl.BlockSpec(tile_block, lambda i, *_: (0, 0, (chunk - skipped) * per_chunk + i)),
-        pl.BlockSpec((rows, span), lambda i, *_: (0, i)),
-        pl.BlockSpec((rows, span), lambda i, *_: (0, i)),
+        pl.BlockSpec(tile_block, lambda i, *_: (0, 0, chunk * per_chunk + i)),
+        pl.BlockSpec((members, span), lambda i, *_: (0, i)),
+        pl.BlockSpec((1, *received.shape[1:]), lambda i, *_: (i, 0, 0)),
         table_spec,
         table_spec,
         table_spec,
@@ -241,7 +357,7 @@
                 pl.BlockSpec(tile_block, lambda i, *_: (0, 0, i)),
             ],
             scratch_shapes=[
-                pltpu.VMEM((3 * tables[0].shape[0], width), jnp.float32),
+                pltpu.VMEM((members, members), jnp.float32),
                 pltpu.VMEM((members + ROWS, span), jnp.bfloat16),
                 pltpu.VMEM((members, span), jnp.bfloat16),
                 pltpu.VMEM((members, layers * width), jnp.bfloat16),
@@ -316,15 +432,19 @@
     lists = neighbour_lists.T
     meta = jnp.stack([member_no, tile_no]).astype(jnp.int32)
 
-    own = members_in_reading_space
+    obs = members_in_reading_space
+    obs_half = obs.shape[1] // 2
+    other_set = lax.dynamic_slice_in_dim(obs, (1 - member_no) * obs_half, obs_half, 1)
+    swapped = lax.ppermute(other_set, "mem", swap)
+    own_set = lax.dynamic_slice_in_dim(obs, member_no * obs_half, obs_half, 1)
+    low_own = lax.ppermute(own_set, both, from_low)
+    high_own = lax.ppermute(own_set, both, from_high)
     half = cols // 2
-    piece = half // CHUNKS
-    prior = []
-    for start, size in ((0, piece), (piece, half - piece)):
-        outgoing = lax.dynamic_slice_in_dim(mine, (1 - member_no) * half + start, size, 2)
-        prior.append(lax.ppermute(outgoing, "mem", swap))
-    low = lax.ppermute(own, both, from_low)
-    high = lax.ppermute(own, both, from_high)
+    outgoing = lax.dynamic_slice_in_dim(mine, (1 - member_no) * half, half, 2)
+    theirs = lax.ppermute(outgoing, "mem", swap)
+    low_other = lax.ppermute(swapped, both, from_low)
+    high_other = lax.ppermute(swapped, both, from_high)
+    tiles_held = (low_own, low_other, own_set, swapped, high_own, high_other)
     slots = jnp.arange(width, dtype=jnp.int32)
     valid = slots[None, :] < valid_reading_numbers[:, None]
     weight = jnp.where(valid, obs_precision_weights.reshape(blocks_dev, width), 0.0)
@@ -333,17 +453,18 @@
     table_high = lax.ppermute(table, both, from_high)
     tables = (table_low, table, table_high)
 
-    to_send = gather_blocks(lists, meta, low, own, high, False, blocks_dev, width)
+    (to_send,) = gather_blocks(lists, meta, tiles_held, False, 1, blocks_dev, width)
+    sums = partial_sums(lists, meta, to_send, tables, blocks_dev, width)
     received = []
     for chunk in range(CHUNKS):
-        received.append(lax.ppermute(to_send[chunk], "mem", swap))
-    held = gather_blocks(lists, meta, low, own, high, True, blocks_dev, width)
+        received.append(lax.ppermute(sums[chunk], "mem", swap))
+    held = gather_blocks(lists, meta, tiles_held, True, CHUNKS, blocks_dev, width)
     output = None
     arrived = []
     for chunk in range(CHUNKS):
         output, sent = analyse(
-            lists, meta, mine, prior[min(chunk, 1)], held[chunk], received[chunk], tables,
-            output, chunk, min(chunk, 1), blocks_dev, width,
+            lists, meta, mine, theirs, held[chunk], received[chunk], tables, output, chunk,
+            blocks_dev, width,
         )
         arrived.append(lax.ppermute(sent, "mem", swap))
     for chunk in range(CHUNKS):

time: 173 us -> 223 us (1.29)
  the two profiles are of different devices: /device:TPU:1 before, /device:TPU:25 now
where the time goes in v1:
time: 223 us; the launch traced here: 222 us
  waiting for transfers between devices  125 us (56%)
  Pallas kernels  58.8 us (26%)
  starting transfers between devices  31.1 us (14%)
  local copies, waits for them, and re-layouts  6.22 us (3%)
    ppermute x1, waiting for transfers between devices, per_device(): swapped = lax.ppermute(other_set, 'mem', swap)  68 us
    ppermute x4, waiting for transfers between devices, per_device(): arrived.append(lax.ppermute(sent, 'mem', swap))  41.6 us
    pallas_call x4, Pallas kernels, analyse(): pl.pallas_call(functools.partial(analysis_body, chunk=chunk, blocks_dev=b...  36 us
    ppermute x1, waiting for transfers between devices, per_device(): high_other = lax.ppermute(swapped, both, from_high)  15.8 us
    pallas_call x2, Pallas kernels, gather_blocks(): pl.pallas_call(functools.partial(gather_body, for_self=for_self, chunks=c...  8.68 us
    pallas_call x1, Pallas kernels, partial_sums(): pl.pallas_call(functools.partial(partial_body, blocks_dev=blocks_dev, wid...  8.56 us
    ppermute x1, starting transfers between devices, per_device(): low_own = lax.ppermute(own_set, both, from_low)  5.56 us
    pallas_call x4, Pallas kernels, place(): pl.pallas_call(functools.partial(place_body, chunk=chunk), grid_spec=pltp...  5.56 us
  transfers between devices with their start and end apart: 16, of which 4 were waited for; matrix products, arithmetic and copies ran while one was open for 1% of the time, Pallas kernels for 26%

profile of v1, /device:TPU:25, one launch (start us, length us, event | category | flops | bytes accessed | tf_op | source)
XLA Modules:
  0.0 222.2 jit_solution(16548499272450039970)
XLA Ops:
  0.0 0.0 copy-start.3
  0.0 0.0 copy-start.1
  0.0 0.0 copy-start.2
  0.0 0.0 copy-start
  0.0 3.5 %dynamic-slice_bitcast_fusion = bf16[10,128,1024]{2,1,0:T(8,128)(2,1)} fusion(bf16[128,10,2048]{2,0,1:T(8,128)(2,1)} %param.6, s32[]{:T(128)S(6)} %select_n.13), kind=kLoop, calls=%fused_computation | loop fusion | bytes 5242884 | tf_op jit(solution)/shard_map/dynamic_slice | solution.py:443
  3.5 1.6 collective-permute-start
  5.2 2.7 %constant_dynamic-slice_fusion = (bf16[128,4096]{1,0:T(8,128)(2,1)S(1)}, bf16[128,4096]{1,0:T(8,128)(2,1)}) fusion(bf16[128,8192]{1,0:T(8,128)(2,1)} %param.7, s32[]{:T(128)S(6)} %select_n.15, s32[]{:T(128)S(6)} %select_n.14), kind=kLoop, calls=%fused_computation.4 | loop fusion | bytes 4194312 | tf_op jit(solution)/shard_map/dynamic_slice | solution.py:437
  7.9 0.0 collective-permute-start.2
  7.9 3.0 %collective-permute-start.4 = (bf16[128,4096]{1,0:T(8,128)(2,1)}, bf16[128,4096]{1,0:T(8,128)(2,1)}, u32[]{:S(2)}, u32[]{:S(2)}) collective-permute-start(bf16[128,4096]{1,0:T(8,128)(2,1)} %get-tuple-element.38.refs_2_), channel_id=1, source_target_pairs={{1,0},{66,1},{3,2},{68,3},{5,4},{70,5},{7,6},{72,7},{9,8},{74,9},{... | collective-permute-start | bytes 3145736 | tf_op jit(solution)/shard_map/ppermute | solution.py:441
  10.8 5.6 %collective-permute-start.1 = (bf16[128,4096]{1,0:T(8,128)(2,1)}, bf16[128,4096]{1,0:T(8,128)(2,1)}, u32[]{:S(2)}, u32[]{:S(2)}) collective-permute-start(bf16[128,4096]{1,0:T(8,128)(2,1)} %get-tuple-element.38.refs_2_), channel_id=1, source_target_pairs={{0,1},{65,2},{2,3},{67,4},{4,5},{69,6},{6,7},{71,8},{8,9},{73,10},... | collective-permute-start | bytes 3145736 | tf_op jit(solution)/shard_map/ppermute | solution.py:440
  16.4 68.0 %collective-permute-done.2.refs_3_ = bf16[128,4096]{1,0:T(8,128)(2,1)} collective-permute-done((bf16[128,4096]{1,0:T(8,128)(2,1)S(1)}, bf16[128,4096]{1,0:T(8,128)(2,1)}, u32[]{:S(2)}, u32[]{:S(2)}) %collective-permute-start.2) | collective-permute-done | bytes 1048608 | tf_op jit(solution)/shard_map/ppermute | solution.py:438
  84.4 3.3 %collective-permute-start.5 = (bf16[128,4096]{1,0:T(8,128)(2,1)}, bf16[128,4096]{1,0:T(8,128)(2,1)}, u32[]{:S(2)}, u32[]{:S(2)}) collective-permute-start(bf16[128,4096]{1,0:T(8,128)(2,1)} %collective-permute-done.2.refs_3_), channel_id=1, source_target_pairs={{1,0},{66,1},{3,2},{68,3},{5,4},{70,5},{7,6},{72,7},{9,8},{74,9},{... | collective-permute-start | bytes 3145736 | tf_op jit(solution)/shard_map/ppermute | solution.py:446
  87.7 5.4 %collective-permute-start.3 = (bf16[128,4096]{1,0:T(8,128)(2,1)}, bf16[128,4096]{1,0:T(8,128)(2,1)}, u32[]{:S(2)}, u32[]{:S(2)}) collective-permute-start(bf16[128,4096]{1,0:T(8,128)(2,1)} %collective-permute-done.2.refs_3_), channel_id=1, source_target_pairs={{0,1},{65,2},{2,3},{67,4},{4,5},{69,6},{6,7},{71,8},{8,9},{73,10},... | collective-permute-start | bytes 3145736 | tf_op jit(solution)/shard_map/ppermute | solution.py:445
  93.1 0.0 copy-done.3
  93.1 0.0 copy-done.1
  93.1 0.1 bitcast_select_fusion
  93.2 0.0 copy-done.2
  93.2 0.0 collective-permute-done.4.refs_4_
  93.2 3.3 %collective-permute-start.7 = (f32[128,128]{1,0:T(8,128)S(1)}, f32[128,128]{1,0:T(8,128)S(1)}, u32[]{:S(2)}, u32[]{:S(2)}) collective-permute-start(f32[128,128]{1,0:T(8,128)S(1)} %pad_maximum_fusion.own), channel_id=1, source_target_pairs={{1,0},{66,1},{3,2},{68,3},{5,4},{70,5},{7,6},{72,7},{9,8},{74,9},{... | collective-permute-start | bytes 196616 | tf_op jit(solution)/shard_map/ppermute | solution.py:453
  96.5 0.0 collective-permute-done.1.refs_0_
  96.5 3.5 %collective-permute-start.6 = (f32[128,128]{1,0:T(8,128)S(1)}, f32[128,128]{1,0:T(8,128)S(1)}, u32[]{:S(2)}, u32[]{:S(2)}) collective-permute-start(f32[128,128]{1,0:T(8,128)S(1)} %pad_maximum_fusion.own), channel_id=1, source_target_pairs={{0,1},{65,2},{2,3},{67,4},{4,5},{69,6},{6,7},{71,8},{8,9},{73,10},... | collective-permute-start | bytes 196616 | tf_op jit(solution)/shard_map/ppermute | solution.py:452
  100.0 0.1 pad_add_fusion.meta
  100.1 15.8 %collective-permute-done.5.refs_5_ = bf16[128,4096]{1,0:T(8,128)(2,1)} collective-permute-done((bf16[128,4096]{1,0:T(8,128)(2,1)}, bf16[128,4096]{1,0:T(8,128)(2,1)}, u32[]{:S(2)}, u32[]{:S(2)}) %collective-permute-start.5) | collective-permute-done | bytes 1048608 | tf_op jit(solution)/shard_map/ppermute | solution.py:446
  115.9 0.0 collective-permute-done.3.refs_1_
  115.9 0.0 copy-done
  115.9 0.0 slice-start
  115.9 4.3 %gather_send.1.held = bf16[256,8192]{1,0:T(8,128)(2,1)S(1)} custom-call(s32[8,16]{1,0:T(8,128)S(1)} %bitcast.16, s32[2]{0:T(128)S(1)} %pad_add_fusion.meta, bf16[128,4096]{1,0:T(8,128)(2,1)} %collective-permute-done.1.refs_0_, bf16[128,4096]{1,0:T(8,128)(2,1)} %collective-permute-done.3.refs_1_, bf16[128,4096]{1,0:T(8,128)(2,1)} %get-tuple-element.38.refs_2_, ...), custom_call_target="tpu_custom_call" | custom-call | bytes 4194304 | tf_op jit(solution)/shard_map/gather_send/pallas_call | solution.py:94
  120.2 0.0 slice-start.1
  120.2 0.0 collective-permute-done.7.high
  120.3 0.0 collective-permute-done.6.low
  120.3 8.6 %partial_sums.1 = (bf16[2,176,256]{2,1,0:T(8,128)(2,1)S(1)}, bf16[2,176,256]{2,1,0:T(8,128)(2,1)S(1)}, bf16[2,176,256]{2,1,0:T(8,128)(2,1)S(1)}, bf16[2,176,256]{2,1,0:T(8,128)(2,1)S(1)}) custom-call(s32[8,16]{1,0:T(8,128)S(1)} %bitcast.17, s32[2]{0:T(128)S(1)} %pad_add_fusion.meta, bf16[256,8192]{1,0:T(8,128)(2,1)S(1)} %gather_send.1.held, ...), custom_call_target="tpu_custom_call" | custom-call | flops 1073741824 | bytes 4194304 | tf_op jit(solution)/shard_map/partial_sums/pallas_call | solution.py:225
  128.8 0.1 collective-permute-start.11
  128.9 1.5 collective-permute-start.10
  130.4 0.1 collective-permute-start.8
  130.5 1.4 collective-permute-start.9
  131.9 4.3 %gather_self.1 = (bf16[256,2048]{1,0:T(8,128)(2,1)S(1)}, bf16[256,2048]{1,0:T(8,128)(2,1)S(1)}, bf16[256,2048]{1,0:T(8,128)(2,1)S(1)}, bf16[256,2048]{1,0:T(8,128)(2,1)S(1)}) custom-call(s32[8,16]{1,0:T(8,128)S(1)} %bitcast.18, s32[2]{0:T(128)S(1)} %pad_add_fusion.meta, bf16[128,4096]{1,0:T(8,128)(2,1)} %collective-permute-done.1.refs_0_, ...), custom_call_target="tpu_custom_call" | custom-call | bytes 4194304 | tf_op jit(solution)/shard_map/gather_self/pallas_call | solution.py:94
  136.2 0.0 collective-permute-done.11.received
  136.2 0.0 collective-permute-done.theirs
  136.2 0.0 slice-done
  136.2 0.0 slice-done.1
  136.2 9.1 %analyse.4 = (bf16[10,128,2048]{2,1,0:T(8,128)(2,1)}, bf16[10,128,256]{2,1,0:T(8,128)(2,1)S(1)}) custom-call(s32[8,16]{1,0:T(8,128)S(1)} %bitcast.19, s32[2]{0:T(128)S(1)} %pad_add_fusion.meta, bf16[10,128,2048]{2,1,0:T(8,128)(2,1)S(1)} %bitcast.12, bf16[10,128,1024]{2,1,0:T(8,128)(2,1)S(1)} %collective-permute-done.theirs, ...), custom_call_target="tpu_custom_call" | custom-call | flops 1811939328 | bytes 3670016 | tf_op jit(solution)/shard_map/analyse/pallas_call | solution.py:349
  145.3 0.0 collective-permute-done.10.received
  145.3 8.9 %analyse.5 = (bf16[10,128,2048]{2,1,0:T(8,128)(2,1)}, bf16[10,128,256]{2,1,0:T(8,128)(2,1)S(1)}) custom-call(s32[8,16]{1,0:T(8,128)S(1)} %bitcast.20, s32[2]{0:T(128)S(1)} %pad_add_fusion.meta, bf16[10,128,2048]{2,1,0:T(8,128)(2,1)S(1)} %bitcast.13, bf16[10,128,1024]{2,1,0:T(8,128)(2,1)S(1)} %collective-permute-done.theirs, ...), custom_call_target="tpu_custom_call", output_to_operand_aliasing={{0}: (9, {})} | custom-call | flops 1811939328 | bytes 3670016 | tf_op jit(solution)/shard_map/analyse/pallas_call | solution.py:349
  154.3 0.0 collective-permute-done.9.received
  154.3 8.8 %analyse.6 = (bf16[10,128,2048]{2,1,0:T(8,128)(2,1)}, bf16[10,128,256]{2,1,0:T(8,128)(2,1)S(1)}) custom-call(s32[8,16]{1,0:T(8,128)S(1)} %bitcast.21, s32[2]{0:T(128)S(1)} %pad_add_fusion.meta, bf16[10,128,2048]{2,1,0:T(8,128)(2,1)S(1)} %bitcast.14, bf16[10,128,1024]{2,1,0:T(8,128)(2,1)S(1)} %collective-permute-done.theirs, ...), custom_call_target="tpu_custom_call", output_to_operand_aliasing={{0}: (9, {})} | custom-call | flops 1811939328 | bytes 3670016 | tf_op jit(solution)/shard_map/analyse/pallas_call | solution.py:349
  163.1 0.3 collective-permute-start.13
  163.4 1.2 collective-permute-start.14
  164.6 0.3 collective-permute-start.15
  164.8 0.0 collective-permute-done.8.received
  164.8 9.2 %analyse.7 = (bf16[10,128,2048]{2,1,0:T(8,128)(2,1)}, bf16[10,128,256]{2,1,0:T(8,128)(2,1)S(1)}) custom-call(s32[8,16]{1,0:T(8,128)S(1)} %bitcast.22, s32[2]{0:T(128)S(1)} %pad_add_fusion.meta, bf16[10,128,2048]{2,1,0:T(8,128)(2,1)S(1)} %bitcast.15, bf16[10,128,1024]{2,1,0:T(8,128)(2,1)S(1)} %collective-permute-done.theirs, ...), custom_call_target="tpu_custom_call", output_to_operand_aliasing={{0}: (9, {})} | custom-call | flops 1811939328 | bytes 3670016 | tf_op jit(solution)/shard_map/analyse/pallas_call | solution.py:349
  174.0 0.8 collective-permute-start.12
  174.8 33.1 %collective-permute-done.15.piece = bf16[10,128,256]{2,1,0:T(8,128)(2,1)S(1)} collective-permute-done((bf16[10,128,256]{2,1,0:T(8,128)(2,1)S(1)}, bf16[10,128,256]{2,1,0:T(8,128)(2,1)S(1)}, u32[]{:S(2)}, u32[]{:S(2)}) %collective-permute-start.15) | collective-permute-done | bytes 655392 | tf_op jit(solution)/shard_map/ppermute | solution.py:469
  207.9 1.4 place.4.output
  209.3 0.0 collective-permute-done.14.piece
  209.3 1.4 place.5.output
  210.7 0.0 collective-permute-done.13.piece
  210.8 1.4 place.6.output
  212.2 8.5 %collective-permute-done.12.piece = bf16[10,128,256]{2,1,0:T(8,128)(2,1)S(1)} collective-permute-done((bf16[10,128,256]{2,1,0:T(8,128)(2,1)S(1)}, bf16[10,128,256]{2,1,0:T(8,128)(2,1)S(1)}, u32[]{:S(2)}, u32[]{:S(2)}) %collective-permute-start.12) | collective-permute-done | bytes 655392 | tf_op jit(solution)/shard_map/ppermute | solution.py:469
  220.7 1.4 place.7
  (2 shorter events, 0.0 us)
Async XLA Ops:
  0.0 93.1 %copy-start.3 = (s32[64]{0:T(128)S(1)}, s32[64]{0:T(128)}, u32[]{:S(2)}) copy-start(s32[64]{0:T(128)} %param.10) | copy-start | bytes 772
  0.0 93.1 %copy-start.1 = (f32[8192]{0:T(1024)S(1)}, f32[8192]{0:T(1024)}, u32[]{:S(2)}) copy-start(f32[8192]{0:T(1024)} %param.9) | copy-start | bytes 98308
  0.0 93.2 %copy-start.2 = (f32[8192]{0:T(1024)S(1)}, f32[8192]{0:T(1024)}, u32[]{:S(2)}) copy-start(f32[8192]{0:T(1024)} %param.8) | copy-start | bytes 98308
  0.0 115.9 %copy-start = (s32[16,8]{0,1:T(8,128)S(1)}, s32[16,8]{0,1:T(8,128)}, u32[]{:S(2)}) copy-start(s32[16,8]{0,1:T(8,128)} %param.11) | copy-start | bytes 1540
  3.5 132.7 %collective-permute-start = (bf16[10,128,1024]{2,1,0:T(8,128)(2,1)}, bf16[10,128,1024]{2,1,0:T(8,128)(2,1)S(1)}, u32[]{:S(2)}, u32[]{:S(2)}) collective-permute-start(bf16[10,128,1024]{2,1,0:T(8,128)(2,1)} %dynamic-slice_bitcast_fusion), channel_id=1, source_target_pairs={{0,64},{64,0},{1,65},{65,1},{2,66},{66,2},{3,67},{67,3},{4,68},{68... | collective-permute-start | bytes 7864328 | tf_op jit(solution)/shard_map/ppermute | solution.py:444
  7.9 76.6 %collective-permute-start.2 = (bf16[128,4096]{1,0:T(8,128)(2,1)S(1)}, bf16[128,4096]{1,0:T(8,128)(2,1)}, u32[]{:S(2)}, u32[]{:S(2)}) collective-permute-start(bf16[128,4096]{1,0:T(8,128)(2,1)S(1)} %get-tuple-element.37), channel_id=1, source_target_pairs={{0,64},{64,0},{1,65},{65,1},{2,66},{66,2},{3,67},{67,3},{4,68},{68... | collective-permute-start | bytes 3145736 | tf_op jit(solution)/shard_map/ppermute | solution.py:438
  7.9 85.3 %collective-permute-start.4 = (bf16[128,4096]{1,0:T(8,128)(2,1)}, bf16[128,4096]{1,0:T(8,128)(2,1)}, u32[]{:S(2)}, u32[]{:S(2)}) collective-permute-start(bf16[128,4096]{1,0:T(8,128)(2,1)} %get-tuple-element.38.refs_2_), channel_id=1, source_target_pairs={{1,0},{66,1},{3,2},{68,3},{5,4},{70,5},{7,6},{72,7},{9,8},{74,9},{... | collective-permute-start | bytes 3145736 | tf_op jit(solution)/shard_map/ppermute | solution.py:441
  10.8 85.7 %collective-permute-start.1 = (bf16[128,4096]{1,0:T(8,128)(2,1)}, bf16[128,4096]{1,0:T(8,128)(2,1)}, u32[]{:S(2)}, u32[]{:S(2)}) collective-permute-start(bf16[128,4096]{1,0:T(8,128)(2,1)} %get-tuple-element.38.refs_2_), channel_id=1, source_target_pairs={{0,1},{65,2},{2,3},{67,4},{4,5},{69,6},{6,7},{71,8},{8,9},{73,10},... | collective-permute-start | bytes 3145736 | tf_op jit(solution)/shard_map/ppermute | solution.py:440
  84.4 31.5 %collective-permute-start.5 = (bf16[128,4096]{1,0:T(8,128)(2,1)}, bf16[128,4096]{1,0:T(8,128)(2,1)}, u32[]{:S(2)}, u32[]{:S(2)}) collective-permute-start(bf16[128,4096]{1,0:T(8,128)(2,1)} %collective-permute-done.2.refs_3_), channel_id=1, source_target_pairs={{1,0},{66,1},{3,2},{68,3},{5,4},{70,5},{7,6},{72,7},{9,8},{74,9},{... | collective-permute-start | bytes 3145736 | tf_op jit(solution)/shard_map/ppermute | solution.py:446
  87.7 28.2 %collective-permute-start.3 = (bf16[128,4096]{1,0:T(8,128)(2,1)}, bf16[128,4096]{1,0:T(8,128)(2,1)}, u32[]{:S(2)}, u32[]{:S(2)}) collective-permute-start(bf16[128,4096]{1,0:T(8,128)(2,1)} %collective-permute-done.2.refs_3_), channel_id=1, source_target_pairs={{0,1},{65,2},{2,3},{67,4},{4,5},{69,6},{6,7},{71,8},{8,9},{73,10},... | collective-permute-start | bytes 3145736 | tf_op jit(solution)/shard_map/ppermute | solution.py:445
  93.2 27.0 %collective-permute-start.7 = (f32[128,128]{1,0:T(8,128)S(1)}, f32[128,128]{1,0:T(8,128)S(1)}, u32[]{:S(2)}, u32[]{:S(2)}) collective-permute-start(f32[128,128]{1,0:T(8,128)S(1)} %pad_maximum_fusion.own), channel_id=1, source_target_pairs={{1,0},{66,1},{3,2},{68,3},{5,4},{70,5},{7,6},{72,7},{9,8},{74,9},{... | collective-permute-start | bytes 196616 | tf_op jit(solution)/shard_map/ppermute | solution.py:453
  96.5 23.8 %collective-permute-start.6 = (f32[128,128]{1,0:T(8,128)S(1)}, f32[128,128]{1,0:T(8,128)S(1)}, u32[]{:S(2)}, u32[]{:S(2)}) collective-permute-start(f32[128,128]{1,0:T(8,128)S(1)} %pad_maximum_fusion.own), channel_id=1, source_target_pairs={{0,1},{65,2},{2,3},{67,4},{4,5},{69,6},{6,7},{71,8},{8,9},{73,10},... | collective-permute-start | bytes 196616 | tf_op jit(solution)/shard_map/ppermute | solution.py:452
  115.9 20.3 %slice-start = ((s8[5242880]{0:T(1024)(128)(4,1)}), s8[4194304]{0:T(1024)(128)(4,1)S(1)}, s32[]{:S(2)}) async-start(s8[5242880]{0:T(1024)(128)(4,1)} %bitcast.10), calls=%async_computation | async-start | bytes 8388608
  120.2 16.0 %slice-start.1 = ((s8[5242880]{0:T(1024)(128)(4,1)}), s8[1048576]{0:T(1024)(128)(4,1)S(1)}, s32[]{:S(2)}) async-start(s8[5242880]{0:T(1024)(128)(4,1)} %bitcast.10), calls=%async_computation.1 | async-start | bytes 2097152
  128.8 7.4 %collective-permute-start.11 = (bf16[2,176,256]{2,1,0:T(8,128)(2,1)S(1)}, bf16[2,176,256]{2,1,0:T(8,128)(2,1)S(1)}, u32[]{:S(2)}, u32[]{:S(2)}) collective-permute-start(bf16[2,176,256]{2,1,0:T(8,128)(2,1)S(1)} %get-tuple-element.28), channel_id=1, source_target_pairs={{0,64},{64,0},{1,65},{65,1},{2,66},{66,2},{3,67},{67,3},{4,68},{68... | collective-permute-start | bytes 540680 | tf_op jit(solution)/shard_map/ppermute | solution.py:460
  128.9 16.4 %collective-permute-start.10 = (bf16[2,176,256]{2,1,0:T(8,128)(2,1)S(1)}, bf16[2,176,256]{2,1,0:T(8,128)(2,1)S(1)}, u32[]{:S(2)}, u32[]{:S(2)}) collective-permute-start(bf16[2,176,256]{2,1,0:T(8,128)(2,1)S(1)} %get-tuple-element.26), channel_id=1, source_target_pairs={{0,64},{64,0},{1,65},{65,1},{2,66},{66,2},{3,67},{67,3},{4,68},{68... | collective-permute-start | bytes 540680 | tf_op jit(solution)/shard_map/ppermute | solution.py:460
  130.4 34.4 %collective-permute-start.8 = (bf16[2,176,256]{2,1,0:T(8,128)(2,1)S(1)}, bf16[2,176,256]{2,1,0:T(8,128)(2,1)S(1)}, u32[]{:S(2)}, u32[]{:S(2)}) collective-permute-start(bf16[2,176,256]{2,1,0:T(8,128)(2,1)S(1)} %get-tuple-element.22), channel_id=1, source_target_pairs={{0,64},{64,0},{1,65},{65,1},{2,66},{66,2},{3,67},{67,3},{4,68},{68... | collective-permute-start | bytes 540680 | tf_op jit(solution)/shard_map/ppermute | solution.py:460
  130.5 23.8 %collective-permute-start.9 = (bf16[2,176,256]{2,1,0:T(8,128)(2,1)S(1)}, bf16[2,176,256]{2,1,0:T(8,128)(2,1)S(1)}, u32[]{:S(2)}, u32[]{:S(2)}) collective-permute-start(bf16[2,176,256]{2,1,0:T(8,128)(2,1)S(1)} %get-tuple-element.24), channel_id=1, source_target_pairs={{0,64},{64,0},{1,65},{65,1},{2,66},{66,2},{3,67},{67,3},{4,68},{68... | collective-permute-start | bytes 540680 | tf_op jit(solution)/shard_map/ppermute | solution.py:460
  163.1 47.7 %collective-permute-start.13 = (bf16[10,128,256]{2,1,0:T(8,128)(2,1)S(1)}, bf16[10,128,256]{2,1,0:T(8,128)(2,1)S(1)}, u32[]{:S(2)}, u32[]{:S(2)}) collective-permute-start(bf16[10,128,256]{2,1,0:T(8,128)(2,1)S(1)} %get-tuple-element.33), channel_id=1, source_target_pairs={{0,64},{64,0},{1,65},{65,1},{2,66},{66,2},{3,67},{67,3},{4,68},{68... | collective-permute-start | bytes 1966088 | tf_op jit(solution)/shard_map/ppermute | solution.py:469
  163.4 46.0 %collective-permute-start.14 = (bf16[10,128,256]{2,1,0:T(8,128)(2,1)S(1)}, bf16[10,128,256]{2,1,0:T(8,128)(2,1)S(1)}, u32[]{:S(2)}, u32[]{:S(2)}) collective-permute-start(bf16[10,128,256]{2,1,0:T(8,128)(2,1)S(1)} %get-tuple-element.34), channel_id=1, source_target_pairs={{0,64},{64,0},{1,65},{65,1},{2,66},{66,2},{3,67},{67,3},{4,68},{68... | collective-permute-start | bytes 1966088 | tf_op jit(solution)/shard_map/ppermute | solution.py:469
  164.6 43.4 %collective-permute-start.15 = (bf16[10,128,256]{2,1,0:T(8,128)(2,1)S(1)}, bf16[10,128,256]{2,1,0:T(8,128)(2,1)S(1)}, u32[]{:S(2)}, u32[]{:S(2)}) collective-permute-start(bf16[10,128,256]{2,1,0:T(8,128)(2,1)S(1)} %get-tuple-element.35), channel_id=1, source_target_pairs={{0,64},{64,0},{1,65},{65,1},{2,66},{66,2},{3,67},{67,3},{4,68},{68... | collective-permute-start | bytes 1966088 | tf_op jit(solution)/shard_map/ppermute | solution.py:469
  174.0 46.7 %collective-permute-start.12 = (bf16[10,128,256]{2,1,0:T(8,128)(2,1)S(1)}, bf16[10,128,256]{2,1,0:T(8,128)(2,1)S(1)}, u32[]{:S(2)}, u32[]{:S(2)}) collective-permute-start(bf16[10,128,256]{2,1,0:T(8,128)(2,1)S(1)} %get-tuple-element.32), channel_id=1, source_target_pairs={{0,64},{64,0},{1,65},{65,1},{2,66},{66,2},{3,67},{67,3},{4,68},{68... | collective-permute-start | bytes 1966088 | tf_op jit(solution)/shard_map/ppermute | solution.py:469

commit v2 on v1

v2 whole, which is shorter than its diff:
```python
import functools

import jax
import jax.numpy as jnp
from jax import lax
from jax.experimental import pallas as pl
from jax.experimental.pallas import tpu as pltpu
from jax.sharding import PartitionSpec as P


NSTEPS = 3
ROWS = 16
AHEAD = 3
STAGES = 4
PIECES = (1, 1, 2, 2, 1, 1)
SUMS = (2, 6)


def side_pairs(tiles, mems, step):
    pairs = []
    for mem in range(mems):
        for tile in range(tiles):
            source = tile + step
            if 0 <= source < tiles:
                crossed = (min(tile, source) % 2) == 1
                source_mem = mems - 1 - mem if crossed else mem
                pairs.append((source_mem * tiles + source, mem * tiles + tile))
    return pairs


def pick_body(source, picked, stage, sems, *, partner):
    size = picked.shape[1]
    mem = lax.axis_index("mem")
    start = pl.multiple_of((1 - mem if partner else mem) * size, size)
    rows = picked.shape[0] // STAGES
    inward, outward = [], []
    for k in range(STAGES):
        at = pl.ds(k * rows, rows)
        inward.append(
            pltpu.make_async_copy(
                source.at[at, pl.ds(start, size)], stage.at[at, :], sems.at[0, k]
            )
        )
        outward.append(pltpu.make_async_copy(stage.at[at, :], picked.at[at, :], sems.at[1, k]))
        inward[k].start()
    for k in range(STAGES):
        inward[k].wait()
        outward[k].start()
    for k in range(STAGES):
        outward[k].wait()


def pick_half(source, partner):
    rows, cols = source.shape
    return pl.pallas_call(
        functools.partial(pick_body, partner=partner),
        in_specs=[pl.BlockSpec(memory_space=pl.ANY)],
        out_specs=pl.BlockSpec(memory_space=pl.ANY),
        scratch_shapes=[
            pltpu.VMEM((rows, cols // 2), source.dtype),
            pltpu.SemaphoreType.DMA((2, STAGES)),
        ],
        out_shape=jax.ShapeDtypeStruct((rows, cols // 2), source.dtype),
        cost_estimate=pl.CostEstimate(
            flops=0, bytes_accessed=2 * source.size, transcendentals=0
        ),
        compiler_params=pltpu.CompilerParams(vmem_limit_bytes=4 << 20),
        name="pick_partner" if partner else "pick_own",
    )(pltpu.with_memory_space_constraint(source, pltpu.HBM))


def locate(lists, meta, row, n, blocks_dev):
    mem, tile = meta[0], meta[1]
    parity = lax.rem(tile, 2)
    local = lists[n, row] - (tile - 1) * blocks_dev
    which = lax.div(local, blocks_dev)
    inside = local - which * blocks_dev
    crossed = ((which == 0) & (parity == 0)) | ((which == 2) & (parity == 1))
    source = jnp.where(crossed, 1 - mem, mem)
    part = lax.div(inside, blocks_dev // 2)
    return which, inside, source, part == source, inside - part * (blocks_dev // 2)


def split(value):
    high = value.astype(jnp.bfloat16)
    return high, (value - high.astype(jnp.float32)).astype(jnp.bfloat16)


def dot(left, right):
    return lax.dot_general(
        left, right, (((1,), (0,)), ((), ())), preferred_element_type=jnp.float32
    )


def dot3(left, right):
    lh, ll = left
    rh, rl = right
    return dot(lh, rh) + (dot(lh, rl) + dot(ll, rh))


def parts3(value):
    high = value.astype(jnp.bfloat16)
    mid, low = split(value - high.astype(jnp.float32))
    return [high, mid, low]


def fetch(lists, meta, owner, block, tiles, raw, sems, blocks_dev, width):
    nloc, count = lists.shape
    rows = tiles[0].shape[0]
    for n in range(nloc):
        which, _, source, here, index = locate(
            lists, meta, owner * (count // 2) + block, n, blocks_dev
        )
        start = pl.multiple_of(index * width, width)
        at = pl.ds(n * width, width)
        first = pl.multiple_of(jnp.where(source == owner, 0, rows), rows)
        second = pl.multiple_of(jnp.where(source == owner, rows, 0), rows)
        for k in range(3):

            @pl.when(here & (which == k))
            def _(k=k, at=at, start=start, first=first, second=second):
                for part, place in ((tiles[2 * k], first), (tiles[2 * k + 1], second)):
                    pltpu.make_async_copy(
                        part.at[:, pl.ds(start, width)],
                        raw.at[block, pl.ds(place, rows), at],
                        sems.at[block],
                    ).start()


def local_gram(
    lists, meta, owner, block, raw, sems, low, own, high, ybuf, sbuf, blocks_dev, width
):
    nloc, count = lists.shape
    members = raw.shape[1]
    row = owner * (count // 2) + block
    found = [locate(lists, meta, row, n, blocks_dev) for n in range(nloc)]
    for n in range(nloc):

        @pl.when(found[n][3])
        def _():
            whole = raw.at[block, :, pl.ds(0, width)]
            pltpu.make_async_copy(whole, whole, sems.at[block]).wait()

    for n in range(nloc):
        which, inside, _, here, _ = found[n]
        at = pl.ds(n * width, width)

        @pl.when(jnp.logical_not(here))
        def _(at=at):
            ybuf[:, at] = jnp.zeros((members + ROWS, width), jnp.bfloat16)
            sbuf[:, at] = jnp.zeros((members, width), jnp.bfloat16)

        @pl.when(here)
        def _(at=at, which=which, inside=inside):
            values = raw[block, :, at].astype(jnp.float32)
            mean = jnp.sum(values, axis=0, keepdims=True) / members

            def entry(index):
                at_low = low[pl.ds(index, 1), :]
                at_own = own[pl.ds(index, 1), :]
                at_high = high[pl.ds(index, 1), :]
                return jnp.where(which == 0, at_low, jnp.where(which == 1, at_own, at_high))

            value = entry(inside)
            weight = entry(inside + blocks_dev)
            ybuf[pl.ds(members, ROWS), at] = jnp.concatenate(
                [*parts3(value - mean), jnp.zeros((ROWS - 3, width), jnp.bfloat16)], axis=0
            )
            pert = (values - mean).astype(jnp.bfloat16)
            ybuf[pl.ds(0, members), at] = pert
            sbuf[:, at] = (pert.astype(jnp.float32) * weight).astype(jnp.bfloat16)

    gram = lax.dot_general(
        ybuf[...], sbuf[...], (((1,), (1,)), ((), ())), preferred_element_type=jnp.float32
    )
    return gram[:members], jnp.sum(gram[members:], axis=0, keepdims=True)


def on_diagonal(size):
    return lax.broadcasted_iota(jnp.int32, (size, size), 0) == lax.broadcasted_iota(
        jnp.int32, (size, size), 1
    )


def sums_body(lists, meta, *refs, for_self, blocks_dev, width):
    tiles, (low, own, high) = refs[:6], refs[6:9]
    outs = refs[9:-4]
    raw, sems, ybuf, sbuf = refs[-4:]
    owner = meta[0] if for_self else 1 - meta[0]
    block = pl.program_id(0)
    blocks = raw.shape[0]

    @pl.when(block == 0)
    def _():
        for early in range(AHEAD):
            fetch(lists, meta, owner, early, tiles, raw, sems, blocks_dev, width)

    @pl.when(block + AHEAD < blocks)
    def _():
        fetch(lists, meta, owner, block + AHEAD, tiles, raw, sems, blocks_dev, width)

    matrix, rhs = local_gram(
        lists, meta, owner, block, raw, sems, low, own, high, ybuf, sbuf, blocks_dev, width
    )
    members = matrix.shape[0]
    if for_self:
        outs[0][0] = matrix
        outs[1][0] = jnp.broadcast_to(rhs, outs[1].shape[1:])
        return
    groups = members // ROWS
    diagonal = jnp.sum(jnp.where(on_diagonal(members), matrix, 0.0), axis=0, keepdims=True)
    lane = lax.broadcasted_iota(jnp.int32, (ROWS, members), 1)
    packed = [matrix[:ROWS]]
    for group in range(1, groups // 2):
        filled = pltpu.roll(matrix[members - group * ROWS :][:ROWS], group * ROWS, 1)
        packed.append(
            jnp.where(lane < group * ROWS, filled, matrix[group * ROWS : (group + 1) * ROWS])
        )
    middle = matrix[members // 2 : members // 2 + ROWS, members // 2 :]
    last = [jnp.concatenate([middle[ROWS // 2 :], middle[: ROWS // 2]], axis=1)]
    last += [part.astype(jnp.float32) for part in parts3(rhs) + parts3(diagonal)]
    last.append(jnp.zeros((ROWS // 2 - 6, members), jnp.float32))
    packed.append(jnp.concatenate(last, axis=0))
    first = 0
    for out, size in zip(outs, SUMS):

        @pl.when((block >= first) & (block < first + size))
        def _(out=out):
            for group, rows in enumerate(packed):
                out[0, pl.ds(group * ROWS, ROWS), :] = rows.astype(jnp.bfloat16)

        first += size


def partial_sums(lists, meta, tiles, tables, for_self, blocks_dev, width):
    nloc, count = lists.shape
    half = count // 2
    members = 2 * tiles[0].shape[0]
    span = nloc * width
    table_spec = pl.BlockSpec(tables[0].shape, lambda i, *_: (0, 0))
    if for_self:
        shapes = [(half, members, members), (half, 8, members)]
        kind = jnp.float32
        out_specs = [pl.BlockSpec((1, *shape[1:]), lambda i, *_: (i, 0, 0)) for shape in shapes]
    else:
        shapes = [(size, members // 2 + ROWS, members) for size in SUMS]
        kind = jnp.bfloat16
        out_specs = [
            pl.BlockSpec(
                (1, *shape[1:]),
                lambda i, *_, first=sum(SUMS[:k]), size=SUMS[k]: (
                    jnp.clip(i - first, 0, size - 1), 0, 0,
                ),
            )
            for k, shape in enumerate(shapes)
        ]
    return pl.pallas_call(
        functools.partial(sums_body, for_self=for_self, blocks_dev=blocks_dev, width=width),
        grid_spec=pltpu.PrefetchScalarGridSpec(
            num_scalar_prefetch=2,
            grid=(half,),
            in_specs=[pl.BlockSpec(memory_space=pl.ANY)] * 6 + [table_spec] * 3,
            out_specs=out_specs,
            scratch_shapes=[
                pltpu.VMEM((half, members, span), jnp.bfloat16),
                pltpu.SemaphoreType.DMA((half,)),
                pltpu.VMEM((members + ROWS, span), jnp.bfloat16),
                pltpu.VMEM((members, span), jnp.bfloat16),
            ],
        ),
        out_shape=[jax.ShapeDtypeStruct(shape, kind) for shape in shapes],
        cost_estimate=pl.CostEstimate(
            flops=2 * half * members * members * span,
            bytes_accessed=2 * members * half * span,
            transcendentals=0,
        ),
        compiler_params=pltpu.CompilerParams(vmem_limit_bytes=20 << 20),
        name="sums_self" if for_self else "sums_send",
    )(lists, meta, *tiles, *tables)


def analysis_body(meta, mine, theirs, ours, our_rhs, received, *refs, width):
    kept, sent, ubuf, xbuf, mbuf = refs[-5:]
    rows = mine.shape[1]
    members = 2 * rows

    matrix = ours[0]
    rhs = our_rhs[0, pl.ds(0, 1), :]
    groups = members // ROWS
    ubuf[pl.ds(0, ROWS), :] = received[0, pl.ds(0, ROWS), :].astype(jnp.float32)
    for group in range(1, groups // 2):
        piece = received[0, pl.ds(group * ROWS, ROWS), :].astype(jnp.float32)
        ubuf[pl.ds(group * ROWS, ROWS), :] = piece
        ubuf[pl.ds(members - group * ROWS, ROWS), :] = pltpu.roll(
            piece, members - group * ROWS, 1
        )
    last = received[0, pl.ds(members // 2, ROWS), :].astype(jnp.float32)
    step = ROWS // 2
    ubuf[pl.ds(members // 2, step), pl.ds(rows, rows)] = last[:step, rows:]
    ubuf[pl.ds(members // 2 + step, step), pl.ds(rows, rows)] = last[:step, :rows]
    rhs = rhs + jnp.sum(last[step : step + 3], axis=0, keepdims=True)
    upper = ubuf[...]
    block_row = lax.div(lax.broadcasted_iota(jnp.int32, (members, members), 0), ROWS)
    block_col = lax.div(lax.broadcasted_iota(jnp.int32, (members, members), 1), ROWS)
    other = jnp.where(block_row <= block_col, upper, upper.T)
    diagonal = on_diagonal(members)
    other = jnp.where(diagonal, jnp.sum(last[step + 3 : step + 6], axis=0, keepdims=True), other)
    matrix = matrix + other
    matrix = matrix + jnp.where(diagonal, members - 1.0, 0.0)
    trace = jnp.sum(
        jnp.sum(jnp.where(diagonal, matrix, 0.0), axis=0, keepdims=True), axis=1, keepdims=True
    )
    scale = trace / members
    iterate = matrix / scale
    eye15 = jnp.where(diagonal, 1.5, 0.0)
    inverse_root = eye15 - 0.5 * iterate
    factor = split(inverse_root)
    iterate = dot3(factor, split(iterate))
    for step in range(1, NSTEPS):
        root_parts = split(inverse_root)
        iterate_parts = split(iterate)
        factor = split(eye15 - 0.5 * dot3(iterate_parts, root_parts))
        if step + 1 < NSTEPS:
            iterate = dot3(factor, iterate_parts)
        inverse_root = dot3(root_parts, factor)
    root_parts = split(inverse_root)
    shift = jnp.broadcast_to(rhs, (ROWS, members))
    shift = dot3(split(shift), root_parts)
    shift = dot3(split(shift), root_parts)[:1] / scale
    trans = (jnp.sqrt((members - 1.0) / scale) * inverse_root + shift).astype(jnp.bfloat16)

    layers = mine.shape[0]
    for layer in range(layers):
        at = pl.ds(layer * width, width)
        first = mine[layer].astype(jnp.float32)
        second = theirs[layer].astype(jnp.float32)
        mean = (
            jnp.sum(first, axis=0, keepdims=True) + jnp.sum(second, axis=0, keepdims=True)
        ) / members
        mbuf[:, at] = mean
        xbuf[pl.ds(0, rows), at] = (first - mean).astype(jnp.bfloat16)
        xbuf[pl.ds(rows, rows), at] = (second - mean).astype(jnp.bfloat16)
    result = (dot(trans, xbuf[...]) + mbuf[...]).astype(jnp.bfloat16)
    for layer in range(layers):
        at = slice(layer * width, (layer + 1) * width)
        kept[layer] = result[:rows, at]
        sent[layer] = result[rows:, at]


def analyse(meta, mine, theirs, ours, our_rhs, received, output, first, size, skipped, width):
    layers, rows, cols = mine.shape
    members = 2 * rows
    half = cols // 2 // width
    flops = 2 * size * members * members * (18 * members + layers * width)

    def mine_at(i, meta):
        return (0, 0, meta[0] * half + first + i)

    tile_block = (layers, rows, width)
    in_specs = [
        pl.BlockSpec(tile_block, mine_at),
        pl.BlockSpec(tile_block, lambda i, *_: (0, 0, first + i)),
        pl.BlockSpec((1, *ours.shape[1:]), lambda i, *_: (first + i, 0, 0)),
        pl.BlockSpec((1, *our_rhs.shape[1:]), lambda i, *_: (first + i, 0, 0)),
        pl.BlockSpec((1, *received.shape[1:]), lambda i, *_: (first - skipped + i, 0, 0)),
    ]
    operands = [mine, theirs, ours, our_rhs, received]
    aliases = {}
    if output is not None:
        in_specs.append(pl.BlockSpec(memory_space=pl.ANY))
        aliases = {1 + len(operands): 0}
        operands.append(output)
    return pl.pallas_call(
        functools.partial(analysis_body, width=width),
        grid_spec=pltpu.PrefetchScalarGridSpec(
            num_scalar_prefetch=1,
            grid=(size,),
            in_specs=in_specs,
            out_specs=[
                pl.BlockSpec(tile_block, mine_at),
                pl.BlockSpec(tile_block, lambda i, *_: (0, 0, i)),
            ],
            scratch_shapes=[
                pltpu.VMEM((members, members), jnp.float32),
                pltpu.VMEM((members, layers * width), jnp.bfloat16),
                pltpu.VMEM((1, layers * width), jnp.float32),
            ],
        ),
        out_shape=[
            jax.ShapeDtypeStruct(mine.shape, jnp.bfloat16),
            jax.ShapeDtypeStruct((layers, rows, size * width), jnp.bfloat16),
        ],
        input_output_aliases=aliases,
        cost_estimate=pl.CostEstimate(
            flops=flops, bytes_accessed=size * 8 * rows * layers * width, transcendentals=0
        ),
        compiler_params=pltpu.CompilerParams(vmem_limit_bytes=20 << 20),
        name="analyse",
    )(meta, *operands)


def place_body(meta, piece, output, placed, sem, *, first, width):
    start = pl.multiple_of((1 - meta[0]) * (placed.shape[2] // 2) + first * width, width)
    copy = pltpu.make_async_copy(piece, placed.at[:, :, pl.ds(start, piece.shape[2])], sem)
    copy.start()
    copy.wait()


def place(meta, piece, output, first, width):
    return pl.pallas_call(
        functools.partial(place_body, first=first, width=width),
        grid_spec=pltpu.PrefetchScalarGridSpec(
            num_scalar_prefetch=1,
            grid=(1,),
            in_specs=[pl.BlockSpec(memory_space=pl.ANY)] * 2,
            out_specs=pl.BlockSpec(memory_space=pl.ANY),
            scratch_shapes=[pltpu.SemaphoreType.DMA],
        ),
        out_shape=jax.ShapeDtypeStruct(output.shape, output.dtype),
        input_output_aliases={2: 0},
        cost_estimate=pl.CostEstimate(
            flops=0, bytes_accessed=4 * piece.size, transcendentals=0
        ),
        compiler_params=pltpu.CompilerParams(vmem_limit_bytes=2 << 20),
        name="place",
    )(meta, piece, output)


def per_device(
    prior_members,
    members_in_reading_space,
    measured_values,
    obs_precision_weights,
    valid_reading_numbers,
    neighbour_lists,
):
    tile_no = lax.axis_index("tile")
    member_no = lax.axis_index("mem")
    tiles = lax.axis_size("tile")
    mems = lax.axis_size("mem")
    both = ("mem", "tile")
    swap = [(0, 1), (1, 0)]
    from_low = side_pairs(tiles, mems, -1)
    from_high = side_pairs(tiles, mems, 1)
    blocks_dev = valid_reading_numbers.shape[0]
    width = members_in_reading_space.shape[1] // blocks_dev
    cols = prior_members.shape[2]

    mine = jnp.transpose(prior_members, (1, 0, 2))
    lists = neighbour_lists.T
    meta = jnp.stack([member_no, tile_no]).astype(jnp.int32)

    obs = members_in_reading_space
    swapped = lax.ppermute(pick_half(obs, True), "mem", swap)
    own_set = pick_half(obs, False)
    low_own = lax.ppermute(own_set, both, from_low)
    high_own = lax.ppermute(own_set, both, from_high)
    half = cols // 2
    outgoing = lax.dynamic_slice_in_dim(mine, (1 - member_no) * half, half, 2)
    theirs = lax.ppermute(outgoing, "mem", swap)
    low_other = lax.ppermute(swapped, both, from_low)
    high_other = lax.ppermute(swapped, both, from_high)
    tiles_held = (low_own, low_other, own_set, swapped, high_own, high_other)
    slots = jnp.arange(width, dtype=jnp.int32)
    valid = slots[None, :] < valid_reading_numbers[:, None]
    weight = jnp.where(valid, obs_precision_weights.reshape(blocks_dev, width), 0.0)
    table = jnp.concatenate([measured_values.reshape(blocks_dev, width), weight], axis=0)
    table_low = lax.ppermute(table, both, from_low)
    table_high = lax.ppermute(table, both, from_high)
    tables = (table_low, table, table_high)

    sums = partial_sums(lists, meta, tiles_held, tables, False, blocks_dev, width)
    received = []
    for piece in sums:
        received.append(lax.ppermute(piece, "mem", swap))
    ours, our_rhs = partial_sums(lists, meta, tiles_held, tables, True, blocks_dev, width)
    output = None
    arrived = []
    for k, size in enumerate(PIECES):
        first = sum(PIECES[:k])
        late = first >= SUMS[0]
        output, sent = analyse(
            meta, mine, theirs, ours, our_rhs, received[late], output, first, size,
            SUMS[0] if late else 0, width,
        )
        arrived.append(lax.ppermute(sent, "mem", swap))
    for k, piece in enumerate(arrived):
        output = place(meta, piece, output, sum(PIECES[:k]), width)
    return jnp.transpose(output, (1, 0, 2))


def solution(mesh):
    in_specs = (
        P("mem", None, "tile"),
        P("mem", "tile"),
        P("tile"),
        P("tile"),
        P("tile"),
        P("tile", None),
    )
    out_specs = P("mem", None, "tile")

    return jax.shard_map(
        per_device, mesh=mesh, in_specs=in_specs, out_specs=out_specs, check_vma=False
    )
```

time: 223 us -> 218 us (0.978)
  the two profiles are of different devices: /device:TPU:25 before, /device:TPU:9 now
where the time goes in v2:
time: 218 us; the launch traced here: 217 us
  waiting for transfers between devices  117 us (54%)
  Pallas kernels  66.3 us (30%)
  starting transfers between devices  30.2 us (14%)
  local copies, waits for them, and re-layouts  3.53 us (2%)
    ppermute x1, waiting for transfers between devices, per_device(): swapped = lax.ppermute(pick_half(obs, True), 'mem', swap)  60.9 us
    pallas_call x6, Pallas kernels, analyse(): pl.pallas_call(functools.partial(analysis_body, width=width), grid_spec=p...  34.8 us
    ppermute x6, waiting for transfers between devices, per_device(): arrived.append(lax.ppermute(sent, 'mem', swap))  31.6 us
    ppermute x1, waiting for transfers between devices, per_device(): high_other = lax.ppermute(swapped, both, from_high)  21.8 us
    pallas_call x2, Pallas kernels, partial_sums(): pl.pallas_call(functools.partial(sums_body, for_self=for_self, blocks_dev...  20.9 us
    pallas_call x6, Pallas kernels, place(): pl.pallas_call(functools.partial(place_body, first=first, width=width), g...  7.89 us
    ppermute x1, starting transfers between devices, per_device(): table_low = lax.ppermute(table, both, from_low)  5.56 us
    ppermute x1, starting transfers between devices, per_device(): low_other = lax.ppermute(swapped, both, from_low)  5.39 us
  transfers between devices with their start and end apart: 16, of which 7 were waited for; matrix products, arithmetic and copies ran while one was open for 0% of the time, Pallas kernels for 26%

profile of v2, /device:TPU:9, one launch (start us, length us, event | category | flops | bytes accessed | tf_op | source)
XLA Modules:
  0.0 217.1 jit_solution(425435632308297119)
XLA Ops:
  0.0 0.0 copy-start.3
  0.0 0.0 copy-start.1
  0.0 0.0 copy-start.2
  0.0 0.0 copy-start
  0.0 3.5 %dynamic-slice_bitcast_fusion = bf16[10,128,1024]{2,1,0:T(8,128)(2,1)} fusion(bf16[128,10,2048]{2,0,1:T(8,128)(2,1)} %param.6, s32[]{:T(128)S(6)} %select_n.7), kind=kLoop, calls=%fused_computation | loop fusion | bytes 5242884 | tf_op jit(solution)/shard_map/dynamic_slice | solution.py:459
  3.5 1.6 collective-permute-start
  5.2 1.3 pick_partner.1
  6.5 0.1 collective-permute-start.2
  6.6 0.0 copy-done.3
  6.6 0.0 copy-done.1
  6.6 0.1 bitcast_select_fusion
  6.6 0.0 copy-done.2
  6.7 2.9 %collective-permute-start.7 = (f32[128,128]{1,0:T(8,128)S(1)}, f32[128,128]{1,0:T(8,128)S(1)}, u32[]{:S(2)}, u32[]{:S(2)}) collective-permute-start(f32[128,128]{1,0:T(8,128)S(1)} %pad_maximum_fusion.refs_7_), channel_id=1, source_target_pairs={{1,0},{66,1},{3,2},{68,3},{5,4},{70,5},{7,6},{72,7},{9,8},{74,9},{... | collective-permute-start | bytes 196616 | tf_op jit(solution)/shard_map/ppermute | solution.py:469
  9.6 5.6 %collective-permute-start.6 = (f32[128,128]{1,0:T(8,128)S(1)}, f32[128,128]{1,0:T(8,128)S(1)}, u32[]{:S(2)}, u32[]{:S(2)}) collective-permute-start(f32[128,128]{1,0:T(8,128)S(1)} %pad_maximum_fusion.refs_7_), channel_id=1, source_target_pairs={{0,1},{65,2},{2,3},{67,4},{4,5},{69,6},{6,7},{71,8},{8,9},{73,10},... | collective-permute-start | bytes 196616 | tf_op jit(solution)/shard_map/ppermute | solution.py:468
  15.2 0.0 slice-start
  15.2 1.4 pick_own.1.refs_2_
  16.6 3.3 %collective-permute-start.4 = (bf16[128,4096]{1,0:T(8,128)(2,1)S(1)}, bf16[128,4096]{1,0:T(8,128)(2,1)}, u32[]{:S(2)}, u32[]{:S(2)}) collective-permute-start(bf16[128,4096]{1,0:T(8,128)(2,1)S(1)} %pick_own.1.refs_2_), channel_id=1, source_target_pairs={{1,0},{66,1},{3,2},{68,3},{5,4},{70,5},{7,6},{72,7},{9,8},{74,9},{... | collective-permute-start | bytes 3145736 | tf_op jit(solution)/shard_map/ppermute | solution.py:457
  19.9 0.0 collective-permute-done.7.refs_8_
  19.9 3.5 %collective-permute-start.1 = (bf16[128,4096]{1,0:T(8,128)(2,1)S(1)}, bf16[128,4096]{1,0:T(8,128)(2,1)}, u32[]{:S(2)}, u32[]{:S(2)}) collective-permute-start(bf16[128,4096]{1,0:T(8,128)(2,1)S(1)} %pick_own.1.refs_2_), channel_id=1, source_target_pairs={{0,1},{65,2},{2,3},{67,4},{4,5},{69,6},{6,7},{71,8},{8,9},{73,10},... | collective-permute-start | bytes 3145736 | tf_op jit(solution)/shard_map/ppermute | solution.py:456
  23.4 60.9 %collective-permute-done.2.refs_3_ = bf16[128,4096]{1,0:T(8,128)(2,1)S(1)} collective-permute-done((bf16[128,4096]{1,0:T(8,128)(2,1)S(1)}, bf16[128,4096]{1,0:T(8,128)(2,1)S(1)}, u32[]{:S(2)}, u32[]{:S(2)}) %collective-permute-start.2) | collective-permute-done | bytes 1048608 | tf_op jit(solution)/shard_map/ppermute | solution.py:454
  84.3 3.3 %collective-permute-start.5 = (bf16[128,4096]{1,0:T(8,128)(2,1)S(1)}, bf16[128,4096]{1,0:T(8,128)(2,1)}, u32[]{:S(2)}, u32[]{:S(2)}) collective-permute-start(bf16[128,4096]{1,0:T(8,128)(2,1)S(1)} %collective-permute-done.2.refs_3_), channel_id=1, source_target_pairs={{1,0},{66,1},{3,2},{68,3},{5,4},{70,5},{7,6},{72,7},{9,8},{74,9},{... | collective-permute-start | bytes 3145736 | tf_op jit(solution)/shard_map/ppermute | solution.py:462
  87.6 0.0 collective-permute-done.6.refs_6_
  87.6 5.4 %collective-permute-start.3 = (bf16[128,4096]{1,0:T(8,128)(2,1)S(1)}, bf16[128,4096]{1,0:T(8,128)(2,1)}, u32[]{:S(2)}, u32[]{:S(2)}) collective-permute-start(bf16[128,4096]{1,0:T(8,128)(2,1)S(1)} %collective-permute-done.2.refs_3_), channel_id=1, source_target_pairs={{0,1},{65,2},{2,3},{67,4},{4,5},{69,6},{6,7},{71,8},{8,9},{73,10},... | collective-permute-start | bytes 3145736 | tf_op jit(solution)/shard_map/ppermute | solution.py:461
  93.0 0.1 pad_add_fusion.meta
  93.1 0.0 collective-permute-done.4.refs_4_
  93.1 0.0 collective-permute-done.1.refs_0_
  93.1 21.8 %collective-permute-done.5.refs_5_ = bf16[128,4096]{1,0:T(8,128)(2,1)} collective-permute-done((bf16[128,4096]{1,0:T(8,128)(2,1)S(1)}, bf16[128,4096]{1,0:T(8,128)(2,1)}, u32[]{:S(2)}, u32[]{:S(2)}) %collective-permute-start.5) | collective-permute-done | bytes 1048608 | tf_op jit(solution)/shard_map/ppermute | solution.py:462
  114.9 0.0 collective-permute-done.3.refs_1_
  114.9 0.0 copy-done
  114.9 0.0 slice-start.1
  114.9 10.8 %sums_send.1 = (bf16[2,144,256]{2,1,0:T(8,128)(2,1)S(1)}, bf16[6,144,256]{2,1,0:T(8,128)(2,1)S(1)}) custom-call(s32[8,16]{1,0:T(8,128)S(1)} %bitcast.18, s32[2]{0:T(128)S(1)} %pad_add_fusion.meta, bf16[128,4096]{1,0:T(8,128)(2,1)} %collective-permute-done.1.refs_0_, bf16[128,4096]{1,0:T(8,128)(2,1)} %collective-permute-done.3.refs_1_, ...), custom_call_target="tpu_custom_call" | custom-call | flops 1073741824 | bytes 4194304 | tf_op jit(solution)/shard_map/sums_send/pallas_call | solution.py:257
  125.7 0.1 collective-permute-start.8
  125.8 1.5 collective-permute-start.9
  127.2 10.0 %sums_self.1 = (f32[8,256,256]{2,1,0:T(8,128)S(1)}, f32[8,8,256]{2,1,0:T(8,128)S(1)}) custom-call(s32[8,16]{1,0:T(8,128)S(1)} %bitcast.19, s32[2]{0:T(128)S(1)} %pad_add_fusion.meta, bf16[128,4096]{1,0:T(8,128)(2,1)} %collective-permute-done.1.refs_0_, bf16[128,4096]{1,0:T(8,128)(2,1)} %collective-permute-done.3.refs_1_, ...), custom_call_target="tpu_custom_call" | custom-call | flops 1073741824 | bytes 4194304 | tf_op jit(solution)/shard_map/sums_self/pallas_call | solution.py:257
  137.3 2.3 %collective-permute-done.9.received = bf16[2,144,256]{2,1,0:T(8,128)(2,1)S(1)} collective-permute-done((bf16[2,144,256]{2,1,0:T(8,128)(2,1)S(1)}, bf16[2,144,256]{2,1,0:T(8,128)(2,1)S(1)}, u32[]{:S(2)}, u32[]{:S(2)}) %collective-permute-start.9) | collective-permute-done | bytes 147488 | tf_op jit(solution)/shard_map/ppermute | solution.py:475
  139.6 0.0 collective-permute-done.theirs
  139.6 0.0 slice-done
  139.6 0.0 slice-done.1
  139.6 4.9 %analyse.6 = (bf16[10,128,2048]{2,1,0:T(8,128)(2,1)}, bf16[10,128,128]{2,1,0:T(8,128)(2,1)S(1)}) custom-call(s32[2]{0:T(128)S(1)} %pad_add_fusion.meta, bf16[10,128,2048]{2,1,0:T(8,128)(2,1)S(1)} %bitcast.12, bf16[10,128,1024]{2,1,0:T(8,128)(2,1)} %collective-permute-done.theirs, f32[8,256,256]{2,1,0:T(8,128)S(1)} %get-tuple-element.21.ours, ...), custom_call_target="tpu_custom_call" | custom-call | flops 771751936 | bytes 1310720 | tf_op jit(solution)/shard_map/analyse/pallas_call | solution.py:373
  144.5 4.9 %analyse.7 = (bf16[10,128,2048]{2,1,0:T(8,128)(2,1)}, bf16[10,128,128]{2,1,0:T(8,128)(2,1)S(1)}) custom-call(s32[2]{0:T(128)S(1)} %pad_add_fusion.meta, bf16[10,128,2048]{2,1,0:T(8,128)(2,1)S(1)} %bitcast.13, bf16[10,128,1024]{2,1,0:T(8,128)(2,1)} %collective-permute-done.theirs, ...), custom_call_target="tpu_custom_call", output_to_operand_aliasing={{0}: (6, {})} | custom-call | flops 771751936 | bytes 1310720 | tf_op jit(solution)/shard_map/analyse/pallas_call | solution.py:373
  149.3 0.0 collective-permute-done.8.received
  149.3 7.7 %analyse.8 = (bf16[10,128,2048]{2,1,0:T(8,128)(2,1)}, bf16[10,128,256]{2,1,0:T(8,128)(2,1)S(1)}) custom-call(s32[2]{0:T(128)S(1)} %pad_add_fusion.meta, bf16[10,128,2048]{2,1,0:T(8,128)(2,1)S(1)} %bitcast.14, bf16[10,128,1024]{2,1,0:T(8,128)(2,1)} %collective-permute-done.theirs, ...), custom_call_target="tpu_custom_call", output_to_operand_aliasing={{0}: (6, {})} | custom-call | flops 1543503872 | bytes 2621440 | tf_op jit(solution)/shard_map/analyse/pallas_call | solution.py:373
  157.0 0.0 collective-permute-start.13
  157.0 7.7 %analyse.9 = (bf16[10,128,2048]{2,1,0:T(8,128)(2,1)}, bf16[10,128,256]{2,1,0:T(8,128)(2,1)S(1)}) custom-call(s32[2]{0:T(128)S(1)} %pad_add_fusion.meta, bf16[10,128,2048]{2,1,0:T(8,128)(2,1)S(1)} %bitcast.15, bf16[10,128,1024]{2,1,0:T(8,128)(2,1)} %collective-permute-done.theirs, ...), custom_call_target="tpu_custom_call", output_to_operand_aliasing={{0}: (6, {})} | custom-call | flops 1543503872 | bytes 2621440 | tf_op jit(solution)/shard_map/analyse/pallas_call | solution.py:373
  164.7 1.5 collective-permute-start.12
  166.2 0.0 collective-permute-start.15
  166.2 1.4 collective-permute-start.14
  167.7 4.9 %analyse.10 = (bf16[10,128,2048]{2,1,0:T(8,128)(2,1)}, bf16[10,128,128]{2,1,0:T(8,128)(2,1)S(1)}) custom-call(s32[2]{0:T(128)S(1)} %pad_add_fusion.meta, bf16[10,128,2048]{2,1,0:T(8,128)(2,1)S(1)} %bitcast.16, bf16[10,128,1024]{2,1,0:T(8,128)(2,1)} %collective-permute-done.theirs, ...), custom_call_target="tpu_custom_call", output_to_operand_aliasing={{0}: (6, {})} | custom-call | flops 771751936 | bytes 1310720 | tf_op jit(solution)/shard_map/analyse/pallas_call | solution.py:373
  172.5 0.0 collective-permute-start.11
  172.5 4.9 %analyse.11 = (bf16[10,128,2048]{2,1,0:T(8,128)(2,1)}, bf16[10,128,128]{2,1,0:T(8,128)(2,1)S(1)}) custom-call(s32[2]{0:T(128)S(1)} %pad_add_fusion.meta, bf16[10,128,2048]{2,1,0:T(8,128)(2,1)S(1)} %bitcast.17, bf16[10,128,1024]{2,1,0:T(8,128)(2,1)} %collective-permute-done.theirs, ...), custom_call_target="tpu_custom_call", output_to_operand_aliasing={{0}: (6, {})} | custom-call | flops 771751936 | bytes 1310720 | tf_op jit(solution)/shard_map/analyse/pallas_call | solution.py:373
  177.4 17.4 %collective-permute-done.15.piece = bf16[10,128,128]{2,1,0:T(8,128)(2,1)S(1)} collective-permute-done((bf16[10,128,128]{2,1,0:T(8,128)(2,1)S(1)}, bf16[10,128,128]{2,1,0:T(8,128)(2,1)S(1)}, u32[]{:S(2)}, u32[]{:S(2)}) %collective-permute-start.15) | collective-permute-done | bytes 327712 | tf_op jit(solution)/shard_map/ppermute | solution.py:486
  194.8 0.0 collective-permute-start.10
  194.8 1.3 place.6.output
  196.1 5.7 %collective-permute-done.14.piece = bf16[10,128,128]{2,1,0:T(8,128)(2,1)S(1)} collective-permute-done((bf16[10,128,128]{2,1,0:T(8,128)(2,1)S(1)}, bf16[10,128,128]{2,1,0:T(8,128)(2,1)S(1)}, u32[]{:S(2)}, u32[]{:S(2)}) %collective-permute-start.14) | collective-permute-done | bytes 327712 | tf_op jit(solution)/shard_map/ppermute | solution.py:486
  201.9 1.3 place.7.output
  203.1 0.0 collective-permute-done.13.piece
  203.2 1.4 place.8.output
  204.6 0.0 collective-permute-done.12.piece
  204.6 1.4 place.9.output
  206.0 2.9 %collective-permute-done.11.piece = bf16[10,128,128]{2,1,0:T(8,128)(2,1)S(1)} collective-permute-done((bf16[10,128,128]{2,1,0:T(8,128)(2,1)S(1)}, bf16[10,128,128]{2,1,0:T(8,128)(2,1)S(1)}, u32[]{:S(2)}, u32[]{:S(2)}) %collective-permute-start.11) | collective-permute-done | bytes 327712 | tf_op jit(solution)/shard_map/ppermute | solution.py:486
  208.9 1.3 place.10.output
  210.2 5.5 %collective-permute-done.10.piece = bf16[10,128,128]{2,1,0:T(8,128)(2,1)S(1)} collective-permute-done((bf16[10,128,128]{2,1,0:T(8,128)(2,1)S(1)}, bf16[10,128,128]{2,1,0:T(8,128)(2,1)S(1)}, u32[]{:S(2)}, u32[]{:S(2)}) %collective-permute-start.10) | collective-permute-done | bytes 327712 | tf_op jit(solution)/shard_map/ppermute | solution.py:486
  215.7 1.3 place.11
  (2 shorter events, 0.0 us)
Async XLA Ops:
  0.0 6.6 %copy-start.3 = (s32[64]{0:T(128)S(1)}, s32[64]{0:T(128)}, u32[]{:S(2)}) copy-start(s32[64]{0:T(128)} %param.10) | copy-start | bytes 772
  0.0 6.6 %copy-start.1 = (f32[8192]{0:T(1024)S(1)}, f32[8192]{0:T(1024)}, u32[]{:S(2)}) copy-start(f32[8192]{0:T(1024)} %param.9) | copy-start | bytes 98308
  0.0 6.6 %copy-start.2 = (f32[8192]{0:T(1024)S(1)}, f32[8192]{0:T(1024)}, u32[]{:S(2)}) copy-start(f32[8192]{0:T(1024)} %param.8) | copy-start | bytes 98308
  0.0 114.8 %copy-start = (s32[16,8]{0,1:T(8,128)S(1)}, s32[16,8]{0,1:T(8,128)}, u32[]{:S(2)}) copy-start(s32[16,8]{0,1:T(8,128)} %param.11) | copy-start | bytes 1540
  3.5 136.0 %collective-permute-start = (bf16[10,128,1024]{2,1,0:T(8,128)(2,1)}, bf16[10,128,1024]{2,1,0:T(8,128)(2,1)}, u32[]{:S(2)}, u32[]{:S(2)}) collective-permute-start(bf16[10,128,1024]{2,1,0:T(8,128)(2,1)} %dynamic-slice_bitcast_fusion), channel_id=1, source_target_pairs={{0,64},{64,0},{1,65},{65,1},{2,66},{66,2},{3,67},{67,3},{4,68},{68... | collective-permute-start | bytes 7864328 | tf_op jit(solution)/shard_map/ppermute | solution.py:460
  6.5 77.9 %collective-permute-start.2 = (bf16[128,4096]{1,0:T(8,128)(2,1)S(1)}, bf16[128,4096]{1,0:T(8,128)(2,1)S(1)}, u32[]{:S(2)}, u32[]{:S(2)}) collective-permute-start(bf16[128,4096]{1,0:T(8,128)(2,1)S(1)} %pick_partner.1), channel_id=1, source_target_pairs={{0,64},{64,0},{1,65},{65,1},{2,66},{66,2},{3,67},{67,3},{4,68},{68... | collective-permute-start | bytes 3145736 | tf_op jit(solution)/shard_map/ppermute | solution.py:454
  6.7 13.2 %collective-permute-start.7 = (f32[128,128]{1,0:T(8,128)S(1)}, f32[128,128]{1,0:T(8,128)S(1)}, u32[]{:S(2)}, u32[]{:S(2)}) collective-permute-start(f32[128,128]{1,0:T(8,128)S(1)} %pad_maximum_fusion.refs_7_), channel_id=1, source_target_pairs={{1,0},{66,1},{3,2},{68,3},{5,4},{70,5},{7,6},{72,7},{9,8},{74,9},{... | collective-permute-start | bytes 196616 | tf_op jit(solution)/shard_map/ppermute | solution.py:469
  9.6 78.0 %collective-permute-start.6 = (f32[128,128]{1,0:T(8,128)S(1)}, f32[128,128]{1,0:T(8,128)S(1)}, u32[]{:S(2)}, u32[]{:S(2)}) collective-permute-start(f32[128,128]{1,0:T(8,128)S(1)} %pad_maximum_fusion.refs_7_), channel_id=1, source_target_pairs={{0,1},{65,2},{2,3},{67,4},{4,5},{69,6},{6,7},{71,8},{8,9},{73,10},... | collective-permute-start | bytes 196616 | tf_op jit(solution)/shard_map/ppermute | solution.py:468
  15.2 124.4 %slice-start = ((s8[5242880]{0:T(1024)(128)(4,1)}), s8[1048576]{0:T(1024)(128)(4,1)S(1)}, s32[]{:S(2)}) async-start(s8[5242880]{0:T(1024)(128)(4,1)} %bitcast.10), calls=%async_computation | async-start | bytes 2097152
  16.6 76.5 %collective-permute-start.4 = (bf16[128,4096]{1,0:T(8,128)(2,1)S(1)}, bf16[128,4096]{1,0:T(8,128)(2,1)}, u32[]{:S(2)}, u32[]{:S(2)}) collective-permute-start(bf16[128,4096]{1,0:T(8,128)(2,1)S(1)} %pick_own.1.refs_2_), channel_id=1, source_target_pairs={{1,0},{66,1},{3,2},{68,3},{5,4},{70,5},{7,6},{72,7},{9,8},{74,9},{... | collective-permute-start | bytes 3145736 | tf_op jit(solution)/shard_map/ppermute | solution.py:457
  19.9 73.2 %collective-permute-start.1 = (bf16[128,4096]{1,0:T(8,128)(2,1)S(1)}, bf16[128,4096]{1,0:T(8,128)(2,1)}, u32[]{:S(2)}, u32[]{:S(2)}) collective-permute-start(bf16[128,4096]{1,0:T(8,128)(2,1)S(1)} %pick_own.1.refs_2_), channel_id=1, source_target_pairs={{0,1},{65,2},{2,3},{67,4},{4,5},{69,6},{6,7},{71,8},{8,9},{73,10},... | collective-permute-start | bytes 3145736 | tf_op jit(solution)/shard_map/ppermute | solution.py:456
  84.3 30.5 %collective-permute-start.5 = (bf16[128,4096]{1,0:T(8,128)(2,1)S(1)}, bf16[128,4096]{1,0:T(8,128)(2,1)}, u32[]{:S(2)}, u32[]{:S(2)}) collective-permute-start(bf16[128,4096]{1,0:T(8,128)(2,1)S(1)} %collective-permute-done.2.refs_3_), channel_id=1, source_target_pairs={{1,0},{66,1},{3,2},{68,3},{5,4},{70,5},{7,6},{72,7},{9,8},{74,9},{... | collective-permute-start | bytes 3145736 | tf_op jit(solution)/shard_map/ppermute | solution.py:462
  87.6 27.3 %collective-permute-start.3 = (bf16[128,4096]{1,0:T(8,128)(2,1)S(1)}, bf16[128,4096]{1,0:T(8,128)(2,1)}, u32[]{:S(2)}, u32[]{:S(2)}) collective-permute-start(bf16[128,4096]{1,0:T(8,128)(2,1)S(1)} %collective-permute-done.2.refs_3_), channel_id=1, source_target_pairs={{0,1},{65,2},{2,3},{67,4},{4,5},{69,6},{6,7},{71,8},{8,9},{73,10},... | collective-permute-start | bytes 3145736 | tf_op jit(solution)/shard_map/ppermute | solution.py:461
  114.9 24.7 %slice-start.1 = ((s8[5242880]{0:T(1024)(128)(4,1)}), s8[4194304]{0:T(1024)(128)(4,1)S(1)}, s32[]{:S(2)}) async-start(s8[5242880]{0:T(1024)(128)(4,1)} %bitcast.10), calls=%async_computation.1 | async-start | bytes 8388608
  125.7 23.6 %collective-permute-start.8 = (bf16[6,144,256]{2,1,0:T(8,128)(2,1)S(1)}, bf16[6,144,256]{2,1,0:T(8,128)(2,1)S(1)}, u32[]{:S(2)}, u32[]{:S(2)}) collective-permute-start(bf16[6,144,256]{2,1,0:T(8,128)(2,1)S(1)} %get-tuple-element.23), channel_id=1, source_target_pairs={{0,64},{64,0},{1,65},{65,1},{2,66},{66,2},{3,67},{67,3},{4,68},{68... | collective-permute-start | bytes 1327112 | tf_op jit(solution)/shard_map/ppermute | solution.py:475
  125.8 13.8 %collective-permute-start.9 = (bf16[2,144,256]{2,1,0:T(8,128)(2,1)S(1)}, bf16[2,144,256]{2,1,0:T(8,128)(2,1)S(1)}, u32[]{:S(2)}, u32[]{:S(2)}) collective-permute-start(bf16[2,144,256]{2,1,0:T(8,128)(2,1)S(1)} %get-tuple-element.24), channel_id=1, source_target_pairs={{0,64},{64,0},{1,65},{65,1},{2,66},{66,2},{3,67},{67,3},{4,68},{68... | collective-permute-start | bytes 442376 | tf_op jit(solution)/shard_map/ppermute | solution.py:475
  157.0 46.1 %collective-permute-start.13 = (bf16[10,128,256]{2,1,0:T(8,128)(2,1)S(1)}, bf16[10,128,256]{2,1,0:T(8,128)(2,1)S(1)}, u32[]{:S(2)}, u32[]{:S(2)}) collective-permute-start(bf16[10,128,256]{2,1,0:T(8,128)(2,1)S(1)} %get-tuple-element.33), channel_id=1, source_target_pairs={{0,64},{64,0},{1,65},{65,1},{2,66},{66,2},{3,67},{67,3},{4,68},{68... | collective-permute-start | bytes 1966088 | tf_op jit(solution)/shard_map/ppermute | solution.py:486
  164.7 39.8 %collective-permute-start.12 = (bf16[10,128,256]{2,1,0:T(8,128)(2,1)S(1)}, bf16[10,128,256]{2,1,0:T(8,128)(2,1)S(1)}, u32[]{:S(2)}, u32[]{:S(2)}) collective-permute-start(bf16[10,128,256]{2,1,0:T(8,128)(2,1)S(1)} %get-tuple-element.32), channel_id=1, source_target_pairs={{0,64},{64,0},{1,65},{65,1},{2,66},{66,2},{3,67},{67,3},{4,68},{68... | collective-permute-start | bytes 1966088 | tf_op jit(solution)/shard_map/ppermute | solution.py:486
  166.2 28.6 %collective-permute-start.15 = (bf16[10,128,128]{2,1,0:T(8,128)(2,1)S(1)}, bf16[10,128,128]{2,1,0:T(8,128)(2,1)S(1)}, u32[]{:S(2)}, u32[]{:S(2)}) collective-permute-start(bf16[10,128,128]{2,1,0:T(8,128)(2,1)S(1)} %get-tuple-element.35), channel_id=1, source_target_pairs={{0,64},{64,0},{1,65},{65,1},{2,66},{66,2},{3,67},{67,3},{4,68},{68... | collective-permute-start | bytes 983048 | tf_op jit(solution)/shard_map/ppermute | solution.py:486
  166.2 35.6 %collective-permute-start.14 = (bf16[10,128,128]{2,1,0:T(8,128)(2,1)S(1)}, bf16[10,128,128]{2,1,0:T(8,128)(2,1)S(1)}, u32[]{:S(2)}, u32[]{:S(2)}) collective-permute-start(bf16[10,128,128]{2,1,0:T(8,128)(2,1)S(1)} %get-tuple-element.34), channel_id=1, source_target_pairs={{0,64},{64,0},{1,65},{65,1},{2,66},{66,2},{3,67},{67,3},{4,68},{68... | collective-permute-start | bytes 983048 | tf_op jit(solution)/shard_map/ppermute | solution.py:486
  172.5 36.4 %collective-permute-start.11 = (bf16[10,128,128]{2,1,0:T(8,128)(2,1)S(1)}, bf16[10,128,128]{2,1,0:T(8,128)(2,1)S(1)}, u32[]{:S(2)}, u32[]{:S(2)}) collective-permute-start(bf16[10,128,128]{2,1,0:T(8,128)(2,1)S(1)} %get-tuple-element.31), channel_id=1, source_target_pairs={{0,64},{64,0},{1,65},{65,1},{2,66},{66,2},{3,67},{67,3},{4,68},{68... | collective-permute-start | bytes 983048 | tf_op jit(solution)/shard_map/ppermute | solution.py:486
  194.8 20.8 %collective-permute-start.10 = (bf16[10,128,128]{2,1,0:T(8,128)(2,1)S(1)}, bf16[10,128,128]{2,1,0:T(8,128)(2,1)S(1)}, u32[]{:S(2)}, u32[]{:S(2)}) collective-permute-start(bf16[10,128,128]{2,1,0:T(8,128)(2,1)S(1)} %get-tuple-element.30), channel_id=1, source_target_pairs={{0,64},{64,0},{1,65},{65,1},{2,66},{66,2},{3,67},{67,3},{4,68},{68... | collective-permute-start | bytes 983048 | tf_op jit(solution)/shard_map/ppermute | solution.py:486

commit v3 on v2

--- a/solution.py
+++ b/solution.py
@@ -11,7 +11,6 @@
 NSTEPS = 3
 ROWS = 16
 AHEAD = 3
-STAGES = 4
 PIECES = (1, 1, 2, 2, 1, 1)
 SUMS = (2, 6)
 
@@ -28,45 +27,30 @@
     return pairs
 
 
-def pick_body(source, picked, stage, sems, *, partner):
+def pick_body(source, *refs, partner):
+    picked, sem = refs[-2:]
     size = picked.shape[1]
     mem = lax.axis_index("mem")
     start = pl.multiple_of((1 - mem if partner else mem) * size, size)
-    rows = picked.shape[0] // STAGES
-    inward, outward = [], []
-    for k in range(STAGES):
-        at = pl.ds(k * rows, rows)
-        inward.append(
-            pltpu.make_async_copy(
-                source.at[at, pl.ds(start, size)], stage.at[at, :], sems.at[0, k]
-            )
-        )
-        outward.append(pltpu.make_async_copy(stage.at[at, :], picked.at[at, :], sems.at[1, k]))
-        inward[k].start()
-    for k in range(STAGES):
-        inward[k].wait()
-        outward[k].start()
-    for k in range(STAGES):
-        outward[k].wait()
-
-
-def pick_half(source, partner):
+    copy = pltpu.make_async_copy(source.at[:, pl.ds(start, size)], picked, sem)
+    copy.start()
+    copy.wait()
+
+
+def pick_half(source, partner, *after):
     rows, cols = source.shape
     return pl.pallas_call(
         functools.partial(pick_body, partner=partner),
-        in_specs=[pl.BlockSpec(memory_space=pl.ANY)],
+        in_specs=[pl.BlockSpec(memory_space=pl.ANY)] * (1 + len(after)),
         out_specs=pl.BlockSpec(memory_space=pl.ANY),
-        scratch_shapes=[
-            pltpu.VMEM((rows, cols // 2), source.dtype),
-            pltpu.SemaphoreType.DMA((2, STAGES)),
-        ],
+        scratch_shapes=[pltpu.SemaphoreType.DMA],
         out_shape=jax.ShapeDtypeStruct((rows, cols // 2), source.dtype),
         cost_estimate=pl.CostEstimate(
             flops=0, bytes_accessed=2 * source.size, transcendentals=0
         ),
         compiler_params=pltpu.CompilerParams(vmem_limit_bytes=4 << 20),
         name="pick_partner" if partner else "pick_own",
-    )(pltpu.with_memory_space_constraint(source, pltpu.HBM))
+    )(pltpu.with_memory_space_constraint(source, pltpu.HBM), *after)
 
 
 def locate(lists, meta, row, n, blocks_dev):
@@ -209,6 +193,7 @@
         return
     groups = members // ROWS
     diagonal = jnp.sum(jnp.where(on_diagonal(members), matrix, 0.0), axis=0, keepdims=True)
+    matrix = 0.5 * (matrix + matrix.T)
     lane = lax.broadcasted_iota(jnp.int32, (ROWS, members), 1)
     packed = [matrix[:ROWS]]
     for group in range(1, groups // 2):
@@ -451,8 +436,9 @@
     meta = jnp.stack([member_no, tile_no]).astype(jnp.int32)
 
     obs = members_in_reading_space
-    swapped = lax.ppermute(pick_half(obs, True), "mem", swap)
-    own_set = pick_half(obs, False)
+    other_set = pick_half(obs, True)
+    swapped = lax.ppermute(other_set, "mem", swap)
+    own_set = pick_half(obs, False, other_set)
     low_own = lax.ppermute(own_set, both, from_low)
     high_own = lax.ppermute(own_set, both, from_high)
     half = cols // 2

time: 218 us -> 218 us (level)
  transfers between devices with their start and end apart: 16 -> 16, of which waited for: 7 -> 7; matrix products, arithmetic and copies ran while one was open for 0% -> 0% of each run, Pallas kernels for 26% -> 27%
where the time goes in v3:
time: 218 us
  waiting for transfers between devices  117 us (54%)
  Pallas kernels  66.7 us (31%)
  starting transfers between devices  30.1 us (14%)
  local copies, waits for them, and re-layouts  3.53 us (2%)
    ppermute x1, waiting for transfers between devices, per_device(): swapped = lax.ppermute(other_set, 'mem', swap)  61 us
    pallas_call x6, Pallas kernels, analyse(): pl.pallas_call(functools.partial(analysis_body, width=width), grid_spec=p...  34.8 us
    ppermute x6, waiting for transfers between devices, per_device(): arrived.append(lax.ppermute(sent, 'mem', swap))  31.7 us
    ppermute x1, waiting for transfers between devices, per_device(): high_other = lax.ppermute(swapped, both, from_high)  21.8 us
    pallas_call x2, Pallas kernels, partial_sums(): pl.pallas_call(functools.partial(sums_body, for_self=for_self, blocks_dev...  21.4 us
    pallas_call x6, Pallas kernels, place(): pl.pallas_call(functools.partial(place_body, first=first, width=width), g...  7.89 us
    ppermute x1, starting transfers between devices, per_device(): table_low = lax.ppermute(table, both, from_low)  5.56 us
    ppermute x1, starting transfers between devices, per_device(): low_other = lax.ppermute(swapped, both, from_low)  5.39 us
  transfers between devices with their start and end apart: 16, of which 7 were waited for; matrix products, arithmetic and copies ran while one was open for 0% of the time, Pallas kernels for 27%

profile of v3, /device:TPU:9, one launch (start us, length us, event | category | flops | bytes accessed | tf_op | source)
XLA Modules:
  0.0 217.8 jit_solution(10557348131700157704)
XLA Ops:
  0.0 0.0 copy-start.3
  0.0 0.0 copy-start.1
  0.0 0.0 copy-start.2
  0.0 0.0 copy-start
  0.0 3.5 %dynamic-slice_bitcast_fusion = bf16[10,128,1024]{2,1,0:T(8,128)(2,1)} fusion(bf16[128,10,2048]{2,0,1:T(8,128)(2,1)} %param.6, s32[]{:T(128)S(6)} %select_n.7), kind=kLoop, calls=%fused_computation | loop fusion | bytes 5242884 | tf_op jit(solution)/shard_map/dynamic_slice | solution.py:445
  3.5 1.6 collective-permute-start
  5.2 1.2 pick_partner.1.refs_0_
  6.4 0.1 collective-permute-start.2
  6.5 0.0 copy-done.3
  6.5 0.0 copy-done.1
  6.5 0.1 bitcast_select_fusion
  6.6 0.0 copy-done.2
  6.6 2.9 %collective-permute-start.7 = (f32[128,128]{1,0:T(8,128)S(1)}, f32[128,128]{1,0:T(8,128)S(1)}, u32[]{:S(2)}, u32[]{:S(2)}) collective-permute-start(f32[128,128]{1,0:T(8,128)S(1)} %pad_maximum_fusion.refs_7_), channel_id=1, source_target_pairs={{1,0},{66,1},{3,2},{68,3},{5,4},{70,5},{7,6},{72,7},{9,8},{74,9},{... | collective-permute-start | bytes 196616 | tf_op jit(solution)/shard_map/ppermute | solution.py:455
  9.6 5.6 %collective-permute-start.6 = (f32[128,128]{1,0:T(8,128)S(1)}, f32[128,128]{1,0:T(8,128)S(1)}, u32[]{:S(2)}, u32[]{:S(2)}) collective-permute-start(f32[128,128]{1,0:T(8,128)S(1)} %pad_maximum_fusion.refs_7_), channel_id=1, source_target_pairs={{0,1},{65,2},{2,3},{67,4},{4,5},{69,6},{6,7},{71,8},{8,9},{73,10},... | collective-permute-start | bytes 196616 | tf_op jit(solution)/shard_map/ppermute | solution.py:454
  15.1 0.0 slice-start
  15.2 1.3 pick_own.1.refs_2_
  16.5 3.3 %collective-permute-start.4 = (bf16[128,4096]{1,0:T(8,128)(2,1)S(1)}, bf16[128,4096]{1,0:T(8,128)(2,1)}, u32[]{:S(2)}, u32[]{:S(2)}) collective-permute-start(bf16[128,4096]{1,0:T(8,128)(2,1)S(1)} %pick_own.1.refs_2_), channel_id=1, source_target_pairs={{1,0},{66,1},{3,2},{68,3},{5,4},{70,5},{7,6},{72,7},{9,8},{74,9},{... | collective-permute-start | bytes 3145736 | tf_op jit(solution)/shard_map/ppermute | solution.py:443
  19.8 0.0 collective-permute-done.7.refs_8_
  19.8 3.5 %collective-permute-start.1 = (bf16[128,4096]{1,0:T(8,128)(2,1)S(1)}, bf16[128,4096]{1,0:T(8,128)(2,1)}, u32[]{:S(2)}, u32[]{:S(2)}) collective-permute-start(bf16[128,4096]{1,0:T(8,128)(2,1)S(1)} %pick_own.1.refs_2_), channel_id=1, source_target_pairs={{0,1},{65,2},{2,3},{67,4},{4,5},{69,6},{6,7},{71,8},{8,9},{73,10},... | collective-permute-start | bytes 3145736 | tf_op jit(solution)/shard_map/ppermute | solution.py:442
  23.3 61.0 %collective-permute-done.2.refs_3_ = bf16[128,4096]{1,0:T(8,128)(2,1)S(1)} collective-permute-done((bf16[128,4096]{1,0:T(8,128)(2,1)S(1)}, bf16[128,4096]{1,0:T(8,128)(2,1)S(1)}, u32[]{:S(2)}, u32[]{:S(2)}) %collective-permute-start.2) | collective-permute-done | bytes 1048608 | tf_op jit(solution)/shard_map/ppermute | solution.py:440
  84.3 3.3 %collective-permute-start.5 = (bf16[128,4096]{1,0:T(8,128)(2,1)S(1)}, bf16[128,4096]{1,0:T(8,128)(2,1)}, u32[]{:S(2)}, u32[]{:S(2)}) collective-permute-start(bf16[128,4096]{1,0:T(8,128)(2,1)S(1)} %collective-permute-done.2.refs_3_), channel_id=1, source_target_pairs={{1,0},{66,1},{3,2},{68,3},{5,4},{70,5},{7,6},{72,7},{9,8},{74,9},{... | collective-permute-start | bytes 3145736 | tf_op jit(solution)/shard_map/ppermute | solution.py:448
  87.6 0.0 collective-permute-done.6.refs_6_
  87.6 5.4 %collective-permute-start.3 = (bf16[128,4096]{1,0:T(8,128)(2,1)S(1)}, bf16[128,4096]{1,0:T(8,128)(2,1)}, u32[]{:S(2)}, u32[]{:S(2)}) collective-permute-start(bf16[128,4096]{1,0:T(8,128)(2,1)S(1)} %collective-permute-done.2.refs_3_), channel_id=1, source_target_pairs={{0,1},{65,2},{2,3},{67,4},{4,5},{69,6},{6,7},{71,8},{8,9},{73,10},... | collective-permute-start | bytes 3145736 | tf_op jit(solution)/shard_map/ppermute | solution.py:447
  93.0 0.1 pad_add_fusion.meta
  93.1 0.0 collective-permute-done.4.refs_4_
  93.1 0.0 collective-permute-done.1.refs_0_
  93.1 21.8 %collective-permute-done.5.refs_5_ = bf16[128,4096]{1,0:T(8,128)(2,1)} collective-permute-done((bf16[128,4096]{1,0:T(8,128)(2,1)S(1)}, bf16[128,4096]{1,0:T(8,128)(2,1)}, u32[]{:S(2)}, u32[]{:S(2)}) %collective-permute-start.5) | collective-permute-done | bytes 1048608 | tf_op jit(solution)/shard_map/ppermute | solution.py:448
  114.9 0.0 collective-permute-done.3.refs_1_
  114.9 0.0 copy-done
  114.9 0.0 slice-start.1
  114.9 11.4 %sums_send.1 = (bf16[2,144,256]{2,1,0:T(8,128)(2,1)S(1)}, bf16[6,144,256]{2,1,0:T(8,128)(2,1)S(1)}) custom-call(s32[8,16]{1,0:T(8,128)S(1)} %bitcast.18, s32[2]{0:T(128)S(1)} %pad_add_fusion.meta, bf16[128,4096]{1,0:T(8,128)(2,1)} %collective-permute-done.1.refs_0_, bf16[128,4096]{1,0:T(8,128)(2,1)} %collective-permute-done.3.refs_1_, ...), custom_call_target="tpu_custom_call" | custom-call | flops 1073741824 | bytes 4194304 | tf_op jit(solution)/shard_map/sums_send/pallas_call | solution.py:242
  126.2 0.1 collective-permute-start.8
  126.3 1.5 collective-permute-start.9
  127.8 10.0 %sums_self.1 = (f32[8,256,256]{2,1,0:T(8,128)S(1)}, f32[8,8,256]{2,1,0:T(8,128)S(1)}) custom-call(s32[8,16]{1,0:T(8,128)S(1)} %bitcast.19, s32[2]{0:T(128)S(1)} %pad_add_fusion.meta, bf16[128,4096]{1,0:T(8,128)(2,1)} %collective-permute-done.1.refs_0_, bf16[128,4096]{1,0:T(8,128)(2,1)} %collective-permute-done.3.refs_1_, ...), custom_call_target="tpu_custom_call" | custom-call | flops 1073741824 | bytes 4194304 | tf_op jit(solution)/shard_map/sums_self/pallas_call | solution.py:242
  137.8 2.3 %collective-permute-done.9.received = bf16[2,144,256]{2,1,0:T(8,128)(2,1)S(1)} collective-permute-done((bf16[2,144,256]{2,1,0:T(8,128)(2,1)S(1)}, bf16[2,144,256]{2,1,0:T(8,128)(2,1)S(1)}, u32[]{:S(2)}, u32[]{:S(2)}) %collective-permute-start.9) | collective-permute-done | bytes 147488 | tf_op jit(solution)/shard_map/ppermute | solution.py:461
  140.2 0.0 collective-permute-done.theirs
  140.2 0.0 slice-done
  140.2 0.0 slice-done.1
  140.2 4.9 %analyse.6 = (bf16[10,128,2048]{2,1,0:T(8,128)(2,1)}, bf16[10,128,128]{2,1,0:T(8,128)(2,1)S(1)}) custom-call(s32[2]{0:T(128)S(1)} %pad_add_fusion.meta, bf16[10,128,2048]{2,1,0:T(8,128)(2,1)S(1)} %bitcast.12, bf16[10,128,1024]{2,1,0:T(8,128)(2,1)} %collective-permute-done.theirs, f32[8,256,256]{2,1,0:T(8,128)S(1)} %get-tuple-element.21.ours, ...), custom_call_target="tpu_custom_call" | custom-call | flops 771751936 | bytes 1310720 | tf_op jit(solution)/shard_map/analyse/pallas_call | solution.py:358
  145.0 4.9 %analyse.7 = (bf16[10,128,2048]{2,1,0:T(8,128)(2,1)}, bf16[10,128,128]{2,1,0:T(8,128)(2,1)S(1)}) custom-call(s32[2]{0:T(128)S(1)} %pad_add_fusion.meta, bf16[10,128,2048]{2,1,0:T(8,128)(2,1)S(1)} %bitcast.13, bf16[10,128,1024]{2,1,0:T(8,128)(2,1)} %collective-permute-done.theirs, ...), custom_call_target="tpu_custom_call", output_to_operand_aliasing={{0}: (6, {})} | custom-call | flops 771751936 | bytes 1310720 | tf_op jit(solution)/shard_map/analyse/pallas_call | solution.py:358
  149.9 0.0 collective-permute-done.8.received
  149.9 7.7 %analyse.8 = (bf16[10,128,2048]{2,1,0:T(8,128)(2,1)}, bf16[10,128,256]{2,1,0:T(8,128)(2,1)S(1)}) custom-call(s32[2]{0:T(128)S(1)} %pad_add_fusion.meta, bf16[10,128,2048]{2,1,0:T(8,128)(2,1)S(1)} %bitcast.14, bf16[10,128,1024]{2,1,0:T(8,128)(2,1)} %collective-permute-done.theirs, ...), custom_call_target="tpu_custom_call", output_to_operand_aliasing={{0}: (6, {})} | custom-call | flops 1543503872 | bytes 2621440 | tf_op jit(solution)/shard_map/analyse/pallas_call | solution.py:358
  157.6 0.0 collective-permute-start.13
  157.6 7.7 %analyse.9 = (bf16[10,128,2048]{2,1,0:T(8,128)(2,1)}, bf16[10,128,256]{2,1,0:T(8,128)(2,1)S(1)}) custom-call(s32[2]{0:T(128)S(1)} %pad_add_fusion.meta, bf16[10,128,2048]{2,1,0:T(8,128)(2,1)S(1)} %bitcast.15, bf16[10,128,1024]{2,1,0:T(8,128)(2,1)} %collective-permute-done.theirs, ...), custom_call_target="tpu_custom_call", output_to_operand_aliasing={{0}: (6, {})} | custom-call | flops 1543503872 | bytes 2621440 | tf_op jit(solution)/shard_map/analyse/pallas_call | solution.py:358
  165.3 1.5 collective-permute-start.12
  166.8 0.0 collective-permute-start.15
  166.8 1.4 collective-permute-start.14
  168.2 4.9 %analyse.10 = (bf16[10,128,2048]{2,1,0:T(8,128)(2,1)}, bf16[10,128,128]{2,1,0:T(8,128)(2,1)S(1)}) custom-call(s32[2]{0:T(128)S(1)} %pad_add_fusion.meta, bf16[10,128,2048]{2,1,0:T(8,128)(2,1)S(1)} %bitcast.16, bf16[10,128,1024]{2,1,0:T(8,128)(2,1)} %collective-permute-done.theirs, ...), custom_call_target="tpu_custom_call", output_to_operand_aliasing={{0}: (6, {})} | custom-call | flops 771751936 | bytes 1310720 | tf_op jit(solution)/shard_map/analyse/pallas_call | solution.py:358
  173.1 0.0 collective-permute-start.11
  173.1 4.9 %analyse.11 = (bf16[10,128,2048]{2,1,0:T(8,128)(2,1)}, bf16[10,128,128]{2,1,0:T(8,128)(2,1)S(1)}) custom-call(s32[2]{0:T(128)S(1)} %pad_add_fusion.meta, bf16[10,128,2048]{2,1,0:T(8,128)(2,1)S(1)} %bitcast.17, bf16[10,128,1024]{2,1,0:T(8,128)(2,1)} %collective-permute-done.theirs, ...), custom_call_target="tpu_custom_call", output_to_operand_aliasing={{0}: (6, {})} | custom-call | flops 771751936 | bytes 1310720 | tf_op jit(solution)/shard_map/analyse/pallas_call | solution.py:358
  178.0 17.4 %collective-permute-done.15.piece = bf16[10,128,128]{2,1,0:T(8,128)(2,1)S(1)} collective-permute-done((bf16[10,128,128]{2,1,0:T(8,128)(2,1)S(1)}, bf16[10,128,128]{2,1,0:T(8,128)(2,1)S(1)}, u32[]{:S(2)}, u32[]{:S(2)}) %collective-permute-start.15) | collective-permute-done | bytes 327712 | tf_op jit(solution)/shard_map/ppermute | solution.py:472
  195.4 0.0 collective-permute-start.10
  195.4 1.3 place.6.output
  196.7 5.7 %collective-permute-done.14.piece = bf16[10,128,128]{2,1,0:T(8,128)(2,1)S(1)} collective-permute-done((bf16[10,128,128]{2,1,0:T(8,128)(2,1)S(1)}, bf16[10,128,128]{2,1,0:T(8,128)(2,1)S(1)}, u32[]{:S(2)}, u32[]{:S(2)}) %collective-permute-start.14) | collective-permute-done | bytes 327712 | tf_op jit(solution)/shard_map/ppermute | solution.py:472
  202.4 1.3 place.7.output
  203.7 0.0 collective-permute-done.13.piece
  203.7 1.4 place.8.output
  205.1 0.0 collective-permute-done.12.piece
  205.2 1.4 place.9.output
  206.6 2.9 %collective-permute-done.11.piece = bf16[10,128,128]{2,1,0:T(8,128)(2,1)S(1)} collective-permute-done((bf16[10,128,128]{2,1,0:T(8,128)(2,1)S(1)}, bf16[10,128,128]{2,1,0:T(8,128)(2,1)S(1)}, u32[]{:S(2)}, u32[]{:S(2)}) %collective-permute-start.11) | collective-permute-done | bytes 327712 | tf_op jit(solution)/shard_map/ppermute | solution.py:472
  209.5 1.3 place.10.output
  210.8 5.6 %collective-permute-done.10.piece = bf16[10,128,128]{2,1,0:T(8,128)(2,1)S(1)} collective-permute-done((bf16[10,128,128]{2,1,0:T(8,128)(2,1)S(1)}, bf16[10,128,128]{2,1,0:T(8,128)(2,1)S(1)}, u32[]{:S(2)}, u32[]{:S(2)}) %collective-permute-start.10) | collective-permute-done | bytes 327712 | tf_op jit(solution)/shard_map/ppermute | solution.py:472
  216.3 1.3 place.11
  (2 shorter events, 0.0 us)
Async XLA Ops:
  0.0 6.5 %copy-start.3 = (s32[64]{0:T(128)S(1)}, s32[64]{0:T(128)}, u32[]{:S(2)}) copy-start(s32[64]{0:T(128)} %param.10) | copy-start | bytes 772
  0.0 6.5 %copy-start.1 = (f32[8192]{0:T(1024)S(1)}, f32[8192]{0:T(1024)}, u32[]{:S(2)}) copy-start(f32[8192]{0:T(1024)} %param.9) | copy-start | bytes 98308
  0.0 6.6 %copy-start.2 = (f32[8192]{0:T(1024)S(1)}, f32[8192]{0:T(1024)}, u32[]{:S(2)}) copy-start(f32[8192]{0:T(1024)} %param.8) | copy-start | bytes 98308
  0.0 114.8 %copy-start = (s32[16,8]{0,1:T(8,128)S(1)}, s32[16,8]{0,1:T(8,128)}, u32[]{:S(2)}) copy-start(s32[16,8]{0,1:T(8,128)} %param.11) | copy-start | bytes 1540
  3.5 136.6 %collective-permute-start = (bf16[10,128,1024]{2,1,0:T(8,128)(2,1)}, bf16[10,128,1024]{2,1,0:T(8,128)(2,1)}, u32[]{:S(2)}, u32[]{:S(2)}) collective-permute-start(bf16[10,128,1024]{2,1,0:T(8,128)(2,1)} %dynamic-slice_bitcast_fusion), channel_id=1, source_target_pairs={{0,64},{64,0},{1,65},{65,1},{2,66},{66,2},{3,67},{67,3},{4,68},{68... | collective-permute-start | bytes 7864328 | tf_op jit(solution)/shard_map/ppermute | solution.py:446
  6.4 77.9 %collective-permute-start.2 = (bf16[128,4096]{1,0:T(8,128)(2,1)S(1)}, bf16[128,4096]{1,0:T(8,128)(2,1)S(1)}, u32[]{:S(2)}, u32[]{:S(2)}) collective-permute-start(bf16[128,4096]{1,0:T(8,128)(2,1)S(1)} %pick_partner.1.refs_0_), channel_id=1, source_target_pairs={{0,64},{64,0},{1,65},{65,1},{2,66},{66,2},{3,67},{67,3},{4,68},{68... | collective-permute-start | bytes 3145736 | tf_op jit(solution)/shard_map/ppermute | solution.py:440
  6.6 13.2 %collective-permute-start.7 = (f32[128,128]{1,0:T(8,128)S(1)}, f32[128,128]{1,0:T(8,128)S(1)}, u32[]{:S(2)}, u32[]{:S(2)}) collective-permute-start(f32[128,128]{1,0:T(8,128)S(1)} %pad_maximum_fusion.refs_7_), channel_id=1, source_target_pairs={{1,0},{66,1},{3,2},{68,3},{5,4},{70,5},{7,6},{72,7},{9,8},{74,9},{... | collective-permute-start | bytes 196616 | tf_op jit(solution)/shard_map/ppermute | solution.py:455
  9.6 78.0 %collective-permute-start.6 = (f32[128,128]{1,0:T(8,128)S(1)}, f32[128,128]{1,0:T(8,128)S(1)}, u32[]{:S(2)}, u32[]{:S(2)}) collective-permute-start(f32[128,128]{1,0:T(8,128)S(1)} %pad_maximum_fusion.refs_7_), channel_id=1, source_target_pairs={{0,1},{65,2},{2,3},{67,4},{4,5},{69,6},{6,7},{71,8},{8,9},{73,10},... | collective-permute-start | bytes 196616 | tf_op jit(solution)/shard_map/ppermute | solution.py:454
  15.1 125.0 %slice-start = ((s8[5242880]{0:T(1024)(128)(4,1)}), s8[1048576]{0:T(1024)(128)(4,1)S(1)}, s32[]{:S(2)}) async-start(s8[5242880]{0:T(1024)(128)(4,1)} %bitcast.10), calls=%async_computation | async-start | bytes 2097152
  16.5 76.6 %collective-permute-start.4 = (bf16[128,4096]{1,0:T(8,128)(2,1)S(1)}, bf16[128,4096]{1,0:T(8,128)(2,1)}, u32[]{:S(2)}, u32[]{:S(2)}) collective-permute-start(bf16[128,4096]{1,0:T(8,128)(2,1)S(1)} %pick_own.1.refs_2_), channel_id=1, source_target_pairs={{1,0},{66,1},{3,2},{68,3},{5,4},{70,5},{7,6},{72,7},{9,8},{74,9},{... | collective-permute-start | bytes 3145736 | tf_op jit(solution)/shard_map/ppermute | solution.py:443
  19.8 73.3 %collective-permute-start.1 = (bf16[128,4096]{1,0:T(8,128)(2,1)S(1)}, bf16[128,4096]{1,0:T(8,128)(2,1)}, u32[]{:S(2)}, u32[]{:S(2)}) collective-permute-start(bf16[128,4096]{1,0:T(8,128)(2,1)S(1)} %pick_own.1.refs_2_), channel_id=1, source_target_pairs={{0,1},{65,2},{2,3},{67,4},{4,5},{69,6},{6,7},{71,8},{8,9},{73,10},... | collective-permute-start | bytes 3145736 | tf_op jit(solution)/shard_map/ppermute | solution.py:442
  84.3 30.5 %collective-permute-start.5 = (bf16[128,4096]{1,0:T(8,128)(2,1)S(1)}, bf16[128,4096]{1,0:T(8,128)(2,1)}, u32[]{:S(2)}, u32[]{:S(2)}) collective-permute-start(bf16[128,4096]{1,0:T(8,128)(2,1)S(1)} %collective-permute-done.2.refs_3_), channel_id=1, source_target_pairs={{1,0},{66,1},{3,2},{68,3},{5,4},{70,5},{7,6},{72,7},{9,8},{74,9},{... | collective-permute-start | bytes 3145736 | tf_op jit(solution)/shard_map/ppermute | solution.py:448
  87.6 27.3 %collective-permute-start.3 = (bf16[128,4096]{1,0:T(8,128)(2,1)S(1)}, bf16[128,4096]{1,0:T(8,128)(2,1)}, u32[]{:S(2)}, u32[]{:S(2)}) collective-permute-start(bf16[128,4096]{1,0:T(8,128)(2,1)S(1)} %collective-permute-done.2.refs_3_), channel_id=1, source_target_pairs={{0,1},{65,2},{2,3},{67,4},{4,5},{69,6},{6,7},{71,8},{8,9},{73,10},... | collective-permute-start | bytes 3145736 | tf_op jit(solution)/shard_map/ppermute | solution.py:447
  114.9 25.3 %slice-start.1 = ((s8[5242880]{0:T(1024)(128)(4,1)}), s8[4194304]{0:T(1024)(128)(4,1)S(1)}, s32[]{:S(2)}) async-start(s8[5242880]{0:T(1024)(128)(4,1)} %bitcast.10), calls=%async_computation.1 | async-start | bytes 8388608
  126.2 23.7 %collective-permute-start.8 = (bf16[6,144,256]{2,1,0:T(8,128)(2,1)S(1)}, bf16[6,144,256]{2,1,0:T(8,128)(2,1)S(1)}, u32[]{:S(2)}, u32[]{:S(2)}) collective-permute-start(bf16[6,144,256]{2,1,0:T(8,128)(2,1)S(1)} %get-tuple-element.23), channel_id=1, source_target_pairs={{0,64},{64,0},{1,65},{65,1},{2,66},{66,2},{3,67},{67,3},{4,68},{68... | collective-permute-start | bytes 1327112 | tf_op jit(solution)/shard_map/ppermute | solution.py:461
  126.3 13.8 %collective-permute-start.9 = (bf16[2,144,256]{2,1,0:T(8,128)(2,1)S(1)}, bf16[2,144,256]{2,1,0:T(8,128)(2,1)S(1)}, u32[]{:S(2)}, u32[]{:S(2)}) collective-permute-start(bf16[2,144,256]{2,1,0:T(8,128)(2,1)S(1)} %get-tuple-element.24), channel_id=1, source_target_pairs={{0,64},{64,0},{1,65},{65,1},{2,66},{66,2},{3,67},{67,3},{4,68},{68... | collective-permute-start | bytes 442376 | tf_op jit(solution)/shard_map/ppermute | solution.py:461
  157.6 46.1 %collective-permute-start.13 = (bf16[10,128,256]{2,1,0:T(8,128)(2,1)S(1)}, bf16[10,128,256]{2,1,0:T(8,128)(2,1)S(1)}, u32[]{:S(2)}, u32[]{:S(2)}) collective-permute-start(bf16[10,128,256]{2,1,0:T(8,128)(2,1)S(1)} %get-tuple-element.33), channel_id=1, source_target_pairs={{0,64},{64,0},{1,65},{65,1},{2,66},{66,2},{3,67},{67,3},{4,68},{68... | collective-permute-start | bytes 1966088 | tf_op jit(solution)/shard_map/ppermute | solution.py:472
  165.3 39.8 %collective-permute-start.12 = (bf16[10,128,256]{2,1,0:T(8,128)(2,1)S(1)}, bf16[10,128,256]{2,1,0:T(8,128)(2,1)S(1)}, u32[]{:S(2)}, u32[]{:S(2)}) collective-permute-start(bf16[10,128,256]{2,1,0:T(8,128)(2,1)S(1)} %get-tuple-element.32), channel_id=1, source_target_pairs={{0,64},{64,0},{1,65},{65,1},{2,66},{66,2},{3,67},{67,3},{4,68},{68... | collective-permute-start | bytes 1966088 | tf_op jit(solution)/shard_map/ppermute | solution.py:472
  166.8 28.6 %collective-permute-start.15 = (bf16[10,128,128]{2,1,0:T(8,128)(2,1)S(1)}, bf16[10,128,128]{2,1,0:T(8,128)(2,1)S(1)}, u32[]{:S(2)}, u32[]{:S(2)}) collective-permute-start(bf16[10,128,128]{2,1,0:T(8,128)(2,1)S(1)} %get-tuple-element.35), channel_id=1, source_target_pairs={{0,64},{64,0},{1,65},{65,1},{2,66},{66,2},{3,67},{67,3},{4,68},{68... | collective-permute-start | bytes 983048 | tf_op jit(solution)/shard_map/ppermute | solution.py:472
  166.8 35.6 %collective-permute-start.14 = (bf16[10,128,128]{2,1,0:T(8,128)(2,1)S(1)}, bf16[10,128,128]{2,1,0:T(8,128)(2,1)S(1)}, u32[]{:S(2)}, u32[]{:S(2)}) collective-permute-start(bf16[10,128,128]{2,1,0:T(8,128)(2,1)S(1)} %get-tuple-element.34), channel_id=1, source_target_pairs={{0,64},{64,0},{1,65},{65,1},{2,66},{66,2},{3,67},{67,3},{4,68},{68... | collective-permute-start | bytes 983048 | tf_op jit(solution)/shard_map/ppermute | solution.py:472
  173.1 36.4 %collective-permute-start.11 = (bf16[10,128,128]{2,1,0:T(8,128)(2,1)S(1)}, bf16[10,128,128]{2,1,0:T(8,128)(2,1)S(1)}, u32[]{:S(2)}, u32[]{:S(2)}) collective-permute-start(bf16[10,128,128]{2,1,0:T(8,128)(2,1)S(1)} %get-tuple-element.31), channel_id=1, source_target_pairs={{0,64},{64,0},{1,65},{65,1},{2,66},{66,2},{3,67},{67,3},{4,68},{68... | collective-permute-start | bytes 983048 | tf_op jit(solution)/shard_map/ppermute | solution.py:472
  195.4 20.9 %collective-permute-start.10 = (bf16[10,128,128]{2,1,0:T(8,128)(2,1)S(1)}, bf16[10,128,128]{2,1,0:T(8,128)(2,1)S(1)}, u32[]{:S(2)}, u32[]{:S(2)}) collective-permute-start(bf16[10,128,128]{2,1,0:T(8,128)(2,1)S(1)} %get-tuple-element.30), channel_id=1, source_target_pairs={{0,64},{64,0},{1,65},{65,1},{2,66},{66,2},{3,67},{67,3},{4,68},{68... | collective-permute-start | bytes 983048 | tf_op jit(solution)/shard_map/ppermute | solution.py:472

commit v4 on v3

--- a/solution.py
+++ b/solution.py
@@ -384,31 +384,28 @@
     )(meta, *operands)
 
 
-def place_body(meta, piece, output, placed, sem, *, first, width):
-    start = pl.multiple_of((1 - meta[0]) * (placed.shape[2] // 2) + first * width, width)
+def place_body(piece, output, placed, sem, *, first, width):
+    mem = lax.axis_index("mem")
+    start = pl.multiple_of((1 - mem) * (placed.shape[2] // 2) + first * width, width)
     copy = pltpu.make_async_copy(piece, placed.at[:, :, pl.ds(start, piece.shape[2])], sem)
     copy.start()
     copy.wait()
 
 
-def place(meta, piece, output, first, width):
+def place(piece, output, first, width):
     return pl.pallas_call(
         functools.partial(place_body, first=first, width=width),
-        grid_spec=pltpu.PrefetchScalarGridSpec(
-            num_scalar_prefetch=1,
-            grid=(1,),
-            in_specs=[pl.BlockSpec(memory_space=pl.ANY)] * 2,
-            out_specs=pl.BlockSpec(memory_space=pl.ANY),
-            scratch_shapes=[pltpu.SemaphoreType.DMA],
-        ),
+        in_specs=[pl.BlockSpec(memory_space=pl.ANY)] * 2,
+        out_specs=pl.BlockSpec(memory_space=pl.ANY),
+        scratch_shapes=[pltpu.SemaphoreType.DMA],
         out_shape=jax.ShapeDtypeStruct(output.shape, output.dtype),
-        input_output_aliases={2: 0},
+        input_output_aliases={1: 0},
         cost_estimate=pl.CostEstimate(
             flops=0, bytes_accessed=4 * piece.size, transcendentals=0
         ),
         compiler_params=pltpu.CompilerParams(vmem_limit_bytes=2 << 20),
         name="place",
-    )(meta, piece, output)
+    )(piece, output)
 
 
 def per_device(
@@ -471,7 +468,7 @@
         )
         arrived.append(lax.ppermute(sent, "mem", swap))
     for k, piece in enumerate(arrived):
-        output = place(meta, piece, output, sum(PIECES[:k]), width)
+        output = place(piece, output, sum(PIECES[:k]), width)
     return jnp.transpose(output, (1, 0, 2))
 
 

time: 218 us -> 218 us (level)
  Pallas kernels: 66.7 us -> 63.5 us
    pallas_call x6, Pallas kernels: 7.89 us -> 4.65 us  [place(): pl.pallas_call(functools.partial(place_body, first=first, width=width), i...]
    ppermute x6, waiting for transfers between devices: 31.7 us -> 34.4 us  [per_device(): arrived.append(lax.ppermute(sent, 'mem', swap))]
  transfers between devices with their start and end apart: 16 -> 16, of which waited for: 7 -> 7; matrix products, arithmetic and copies ran while one was open for 0% -> 0% of each run, Pallas kernels for 27% -> 25%
where the time goes in v4:
time: 218 us; the launch traced here: 217 us
  waiting for transfers between devices  119 us (55%)
  Pallas kernels  63.5 us (29%)
  starting transfers between devices  30.1 us (14%)
  local copies, waits for them, and re-layouts  3.53 us (2%)
    ppermute x1, waiting for transfers between devices, per_device(): swapped = lax.ppermute(other_set, 'mem', swap)  61 us
    pallas_call x6, Pallas kernels, analyse(): pl.pallas_call(functools.partial(analysis_body, width=width), grid_spec=p...  34.8 us
    ppermute x6, waiting for transfers between devices, per_device(): arrived.append(lax.ppermute(sent, 'mem', swap))  34.4 us
    ppermute x1, waiting for transfers between devices, per_device(): high_other = lax.ppermute(swapped, both, from_high)  21.8 us
    pallas_call x2, Pallas kernels, partial_sums(): pl.pallas_call(functools.partial(sums_body, for_self=for_self, blocks_dev...  21.4 us
    ppermute x1, starting transfers between devices, per_device(): table_low = lax.ppermute(table, both, from_low)  5.56 us
    ppermute x1, starting transfers between devices, per_device(): low_other = lax.ppermute(swapped, both, from_low)  5.39 us
    pallas_call x6, Pallas kernels, place(): pl.pallas_call(functools.partial(place_body, first=first, width=width), i...  4.65 us
  transfers between devices with their start and end apart: 16, of which 7 were waited for; matrix products, arithmetic and copies ran while one was open for 0% of the time, Pallas kernels for 25%

profile of v4, /device:TPU:9, one launch (start us, length us, event | category | flops | bytes accessed | tf_op | source)
XLA Modules:
  0.0 217.2 jit_solution(14306483773181614622)
XLA Ops:
  0.0 0.0 copy-start.3
  0.0 0.0 copy-start.1
  0.0 0.0 copy-start.2
  0.0 0.0 copy-start
  0.0 3.5 %dynamic-slice_bitcast_fusion = bf16[10,128,1024]{2,1,0:T(8,128)(2,1)} fusion(bf16[128,10,2048]{2,0,1:T(8,128)(2,1)} %param.6, s32[]{:T(128)S(6)} %select_n.7), kind=kLoop, calls=%fused_computation | loop fusion | bytes 5242884 | tf_op jit(solution)/shard_map/dynamic_slice | solution.py:442
  3.5 1.6 collective-permute-start
  5.2 1.2 pick_partner.1.refs_0_
  6.4 0.1 collective-permute-start.2
  6.5 0.0 copy-done.3
  6.5 0.0 copy-done.1
  6.5 0.1 bitcast_select_fusion
  6.6 0.0 copy-done.2
  6.6 2.9 %collective-permute-start.7 = (f32[128,128]{1,0:T(8,128)S(1)}, f32[128,128]{1,0:T(8,128)S(1)}, u32[]{:S(2)}, u32[]{:S(2)}) collective-permute-start(f32[128,128]{1,0:T(8,128)S(1)} %pad_maximum_fusion.refs_7_), channel_id=1, source_target_pairs={{1,0},{66,1},{3,2},{68,3},{5,4},{70,5},{7,6},{72,7},{9,8},{74,9},{... | collective-permute-start | bytes 196616 | tf_op jit(solution)/shard_map/ppermute | solution.py:452
  9.6 5.6 %collective-permute-start.6 = (f32[128,128]{1,0:T(8,128)S(1)}, f32[128,128]{1,0:T(8,128)S(1)}, u32[]{:S(2)}, u32[]{:S(2)}) collective-permute-start(f32[128,128]{1,0:T(8,128)S(1)} %pad_maximum_fusion.refs_7_), channel_id=1, source_target_pairs={{0,1},{65,2},{2,3},{67,4},{4,5},{69,6},{6,7},{71,8},{8,9},{73,10},... | collective-permute-start | bytes 196616 | tf_op jit(solution)/shard_map/ppermute | solution.py:451
  15.1 0.0 slice-start
  15.2 1.3 pick_own.1.refs_2_
  16.5 3.3 %collective-permute-start.4 = (bf16[128,4096]{1,0:T(8,128)(2,1)S(1)}, bf16[128,4096]{1,0:T(8,128)(2,1)}, u32[]{:S(2)}, u32[]{:S(2)}) collective-permute-start(bf16[128,4096]{1,0:T(8,128)(2,1)S(1)} %pick_own.1.refs_2_), channel_id=1, source_target_pairs={{1,0},{66,1},{3,2},{68,3},{5,4},{70,5},{7,6},{72,7},{9,8},{74,9},{... | collective-permute-start | bytes 3145736 | tf_op jit(solution)/shard_map/ppermute | solution.py:440
  19.8 0.0 collective-permute-done.7.refs_8_
  19.8 3.5 %collective-permute-start.1 = (bf16[128,4096]{1,0:T(8,128)(2,1)S(1)}, bf16[128,4096]{1,0:T(8,128)(2,1)}, u32[]{:S(2)}, u32[]{:S(2)}) collective-permute-start(bf16[128,4096]{1,0:T(8,128)(2,1)S(1)} %pick_own.1.refs_2_), channel_id=1, source_target_pairs={{0,1},{65,2},{2,3},{67,4},{4,5},{69,6},{6,7},{71,8},{8,9},{73,10},... | collective-permute-start | bytes 3145736 | tf_op jit(solution)/shard_map/ppermute | solution.py:439
  23.3 61.0 %collective-permute-done.2.refs_3_ = bf16[128,4096]{1,0:T(8,128)(2,1)S(1)} collective-permute-done((bf16[128,4096]{1,0:T(8,128)(2,1)S(1)}, bf16[128,4096]{1,0:T(8,128)(2,1)S(1)}, u32[]{:S(2)}, u32[]{:S(2)}) %collective-permute-start.2) | collective-permute-done | bytes 1048608 | tf_op jit(solution)/shard_map/ppermute | solution.py:437
  84.3 3.3 %collective-permute-start.5 = (bf16[128,4096]{1,0:T(8,128)(2,1)S(1)}, bf16[128,4096]{1,0:T(8,128)(2,1)}, u32[]{:S(2)}, u32[]{:S(2)}) collective-permute-start(bf16[128,4096]{1,0:T(8,128)(2,1)S(1)} %collective-permute-done.2.refs_3_), channel_id=1, source_target_pairs={{1,0},{66,1},{3,2},{68,3},{5,4},{70,5},{7,6},{72,7},{9,8},{74,9},{... | collective-permute-start | bytes 3145736 | tf_op jit(solution)/shard_map/ppermute | solution.py:445
  87.6 0.0 collective-permute-done.6.refs_6_
  87.6 5.4 %collective-permute-start.3 = (bf16[128,4096]{1,0:T(8,128)(2,1)S(1)}, bf16[128,4096]{1,0:T(8,128)(2,1)}, u32[]{:S(2)}, u32[]{:S(2)}) collective-permute-start(bf16[128,4096]{1,0:T(8,128)(2,1)S(1)} %collective-permute-done.2.refs_3_), channel_id=1, source_target_pairs={{0,1},{65,2},{2,3},{67,4},{4,5},{69,6},{6,7},{71,8},{8,9},{73,10},... | collective-permute-start | bytes 3145736 | tf_op jit(solution)/shard_map/ppermute | solution.py:444
  93.0 0.1 pad_add_fusion.meta
  93.1 0.0 collective-permute-done.4.refs_4_
  93.1 0.0 collective-permute-done.1.refs_0_
  93.1 21.8 %collective-permute-done.5.refs_5_ = bf16[128,4096]{1,0:T(8,128)(2,1)} collective-permute-done((bf16[128,4096]{1,0:T(8,128)(2,1)S(1)}, bf16[128,4096]{1,0:T(8,128)(2,1)}, u32[]{:S(2)}, u32[]{:S(2)}) %collective-permute-start.5) | collective-permute-done | bytes 1048608 | tf_op jit(solution)/shard_map/ppermute | solution.py:445
  114.9 0.0 collective-permute-done.3.refs_1_
  114.9 0.0 copy-done
  114.9 0.0 slice-start.1
  114.9 11.4 %sums_send.1 = (bf16[2,144,256]{2,1,0:T(8,128)(2,1)S(1)}, bf16[6,144,256]{2,1,0:T(8,128)(2,1)S(1)}) custom-call(s32[8,16]{1,0:T(8,128)S(1)} %bitcast.18, s32[2]{0:T(128)S(1)} %pad_add_fusion.meta, bf16[128,4096]{1,0:T(8,128)(2,1)} %collective-permute-done.1.refs_0_, bf16[128,4096]{1,0:T(8,128)(2,1)} %collective-permute-done.3.refs_1_, ...), custom_call_target="tpu_custom_call" | custom-call | flops 1073741824 | bytes 4194304 | tf_op jit(solution)/shard_map/sums_send/pallas_call | solution.py:242
  126.2 0.1 collective-permute-start.8
  126.3 1.5 collective-permute-start.9
  127.8 10.0 %sums_self.1 = (f32[8,256,256]{2,1,0:T(8,128)S(1)}, f32[8,8,256]{2,1,0:T(8,128)S(1)}) custom-call(s32[8,16]{1,0:T(8,128)S(1)} %bitcast.19, s32[2]{0:T(128)S(1)} %pad_add_fusion.meta, bf16[128,4096]{1,0:T(8,128)(2,1)} %collective-permute-done.1.refs_0_, bf16[128,4096]{1,0:T(8,128)(2,1)} %collective-permute-done.3.refs_1_, ...), custom_call_target="tpu_custom_call" | custom-call | flops 1073741824 | bytes 4194304 | tf_op jit(solution)/shard_map/sums_self/pallas_call | solution.py:242
  137.8 2.3 %collective-permute-done.9.received = bf16[2,144,256]{2,1,0:T(8,128)(2,1)S(1)} collective-permute-done((bf16[2,144,256]{2,1,0:T(8,128)(2,1)S(1)}, bf16[2,144,256]{2,1,0:T(8,128)(2,1)S(1)}, u32[]{:S(2)}, u32[]{:S(2)}) %collective-permute-start.9) | collective-permute-done | bytes 147488 | tf_op jit(solution)/shard_map/ppermute | solution.py:458
  140.2 0.0 collective-permute-done.theirs
  140.2 0.0 slice-done
  140.2 0.0 slice-done.1
  140.2 4.9 %analyse.6 = (bf16[10,128,2048]{2,1,0:T(8,128)(2,1)}, bf16[10,128,128]{2,1,0:T(8,128)(2,1)S(1)}) custom-call(s32[2]{0:T(128)S(1)} %pad_add_fusion.meta, bf16[10,128,2048]{2,1,0:T(8,128)(2,1)S(1)} %bitcast.12, bf16[10,128,1024]{2,1,0:T(8,128)(2,1)} %collective-permute-done.theirs, f32[8,256,256]{2,1,0:T(8,128)S(1)} %get-tuple-element.21.ours, ...), custom_call_target="tpu_custom_call" | custom-call | flops 771751936 | bytes 1310720 | tf_op jit(solution)/shard_map/analyse/pallas_call | solution.py:358
  145.0 4.9 %analyse.7 = (bf16[10,128,2048]{2,1,0:T(8,128)(2,1)}, bf16[10,128,128]{2,1,0:T(8,128)(2,1)S(1)}) custom-call(s32[2]{0:T(128)S(1)} %pad_add_fusion.meta, bf16[10,128,2048]{2,1,0:T(8,128)(2,1)S(1)} %bitcast.13, bf16[10,128,1024]{2,1,0:T(8,128)(2,1)} %collective-permute-done.theirs, ...), custom_call_target="tpu_custom_call", output_to_operand_aliasing={{0}: (6, {})} | custom-call | flops 771751936 | bytes 1310720 | tf_op jit(solution)/shard_map/analyse/pallas_call | solution.py:358
  149.9 0.0 collective-permute-done.8.received
  149.9 7.7 %analyse.8 = (bf16[10,128,2048]{2,1,0:T(8,128)(2,1)}, bf16[10,128,256]{2,1,0:T(8,128)(2,1)S(1)}) custom-call(s32[2]{0:T(128)S(1)} %pad_add_fusion.meta, bf16[10,128,2048]{2,1,0:T(8,128)(2,1)S(1)} %bitcast.14, bf16[10,128,1024]{2,1,0:T(8,128)(2,1)} %collective-permute-done.theirs, ...), custom_call_target="tpu_custom_call", output_to_operand_aliasing={{0}: (6, {})} | custom-call | flops 1543503872 | bytes 2621440 | tf_op jit(solution)/shard_map/analyse/pallas_call | solution.py:358
  157.6 0.0 collective-permute-start.13
  157.6 7.7 %analyse.9 = (bf16[10,128,2048]{2,1,0:T(8,128)(2,1)}, bf16[10,128,256]{2,1,0:T(8,128)(2,1)S(1)}) custom-call(s32[2]{0:T(128)S(1)} %pad_add_fusion.meta, bf16[10,128,2048]{2,1,0:T(8,128)(2,1)S(1)} %bitcast.15, bf16[10,128,1024]{2,1,0:T(8,128)(2,1)} %collective-permute-done.theirs, ...), custom_call_target="tpu_custom_call", output_to_operand_aliasing={{0}: (6, {})} | custom-call | flops 1543503872 | bytes 2621440 | tf_op jit(solution)/shard_map/analyse/pallas_call | solution.py:358
  165.3 1.5 collective-permute-start.12
  166.8 0.0 collective-permute-start.15
  166.8 1.4 collective-permute-start.14
  168.2 4.9 %analyse.10 = (bf16[10,128,2048]{2,1,0:T(8,128)(2,1)}, bf16[10,128,128]{2,1,0:T(8,128)(2,1)S(1)}) custom-call(s32[2]{0:T(128)S(1)} %pad_add_fusion.meta, bf16[10,128,2048]{2,1,0:T(8,128)(2,1)S(1)} %bitcast.16, bf16[10,128,1024]{2,1,0:T(8,128)(2,1)} %collective-permute-done.theirs, ...), custom_call_target="tpu_custom_call", output_to_operand_aliasing={{0}: (6, {})} | custom-call | flops 771751936 | bytes 1310720 | tf_op jit(solution)/shard_map/analyse/pallas_call | solution.py:358
  173.1 0.0 collective-permute-start.11
  173.1 4.9 %analyse.11 = (bf16[10,128,2048]{2,1,0:T(8,128)(2,1)}, bf16[10,128,128]{2,1,0:T(8,128)(2,1)S(1)}) custom-call(s32[2]{0:T(128)S(1)} %pad_add_fusion.meta, bf16[10,128,2048]{2,1,0:T(8,128)(2,1)S(1)} %bitcast.17, bf16[10,128,1024]{2,1,0:T(8,128)(2,1)} %collective-permute-done.theirs, ...), custom_call_target="tpu_custom_call", output_to_operand_aliasing={{0}: (6, {})} | custom-call | flops 771751936 | bytes 1310720 | tf_op jit(solution)/shard_map/analyse/pallas_call | solution.py:358
  178.0 17.4 %collective-permute-done.15.piece = bf16[10,128,128]{2,1,0:T(8,128)(2,1)S(1)} collective-permute-done((bf16[10,128,128]{2,1,0:T(8,128)(2,1)S(1)}, bf16[10,128,128]{2,1,0:T(8,128)(2,1)S(1)}, u32[]{:S(2)}, u32[]{:S(2)}) %collective-permute-start.15) | collective-permute-done | bytes 327712 | tf_op jit(solution)/shard_map/ppermute | solution.py:469
  195.4 0.0 collective-permute-start.10
  195.4 0.7 place.6.output
  196.2 6.3 %collective-permute-done.14.piece = bf16[10,128,128]{2,1,0:T(8,128)(2,1)S(1)} collective-permute-done((bf16[10,128,128]{2,1,0:T(8,128)(2,1)S(1)}, bf16[10,128,128]{2,1,0:T(8,128)(2,1)S(1)}, u32[]{:S(2)}, u32[]{:S(2)}) %collective-permute-start.14) | collective-permute-done | bytes 327712 | tf_op jit(solution)/shard_map/ppermute | solution.py:469
  202.4 0.7 place.7.output
  203.2 0.0 collective-permute-done.13.piece
  203.2 0.9 place.8.output
  204.1 0.0 collective-permute-done.12.piece
  204.1 0.9 place.9.output
  204.9 4.5 %collective-permute-done.11.piece = bf16[10,128,128]{2,1,0:T(8,128)(2,1)S(1)} collective-permute-done((bf16[10,128,128]{2,1,0:T(8,128)(2,1)S(1)}, bf16[10,128,128]{2,1,0:T(8,128)(2,1)S(1)}, u32[]{:S(2)}, u32[]{:S(2)}) %collective-permute-start.11) | collective-permute-done | bytes 327712 | tf_op jit(solution)/shard_map/ppermute | solution.py:469
  209.5 0.7 place.10.output
  210.2 6.1 %collective-permute-done.10.piece = bf16[10,128,128]{2,1,0:T(8,128)(2,1)S(1)} collective-permute-done((bf16[10,128,128]{2,1,0:T(8,128)(2,1)S(1)}, bf16[10,128,128]{2,1,0:T(8,128)(2,1)S(1)}, u32[]{:S(2)}, u32[]{:S(2)}) %collective-permute-start.10) | collective-permute-done | bytes 327712 | tf_op jit(solution)/shard_map/ppermute | solution.py:469
  216.3 0.7 place.11
  (2 shorter events, 0.0 us)
Async XLA Ops:
  0.0 6.5 %copy-start.3 = (s32[64]{0:T(128)S(1)}, s32[64]{0:T(128)}, u32[]{:S(2)}) copy-start(s32[64]{0:T(128)} %param.10) | copy-start | bytes 772
  0.0 6.5 %copy-start.1 = (f32[8192]{0:T(1024)S(1)}, f32[8192]{0:T(1024)}, u32[]{:S(2)}) copy-start(f32[8192]{0:T(1024)} %param.9) | copy-start | bytes 98308
  0.0 6.6 %copy-start.2 = (f32[8192]{0:T(1024)S(1)}, f32[8192]{0:T(1024)}, u32[]{:S(2)}) copy-start(f32[8192]{0:T(1024)} %param.8) | copy-start | bytes 98308
  0.0 114.8 %copy-start = (s32[16,8]{0,1:T(8,128)S(1)}, s32[16,8]{0,1:T(8,128)}, u32[]{:S(2)}) copy-start(s32[16,8]{0,1:T(8,128)} %param.11) | copy-start | bytes 1540
  3.5 136.6 %collective-permute-start = (bf16[10,128,1024]{2,1,0:T(8,128)(2,1)}, bf16[10,128,1024]{2,1,0:T(8,128)(2,1)}, u32[]{:S(2)}, u32[]{:S(2)}) collective-permute-start(bf16[10,128,1024]{2,1,0:T(8,128)(2,1)} %dynamic-slice_bitcast_fusion), channel_id=1, source_target_pairs={{0,64},{64,0},{1,65},{65,1},{2,66},{66,2},{3,67},{67,3},{4,68},{68... | collective-permute-start | bytes 7864328 | tf_op jit(solution)/shard_map/ppermute | solution.py:443
  6.4 77.9 %collective-permute-start.2 = (bf16[128,4096]{1,0:T(8,128)(2,1)S(1)}, bf16[128,4096]{1,0:T(8,128)(2,1)S(1)}, u32[]{:S(2)}, u32[]{:S(2)}) collective-permute-start(bf16[128,4096]{1,0:T(8,128)(2,1)S(1)} %pick_partner.1.refs_0_), channel_id=1, source_target_pairs={{0,64},{64,0},{1,65},{65,1},{2,66},{66,2},{3,67},{67,3},{4,68},{68... | collective-permute-start | bytes 3145736 | tf_op jit(solution)/shard_map/ppermute | solution.py:437
  6.6 13.2 %collective-permute-start.7 = (f32[128,128]{1,0:T(8,128)S(1)}, f32[128,128]{1,0:T(8,128)S(1)}, u32[]{:S(2)}, u32[]{:S(2)}) collective-permute-start(f32[128,128]{1,0:T(8,128)S(1)} %pad_maximum_fusion.refs_7_), channel_id=1, source_target_pairs={{1,0},{66,1},{3,2},{68,3},{5,4},{70,5},{7,6},{72,7},{9,8},{74,9},{... | collective-permute-start | bytes 196616 | tf_op jit(solution)/shard_map/ppermute | solution.py:452
  9.6 78.0 %collective-permute-start.6 = (f32[128,128]{1,0:T(8,128)S(1)}, f32[128,128]{1,0:T(8,128)S(1)}, u32[]{:S(2)}, u32[]{:S(2)}) collective-permute-start(f32[128,128]{1,0:T(8,128)S(1)} %pad_maximum_fusion.refs_7_), channel_id=1, source_target_pairs={{0,1},{65,2},{2,3},{67,4},{4,5},{69,6},{6,7},{71,8},{8,9},{73,10},... | collective-permute-start | bytes 196616 | tf_op jit(solution)/shard_map/ppermute | solution.py:451
  15.1 125.0 %slice-start = ((s8[5242880]{0:T(1024)(128)(4,1)}), s8[1048576]{0:T(1024)(128)(4,1)S(1)}, s32[]{:S(2)}) async-start(s8[5242880]{0:T(1024)(128)(4,1)} %bitcast.10), calls=%async_computation | async-start | bytes 2097152
  16.5 76.6 %collective-permute-start.4 = (bf16[128,4096]{1,0:T(8,128)(2,1)S(1)}, bf16[128,4096]{1,0:T(8,128)(2,1)}, u32[]{:S(2)}, u32[]{:S(2)}) collective-permute-start(bf16[128,4096]{1,0:T(8,128)(2,1)S(1)} %pick_own.1.refs_2_), channel_id=1, source_target_pairs={{1,0},{66,1},{3,2},{68,3},{5,4},{70,5},{7,6},{72,7},{9,8},{74,9},{... | collective-permute-start | bytes 3145736 | tf_op jit(solution)/shard_map/ppermute | solution.py:440
  19.8 73.3 %collective-permute-start.1 = (bf16[128,4096]{1,0:T(8,128)(2,1)S(1)}, bf16[128,4096]{1,0:T(8,128)(2,1)}, u32[]{:S(2)}, u32[]{:S(2)}) collective-permute-start(bf16[128,4096]{1,0:T(8,128)(2,1)S(1)} %pick_own.1.refs_2_), channel_id=1, source_target_pairs={{0,1},{65,2},{2,3},{67,4},{4,5},{69,6},{6,7},{71,8},{8,9},{73,10},... | collective-permute-start | bytes 3145736 | tf_op jit(solution)/shard_map/ppermute | solution.py:439
  84.3 30.5 %collective-permute-start.5 = (bf16[128,4096]{1,0:T(8,128)(2,1)S(1)}, bf16[128,4096]{1,0:T(8,128)(2,1)}, u32[]{:S(2)}, u32[]{:S(2)}) collective-permute-start(bf16[128,4096]{1,0:T(8,128)(2,1)S(1)} %collective-permute-done.2.refs_3_), channel_id=1, source_target_pairs={{1,0},{66,1},{3,2},{68,3},{5,4},{70,5},{7,6},{72,7},{9,8},{74,9},{... | collective-permute-start | bytes 3145736 | tf_op jit(solution)/shard_map/ppermute | solution.py:445
  87.6 27.3 %collective-permute-start.3 = (bf16[128,4096]{1,0:T(8,128)(2,1)S(1)}, bf16[128,4096]{1,0:T(8,128)(2,1)}, u32[]{:S(2)}, u32[]{:S(2)}) collective-permute-start(bf16[128,4096]{1,0:T(8,128)(2,1)S(1)} %collective-permute-done.2.refs_3_), channel_id=1, source_target_pairs={{0,1},{65,2},{2,3},{67,4},{4,5},{69,6},{6,7},{71,8},{8,9},{73,10},... | collective-permute-start | bytes 3145736 | tf_op jit(solution)/shard_map/ppermute | solution.py:444
  114.9 25.3 %slice-start.1 = ((s8[5242880]{0:T(1024)(128)(4,1)}), s8[4194304]{0:T(1024)(128)(4,1)S(1)}, s32[]{:S(2)}) async-start(s8[5242880]{0:T(1024)(128)(4,1)} %bitcast.10), calls=%async_computation.1 | async-start | bytes 8388608
  126.2 23.7 %collective-permute-start.8 = (bf16[6,144,256]{2,1,0:T(8,128)(2,1)S(1)}, bf16[6,144,256]{2,1,0:T(8,128)(2,1)S(1)}, u32[]{:S(2)}, u32[]{:S(2)}) collective-permute-start(bf16[6,144,256]{2,1,0:T(8,128)(2,1)S(1)} %get-tuple-element.23), channel_id=1, source_target_pairs={{0,64},{64,0},{1,65},{65,1},{2,66},{66,2},{3,67},{67,3},{4,68},{68... | collective-permute-start | bytes 1327112 | tf_op jit(solution)/shard_map/ppermute | solution.py:458
  126.3 13.8 %collective-permute-start.9 = (bf16[2,144,256]{2,1,0:T(8,128)(2,1)S(1)}, bf16[2,144,256]{2,1,0:T(8,128)(2,1)S(1)}, u32[]{:S(2)}, u32[]{:S(2)}) collective-permute-start(bf16[2,144,256]{2,1,0:T(8,128)(2,1)S(1)} %get-tuple-element.24), channel_id=1, source_target_pairs={{0,64},{64,0},{1,65},{65,1},{2,66},{66,2},{3,67},{67,3},{4,68},{68... | collective-permute-start | bytes 442376 | tf_op jit(solution)/shard_map/ppermute | solution.py:458
  157.6 45.6 %collective-permute-start.13 = (bf16[10,128,256]{2,1,0:T(8,128)(2,1)S(1)}, bf16[10,128,256]{2,1,0:T(8,128)(2,1)S(1)}, u32[]{:S(2)}, u32[]{:S(2)}) collective-permute-start(bf16[10,128,256]{2,1,0:T(8,128)(2,1)S(1)} %get-tuple-element.33), channel_id=1, source_target_pairs={{0,64},{64,0},{1,65},{65,1},{2,66},{66,2},{3,67},{67,3},{4,68},{68... | collective-permute-start | bytes 1966088 | tf_op jit(solution)/shard_map/ppermute | solution.py:469
  165.3 38.8 %collective-permute-start.12 = (bf16[10,128,256]{2,1,0:T(8,128)(2,1)S(1)}, bf16[10,128,256]{2,1,0:T(8,128)(2,1)S(1)}, u32[]{:S(2)}, u32[]{:S(2)}) collective-permute-start(bf16[10,128,256]{2,1,0:T(8,128)(2,1)S(1)} %get-tuple-element.32), channel_id=1, source_target_pairs={{0,64},{64,0},{1,65},{65,1},{2,66},{66,2},{3,67},{67,3},{4,68},{68... | collective-permute-start | bytes 1966088 | tf_op jit(solution)/shard_map/ppermute | solution.py:469
  166.8 28.6 %collective-permute-start.15 = (bf16[10,128,128]{2,1,0:T(8,128)(2,1)S(1)}, bf16[10,128,128]{2,1,0:T(8,128)(2,1)S(1)}, u32[]{:S(2)}, u32[]{:S(2)}) collective-permute-start(bf16[10,128,128]{2,1,0:T(8,128)(2,1)S(1)} %get-tuple-element.35), channel_id=1, source_target_pairs={{0,64},{64,0},{1,65},{65,1},{2,66},{66,2},{3,67},{67,3},{4,68},{68... | collective-permute-start | bytes 983048 | tf_op jit(solution)/shard_map/ppermute | solution.py:469
  166.8 35.6 %collective-permute-start.14 = (bf16[10,128,128]{2,1,0:T(8,128)(2,1)S(1)}, bf16[10,128,128]{2,1,0:T(8,128)(2,1)S(1)}, u32[]{:S(2)}, u32[]{:S(2)}) collective-permute-start(bf16[10,128,128]{2,1,0:T(8,128)(2,1)S(1)} %get-tuple-element.34), channel_id=1, source_target_pairs={{0,64},{64,0},{1,65},{65,1},{2,66},{66,2},{3,67},{67,3},{4,68},{68... | collective-permute-start | bytes 983048 | tf_op jit(solution)/shard_map/ppermute | solution.py:469
  173.1 36.4 %collective-permute-start.11 = (bf16[10,128,128]{2,1,0:T(8,128)(2,1)S(1)}, bf16[10,128,128]{2,1,0:T(8,128)(2,1)S(1)}, u32[]{:S(2)}, u32[]{:S(2)}) collective-permute-start(bf16[10,128,128]{2,1,0:T(8,128)(2,1)S(1)} %get-tuple-element.31), channel_id=1, source_target_pairs={{0,64},{64,0},{1,65},{65,1},{2,66},{66,2},{3,67},{67,3},{4,68},{68... | collective-permute-start | bytes 983048 | tf_op jit(solution)/shard_map/ppermute | solution.py:469
  195.4 20.9 %collective-permute-start.10 = (bf16[10,128,128]{2,1,0:T(8,128)(2,1)S(1)}, bf16[10,128,128]{2,1,0:T(8,128)(2,1)S(1)}, u32[]{:S(2)}, u32[]{:S(2)}) collective-permute-start(bf16[10,128,128]{2,1,0:T(8,128)(2,1)S(1)} %get-tuple-element.30), channel_id=1, source_target_pairs={{0,64},{64,0},{1,65},{65,1},{2,66},{66,2},{3,67},{67,3},{4,68},{68... | collective-permute-start | bytes 983048 | tf_op jit(solution)/shard_map/ppermute | solution.py:469
